TPU v7x, 512 devices: a whole 4x8x8 slice. The times are simulated.
512 devices in a mesh: seq: 32 (over x, y), row: 4 (over z_lo), col: 4 (over z_hi, core).
Axes of the slice: x: 4, y: 8, z: 8 (z_hi: 2, z_lo: 4; z = z_hi * 4 + z_lo), core: 2. Of those that a mesh axis runs over, the one named last changes fastest.
Arguments:
- hidden_in: bfloat16 [4096, 2048], P('seq', ('row', 'col')), may hold values from -6 to 6
- seg_ids: int32 [4096], replicated, may hold values from 0 to 7, never falling along the last dimension, each value on 1 to 2048 neighbouring positions
- norm_gain: float32 [2048], replicated, may hold values from 0.25 to 1.75
- w_query: bfloat16 [2048, 1024], P(None, 'row'), may hold values from -0.125 to 0.125
- w_key: bfloat16 [2048, 1024], P(None, 'row'), may hold values from -0.125 to 0.125
- w_value: bfloat16 [2048, 2048], P(None, ('row', 'col')), may hold values from -0.125 to 0.125
- w_gate: bfloat16 [2048, 2048], P(None, ('row', 'col')), may hold values from -0.125 to 0.125
- w_decay_down: bfloat16 [2048, 16], replicated, may hold values from -0.125 to 0.125
- w_decay_up: bfloat16 [16, 1024], P(None, 'row'), may hold values from -1.5 to 1.5
- decay_bias: float32 [1024], P('row'), may hold values from -2 to 12
- conv_query: float32 [4, 1024], P(None, 'row'), may hold values from -3 to 3
- conv_key: float32 [4, 1024], P(None, 'row'), may hold values from -3 to 3
- conv_value: float32 [4, 2048], P(None, ('row', 'col')), may hold values from -3 to 3
- head_gain: float32 [512], P('col'), may hold values from 0.25 to 1.75
- w_out: bfloat16 [2048, 2048], P(('row', 'col')), may hold values from -0.1875 to 0.1875
Outputs:
- mixed: bfloat16 [4096, 2048], P('seq', ('row', 'col'))
Inputs may be any that keep to these rules, and one draw needn't show every extreme that they name: seg_ids never fall along the tokens; each of the 8 prompts holds 1 to 2048 consecutive tokens, and one holds exactly 2048.
All inputs are finite; a program needn't handle non-finite values.
Results may differ from a plain program's by a relative error of at most 0.014.
Values may be sent and summed in bfloat16 or wider, within the bound.
No kernel may reach another device: no remote copies, remote signals or barrier semaphores. Data moves between devices by JAX's collectives and lax.ppermute only.
A program may use at most 64 MiB of HBM per device.

v0:
```python
import jax
import jax.numpy as jnp
from jax import lax
from jax.sharding import PartitionSpec as P

HEAD_V = 512
SPAN = 64


highest = lax.Precision.HIGHEST


def shifted(array, axis, by):
    size = lax.axis_size(axis)
    pairs = [(i, i + by) for i in range(size) if 0 <= i + by < size]
    return lax.ppermute(array, axis, pairs)


def span_step(state, queries, keys_c, values_c, log_decay, segments, seg_before):
    width = segments.shape[0]
    cumulated = jnp.cumsum(log_decay, axis=0)
    row_iota = lax.broadcasted_iota(jnp.int32, (width, width), 0)
    col_iota = lax.broadcasted_iota(jnp.int32, (width, width), 1)
    visible = (segments[:, None] == segments[None, :]) & (row_iota >= col_iota)
    spread = jnp.minimum(cumulated[:, None, :] - cumulated[None, :, :], 0.0)
    weights = jnp.sum(queries[:, None, :] * keys_c[None, :, :] * jnp.exp(spread), axis=2)
    weights = jnp.where(visible, weights, 0.0)
    carried = (segments == seg_before)[:, None]
    reach = jnp.where(carried, queries * jnp.exp(cumulated), 0.0)
    outputs = jnp.dot(weights, values_c, precision=highest) + jnp.dot(
        reach, state, precision=highest
    )
    final = cumulated[-1]
    tail = (segments == segments[-1])[:, None]
    pushed = jnp.where(tail, keys_c * jnp.exp(final[None, :] - cumulated), 0.0)
    keep = jnp.where(segments[-1] == seg_before, jnp.exp(final), 0.0)
    state_new = state * keep[:, None] + jnp.einsum("ck,cv->kv", pushed, values_c, precision=highest)
    return (state_new, outputs, cumulated)


def short_conv(extended, kernel, seg_ext, segments):
    length = segments.shape[0]
    taps = kernel.shape[0]
    total = jnp.zeros((length, extended.shape[1]), jnp.float32)
    for j in range(taps):
        offset = taps - 1 - j
        same = (seg_ext[offset : offset + length] == segments)[:, None]
        total = total + jnp.where(
            same, kernel[j][None, :] * extended[offset : offset + length], 0.0
        )
    return total


def shards(
    hidden_in,
    seg_ids,
    norm_gain,
    w_query,
    w_key,
    w_value,
    w_gate,
    w_decay_down,
    w_decay_up,
    decay_bias,
    conv_query,
    conv_key,
    conv_value,
    head_gain,
    w_out,
):
    rows = hidden_in.shape[0]
    taps = conv_query.shape[0]
    head_k = w_query.shape[1]
    whole = lax.all_gather(hidden_in, ("row", "col"), axis=1, tiled=True)
    activ = whole.astype(jnp.float32)
    normed = (
        activ * lax.rsqrt(jnp.mean(activ * activ, axis=1, keepdims=True) + 1e-06) * norm_gain
    ).astype(jnp.bfloat16)
    query_pre = jnp.dot(normed, w_query, preferred_element_type=jnp.float32)
    key_pre = jnp.dot(normed, w_key, preferred_element_type=jnp.float32)
    value_pre = jnp.dot(normed, w_value, preferred_element_type=jnp.float32)
    gate_pre = jnp.dot(normed, w_gate, preferred_element_type=jnp.float32)
    rank_part = jnp.dot(normed, w_decay_down, preferred_element_type=jnp.float32)
    log_decay = (
        jax.nn.log_sigmoid(
            jnp.dot(rank_part, w_decay_up.astype(jnp.float32), precision=highest) + decay_bias
        )
        / 16.0
    )
    position = lax.axis_index("seq") * rows
    padded_ids = jnp.concatenate([jnp.full((taps - 1,), -1, jnp.int32), seg_ids])
    seg_ext = lax.dynamic_slice_in_dim(padded_ids, position, rows + taps - 1)
    segments = seg_ext[taps - 1 :]
    seg_before = seg_ext[taps - 2]
    stacked = jnp.concatenate([query_pre, key_pre, value_pre], axis=1)
    edge = shifted(stacked[rows - (taps - 1) :], "seq", 1)
    extended = jnp.concatenate([edge, stacked], axis=0)
    kernel = jnp.concatenate([conv_query, conv_key, conv_value], axis=1)
    mixed_in = jax.nn.silu(short_conv(extended, kernel, seg_ext, segments))
    queries = mixed_in[:, :head_k] * head_k ** (-0.5)
    keys_all = mixed_in[:, head_k : 2 * head_k]
    values_all = mixed_in[:, 2 * head_k :]
    value_width = values_all.shape[1]
    blocks = rows // SPAN
    befores = seg_ext[taps - 2 : taps - 2 + rows : SPAN]

    def advance(carry, pieces):
        state, total = carry
        state_new, outputs, cumulated = span_step(
            state, pieces[0], pieces[1], pieces[2], pieces[3], pieces[4], pieces[5]
        )
        reach = jnp.where(
            (pieces[4] == seg_before)[:, None], pieces[0] * jnp.exp(total[None, :] + cumulated), 0.0
        )
        return ((state_new, total + cumulated[-1]), (outputs, reach))

    start_carry = (jnp.zeros((head_k, value_width), jnp.float32), jnp.zeros((head_k,), jnp.float32))
    carried_out, stacked_out = lax.scan(
        advance,
        start_carry,
        (
            queries.reshape(blocks, SPAN, head_k),
            keys_all.reshape(blocks, SPAN, head_k),
            values_all.reshape(blocks, SPAN, value_width),
            log_decay.reshape(blocks, SPAN, head_k),
            segments.reshape(blocks, SPAN),
            befores,
        ),
    )
    local_state, decay_total = carried_out
    outputs, reach = stacked_out
    decay_dev = jnp.where(segments[-1] == seg_before, jnp.exp(decay_total), 0.0)

    def turn(step_index, incoming_state):
        return shifted(
            (decay_dev[:, None] * incoming_state + local_state).astype(jnp.bfloat16), "seq", 1
        ).astype(jnp.float32)

    incoming = lax.fori_loop(0, lax.axis_size("seq") - 1, turn, jnp.zeros_like(local_state))
    attended = outputs.reshape(rows, value_width) + jnp.dot(
        reach.reshape(rows, head_k), incoming, precision=highest
    )
    squares = lax.psum(jnp.sum(attended * attended, axis=1), "col")
    scale_rows = lax.rsqrt(squares / HEAD_V + 1e-05)
    gated = (attended * scale_rows[:, None] * head_gain * jax.nn.silu(gate_pre)).astype(
        jnp.bfloat16
    )
    terms = jnp.dot(gated, w_out, preferred_element_type=jnp.float32)
    summed = lax.psum_scatter(
        terms.astype(jnp.bfloat16), ("row", "col"), scatter_dimension=1, tiled=True
    ).astype(jnp.float32)
    return (hidden_in.astype(jnp.float32) + summed).astype(jnp.bfloat16)


def solution(mesh):
    return jax.shard_map(
        shards,
        mesh=mesh,
        in_specs=(
            P("seq", ("row", "col")),
            P(),
            P(),
            P(None, "row"),
            P(None, "row"),
            P(None, ("row", "col")),
            P(None, ("row", "col")),
            P(),
            P(None, "row"),
            P("row"),
            P(None, "row"),
            P(None, "row"),
            P(None, ("row", "col")),
            P("col"),
            P(("row", "col"), None),
        ),
        out_specs=P("seq", ("row", "col")),
        check_vma=False,
    )
```

profile of v0, /device:TPU:1, one launch (start us, length us, event | category | flops | bytes accessed | tf_op | source)
XLA Modules:
  0.0 425.3 jit_solution(11821736212391899201)
XLA Ops:
  6.5 35.7 %all_gather.3 = bf16[128,2048]{1,0:T(8,128)(2,1)S(1)} all-gather(bf16[128,128]{1,0:T(8,128)(2,1)} %param.19), channel_id=1, replica_groups=mesh['seq'=32,'row'=4,'col'=4] {'row','col'}, dimensions={1}, use_global_device_ids=true | all-gather | bytes 557056 | tf_op jit(solution)/shard_map/all_gather | solution.py:74
  51.8 12.9 %while.28 = (s32[]{:T(128)}, f32[256,128]{1,0:T(8,128)S(1)}, f32[256]{0:T(256)S(1)}, f32[2,64,128]{2,1,0:T(8,128)S(1)}, f32[2,64,256]{2,1,0:T(8,128)S(1)}, /*ind...) while((s32[]{:T(128)}, f32[256,128]{1,0:T(8,128)S(1)}, ...), condition=%wide.region_4.5_spmd.clone, body=%wide.region_1.4_spmd.clone.sunk | while | flops 63181764 | bytes 1736343 | solution.py:118
  64.8 204.3 %while.29 = (s32[]{:T(128)}, f32[256,128]{1,0:T(8,128)S(1)}, f32[256]{0:T(256)S(1)}, f32[256,128]{1,0:T(8,128)S(1)}, s32[]{:T(128)}, /*index=5*/s32[]{:T(128)}) while((s32[]{:T(128)}, f32[256,128]{1,0:T(8,128)S(1)}, f32[256]{0:T(256)S(1)}, f32[256,128]{1,0:T(8,128)S(1)}, s32[]{:T(128)}, /*index=5*/s32[]{:T(128)}) %tuple.66), condition=%wide.region_6.7_spmd.clone, body=%wide.region_5.6_spmd.clone.sunk | while | flops 163843 | bytes 787575 | solution.py:139
  97.0 4.9 %collective-permute-start = (bf16[256,128]{1,0:T(8,128)(2,1)S(1)}, bf16[256,128]{1,0:T(8,128)(2,1)S(1)}, u32[]{:S(2)}, u32[]{:S(2)}) collective-permute-start(bf16[256,128]{1,0:T(8,128)(2,1)S(1)} %fusion.105), channel_id=1, source_target_pairs={{0,16},{16,32},{32,48},{48,64},{64,80},{80,96},{96,112},{112,128},... | collective-permute-start | bytes 196616 | tf_op jit(solution)/shard_map/while/body/eval_jaxpr/ppermute | solution.py:16
  103.6 5.0 %collective-permute-start = (bf16[256,128]{1,0:T(8,128)(2,1)S(1)}, bf16[256,128]{1,0:T(8,128)(2,1)S(1)}, u32[]{:S(2)}, u32[]{:S(2)}) collective-permute-start(bf16[256,128]{1,0:T(8,128)(2,1)S(1)} %fusion.105), channel_id=1, source_target_pairs={{0,16},{16,32},{32,48},{48,64},{64,80},{80,96},{96,112},{112,128},... | collective-permute-start | bytes 196616 | tf_op jit(solution)/shard_map/while/body/eval_jaxpr/ppermute | solution.py:16
  110.1 5.1 %collective-permute-start = (bf16[256,128]{1,0:T(8,128)(2,1)S(1)}, bf16[256,128]{1,0:T(8,128)(2,1)S(1)}, u32[]{:S(2)}, u32[]{:S(2)}) collective-permute-start(bf16[256,128]{1,0:T(8,128)(2,1)S(1)} %fusion.105), channel_id=1, source_target_pairs={{0,16},{16,32},{32,48},{48,64},{64,80},{80,96},{96,112},{112,128},... | collective-permute-start | bytes 196616 | tf_op jit(solution)/shard_map/while/body/eval_jaxpr/ppermute | solution.py:16
  116.6 5.3 %collective-permute-start = (bf16[256,128]{1,0:T(8,128)(2,1)S(1)}, bf16[256,128]{1,0:T(8,128)(2,1)S(1)}, u32[]{:S(2)}, u32[]{:S(2)}) collective-permute-start(bf16[256,128]{1,0:T(8,128)(2,1)S(1)} %fusion.105), channel_id=1, source_target_pairs={{0,16},{16,32},{32,48},{48,64},{64,80},{80,96},{96,112},{112,128},... | collective-permute-start | bytes 196616 | tf_op jit(solution)/shard_map/while/body/eval_jaxpr/ppermute | solution.py:16
  142.5 5.2 %collective-permute-start = (bf16[256,128]{1,0:T(8,128)(2,1)S(1)}, bf16[256,128]{1,0:T(8,128)(2,1)S(1)}, u32[]{:S(2)}, u32[]{:S(2)}) collective-permute-start(bf16[256,128]{1,0:T(8,128)(2,1)S(1)} %fusion.105), channel_id=1, source_target_pairs={{0,16},{16,32},{32,48},{48,64},{64,80},{80,96},{96,112},{112,128},... | collective-permute-start | bytes 196616 | tf_op jit(solution)/shard_map/while/body/eval_jaxpr/ppermute | solution.py:16
  149.1 5.2 %collective-permute-start = (bf16[256,128]{1,0:T(8,128)(2,1)S(1)}, bf16[256,128]{1,0:T(8,128)(2,1)S(1)}, u32[]{:S(2)}, u32[]{:S(2)}) collective-permute-start(bf16[256,128]{1,0:T(8,128)(2,1)S(1)} %fusion.105), channel_id=1, source_target_pairs={{0,16},{16,32},{32,48},{48,64},{64,80},{80,96},{96,112},{112,128},... | collective-permute-start | bytes 196616 | tf_op jit(solution)/shard_map/while/body/eval_jaxpr/ppermute | solution.py:16
  161.9 5.3 %collective-permute-start = (bf16[256,128]{1,0:T(8,128)(2,1)S(1)}, bf16[256,128]{1,0:T(8,128)(2,1)S(1)}, u32[]{:S(2)}, u32[]{:S(2)}) collective-permute-start(bf16[256,128]{1,0:T(8,128)(2,1)S(1)} %fusion.105), channel_id=1, source_target_pairs={{0,16},{16,32},{32,48},{48,64},{64,80},{80,96},{96,112},{112,128},... | collective-permute-start | bytes 196616 | tf_op jit(solution)/shard_map/while/body/eval_jaxpr/ppermute | solution.py:16
  181.4 5.6 %collective-permute-start = (bf16[256,128]{1,0:T(8,128)(2,1)S(1)}, bf16[256,128]{1,0:T(8,128)(2,1)S(1)}, u32[]{:S(2)}, u32[]{:S(2)}) collective-permute-start(bf16[256,128]{1,0:T(8,128)(2,1)S(1)} %fusion.105), channel_id=1, source_target_pairs={{0,16},{16,32},{32,48},{48,64},{64,80},{80,96},{96,112},{112,128},... | collective-permute-start | bytes 196616 | tf_op jit(solution)/shard_map/while/body/eval_jaxpr/ppermute | solution.py:16
  188.5 5.6 %collective-permute-start = (bf16[256,128]{1,0:T(8,128)(2,1)S(1)}, bf16[256,128]{1,0:T(8,128)(2,1)S(1)}, u32[]{:S(2)}, u32[]{:S(2)}) collective-permute-start(bf16[256,128]{1,0:T(8,128)(2,1)S(1)} %fusion.105), channel_id=1, source_target_pairs={{0,16},{16,32},{32,48},{48,64},{64,80},{80,96},{96,112},{112,128},... | collective-permute-start | bytes 196616 | tf_op jit(solution)/shard_map/while/body/eval_jaxpr/ppermute | solution.py:16
  195.5 5.9 %collective-permute-start = (bf16[256,128]{1,0:T(8,128)(2,1)S(1)}, bf16[256,128]{1,0:T(8,128)(2,1)S(1)}, u32[]{:S(2)}, u32[]{:S(2)}) collective-permute-start(bf16[256,128]{1,0:T(8,128)(2,1)S(1)} %fusion.105), channel_id=1, source_target_pairs={{0,16},{16,32},{32,48},{48,64},{64,80},{80,96},{96,112},{112,128},... | collective-permute-start | bytes 196616 | tf_op jit(solution)/shard_map/while/body/eval_jaxpr/ppermute | solution.py:16
  202.9 5.7 %collective-permute-start = (bf16[256,128]{1,0:T(8,128)(2,1)S(1)}, bf16[256,128]{1,0:T(8,128)(2,1)S(1)}, u32[]{:S(2)}, u32[]{:S(2)}) collective-permute-start(bf16[256,128]{1,0:T(8,128)(2,1)S(1)} %fusion.105), channel_id=1, source_target_pairs={{0,16},{16,32},{32,48},{48,64},{64,80},{80,96},{96,112},{112,128},... | collective-permute-start | bytes 196616 | tf_op jit(solution)/shard_map/while/body/eval_jaxpr/ppermute | solution.py:16
  210.4 6.0 %collective-permute-start = (bf16[256,128]{1,0:T(8,128)(2,1)S(1)}, bf16[256,128]{1,0:T(8,128)(2,1)S(1)}, u32[]{:S(2)}, u32[]{:S(2)}) collective-permute-start(bf16[256,128]{1,0:T(8,128)(2,1)S(1)} %fusion.105), channel_id=1, source_target_pairs={{0,16},{16,32},{32,48},{48,64},{64,80},{80,96},{96,112},{112,128},... | collective-permute-start | bytes 196616 | tf_op jit(solution)/shard_map/while/body/eval_jaxpr/ppermute | solution.py:16
  217.9 5.7 %collective-permute-start = (bf16[256,128]{1,0:T(8,128)(2,1)S(1)}, bf16[256,128]{1,0:T(8,128)(2,1)S(1)}, u32[]{:S(2)}, u32[]{:S(2)}) collective-permute-start(bf16[256,128]{1,0:T(8,128)(2,1)S(1)} %fusion.105), channel_id=1, source_target_pairs={{0,16},{16,32},{32,48},{48,64},{64,80},{80,96},{96,112},{112,128},... | collective-permute-start | bytes 196616 | tf_op jit(solution)/shard_map/while/body/eval_jaxpr/ppermute | solution.py:16
  225.1 5.6 %collective-permute-start = (bf16[256,128]{1,0:T(8,128)(2,1)S(1)}, bf16[256,128]{1,0:T(8,128)(2,1)S(1)}, u32[]{:S(2)}, u32[]{:S(2)}) collective-permute-start(bf16[256,128]{1,0:T(8,128)(2,1)S(1)} %fusion.105), channel_id=1, source_target_pairs={{0,16},{16,32},{32,48},{48,64},{64,80},{80,96},{96,112},{112,128},... | collective-permute-start | bytes 196616 | tf_op jit(solution)/shard_map/while/body/eval_jaxpr/ppermute | solution.py:16
  232.1 6.2 %collective-permute-start = (bf16[256,128]{1,0:T(8,128)(2,1)S(1)}, bf16[256,128]{1,0:T(8,128)(2,1)S(1)}, u32[]{:S(2)}, u32[]{:S(2)}) collective-permute-start(bf16[256,128]{1,0:T(8,128)(2,1)S(1)} %fusion.105), channel_id=1, source_target_pairs={{0,16},{16,32},{32,48},{48,64},{64,80},{80,96},{96,112},{112,128},... | collective-permute-start | bytes 196616 | tf_op jit(solution)/shard_map/while/body/eval_jaxpr/ppermute | solution.py:16
  239.7 5.6 %collective-permute-start = (bf16[256,128]{1,0:T(8,128)(2,1)S(1)}, bf16[256,128]{1,0:T(8,128)(2,1)S(1)}, u32[]{:S(2)}, u32[]{:S(2)}) collective-permute-start(bf16[256,128]{1,0:T(8,128)(2,1)S(1)} %fusion.105), channel_id=1, source_target_pairs={{0,16},{16,32},{32,48},{48,64},{64,80},{80,96},{96,112},{112,128},... | collective-permute-start | bytes 196616 | tf_op jit(solution)/shard_map/while/body/eval_jaxpr/ppermute | solution.py:16
  246.8 5.5 %collective-permute-start = (bf16[256,128]{1,0:T(8,128)(2,1)S(1)}, bf16[256,128]{1,0:T(8,128)(2,1)S(1)}, u32[]{:S(2)}, u32[]{:S(2)}) collective-permute-start(bf16[256,128]{1,0:T(8,128)(2,1)S(1)} %fusion.105), channel_id=1, source_target_pairs={{0,16},{16,32},{32,48},{48,64},{64,80},{80,96},{96,112},{112,128},... | collective-permute-start | bytes 196616 | tf_op jit(solution)/shard_map/while/body/eval_jaxpr/ppermute | solution.py:16
  253.7 6.3 %collective-permute-start = (bf16[256,128]{1,0:T(8,128)(2,1)S(1)}, bf16[256,128]{1,0:T(8,128)(2,1)S(1)}, u32[]{:S(2)}, u32[]{:S(2)}) collective-permute-start(bf16[256,128]{1,0:T(8,128)(2,1)S(1)} %fusion.105), channel_id=1, source_target_pairs={{0,16},{16,32},{32,48},{48,64},{64,80},{80,96},{96,112},{112,128},... | collective-permute-start | bytes 196616 | tf_op jit(solution)/shard_map/while/body/eval_jaxpr/ppermute | solution.py:16
  261.5 5.8 %collective-permute-start = (bf16[256,128]{1,0:T(8,128)(2,1)S(1)}, bf16[256,128]{1,0:T(8,128)(2,1)S(1)}, u32[]{:S(2)}, u32[]{:S(2)}) collective-permute-start(bf16[256,128]{1,0:T(8,128)(2,1)S(1)} %fusion.105), channel_id=1, source_target_pairs={{0,16},{16,32},{32,48},{48,64},{64,80},{80,96},{96,112},{112,128},... | collective-permute-start | bytes 196616 | tf_op jit(solution)/shard_map/while/body/eval_jaxpr/ppermute | solution.py:16
  269.6 42.8 %psum.7 = f32[128]{0:T(128)S(1)} all-reduce(f32[128]{0:T(128)S(1)} %get-tuple-element.205), channel_id=1, replica_groups=mesh['seq'=32,'row'=4,'col'=4] {'col'}, use_global_device_ids=true, to_apply=%region_8.9 | all-reduce | flops 128 | bytes 1024 | tf_op jit(solution)/shard_map/psum | solution.py:143
  314.3 102.6 %reduce-scatter.4.cloned.1.call-done = bf16[128,128]{1,0:T(8,128)(2,1)} async-done(((bf16[2048,128]{1,0:T(8,128)(2,1)}), bf16[128,128]{1,0:T(8,128)(2,1)}) %reduce-scatter.4.cloned.1.call-update) | async-done | bytes 32784
  (201 shorter events, 120.1 us)
Async XLA Ops:
  6.5 410.4 %reduce-scatter.4.cloned.1.call-start = ((), (), s32[]{:S(2)}) async-start(), calls=%async_computation.1 | async-start | bytes 557056
  45.1 6.3 %collective-permute-start.1 = (f32[3,640]{1,0:T(4,128)S(1)}, f32[3,640]{1,0:T(4,128)S(1)}, u32[]{:S(2)}, u32[]{:S(2)}) collective-permute-start(f32[3,640]{1,0:T(4,128)S(1)} %slice.88), channel_id=1, source_target_pairs={{0,16},{16,32},{32,48},{48,64},{64,80},{80,96},{96,112},{112,128},... | collective-permute-start | bytes 23048 | tf_op jit(solution)/shard_map/ppermute | solution.py:16
  90.7 6.2 %collective-permute-start = (bf16[256,128]{1,0:T(8,128)(2,1)S(1)}, bf16[256,128]{1,0:T(8,128)(2,1)S(1)}, u32[]{:S(2)}, u32[]{:S(2)}) collective-permute-start(bf16[256,128]{1,0:T(8,128)(2,1)S(1)} %fusion.105), channel_id=1, source_target_pairs={{0,16},{16,32},{32,48},{48,64},{64,80},{80,96},{96,112},{112,128},... | collective-permute-start | bytes 196616 | tf_op jit(solution)/shard_map/while/body/eval_jaxpr/ppermute | solution.py:16
  97.0 6.5 %collective-permute-start = (bf16[256,128]{1,0:T(8,128)(2,1)S(1)}, bf16[256,128]{1,0:T(8,128)(2,1)S(1)}, u32[]{:S(2)}, u32[]{:S(2)}) collective-permute-start(bf16[256,128]{1,0:T(8,128)(2,1)S(1)} %fusion.105), channel_id=1, source_target_pairs={{0,16},{16,32},{32,48},{48,64},{64,80},{80,96},{96,112},{112,128},... | collective-permute-start | bytes 196616 | tf_op jit(solution)/shard_map/while/body/eval_jaxpr/ppermute | solution.py:16
  103.6 6.3 %collective-permute-start = (bf16[256,128]{1,0:T(8,128)(2,1)S(1)}, bf16[256,128]{1,0:T(8,128)(2,1)S(1)}, u32[]{:S(2)}, u32[]{:S(2)}) collective-permute-start(bf16[256,128]{1,0:T(8,128)(2,1)S(1)} %fusion.105), channel_id=1, source_target_pairs={{0,16},{16,32},{32,48},{48,64},{64,80},{80,96},{96,112},{112,128},... | collective-permute-start | bytes 196616 | tf_op jit(solution)/shard_map/while/body/eval_jaxpr/ppermute | solution.py:16
  110.1 6.5 %collective-permute-start = (bf16[256,128]{1,0:T(8,128)(2,1)S(1)}, bf16[256,128]{1,0:T(8,128)(2,1)S(1)}, u32[]{:S(2)}, u32[]{:S(2)}) collective-permute-start(bf16[256,128]{1,0:T(8,128)(2,1)S(1)} %fusion.105), channel_id=1, source_target_pairs={{0,16},{16,32},{32,48},{48,64},{64,80},{80,96},{96,112},{112,128},... | collective-permute-start | bytes 196616 | tf_op jit(solution)/shard_map/while/body/eval_jaxpr/ppermute | solution.py:16
  116.6 6.6 %collective-permute-start = (bf16[256,128]{1,0:T(8,128)(2,1)S(1)}, bf16[256,128]{1,0:T(8,128)(2,1)S(1)}, u32[]{:S(2)}, u32[]{:S(2)}) collective-permute-start(bf16[256,128]{1,0:T(8,128)(2,1)S(1)} %fusion.105), channel_id=1, source_target_pairs={{0,16},{16,32},{32,48},{48,64},{64,80},{80,96},{96,112},{112,128},... | collective-permute-start | bytes 196616 | tf_op jit(solution)/shard_map/while/body/eval_jaxpr/ppermute | solution.py:16
  123.4 6.2 %collective-permute-start = (bf16[256,128]{1,0:T(8,128)(2,1)S(1)}, bf16[256,128]{1,0:T(8,128)(2,1)S(1)}, u32[]{:S(2)}, u32[]{:S(2)}) collective-permute-start(bf16[256,128]{1,0:T(8,128)(2,1)S(1)} %fusion.105), channel_id=1, source_target_pairs={{0,16},{16,32},{32,48},{48,64},{64,80},{80,96},{96,112},{112,128},... | collective-permute-start | bytes 196616 | tf_op jit(solution)/shard_map/while/body/eval_jaxpr/ppermute | solution.py:16
  129.8 6.2 %collective-permute-start = (bf16[256,128]{1,0:T(8,128)(2,1)S(1)}, bf16[256,128]{1,0:T(8,128)(2,1)S(1)}, u32[]{:S(2)}, u32[]{:S(2)}) collective-permute-start(bf16[256,128]{1,0:T(8,128)(2,1)S(1)} %fusion.105), channel_id=1, source_target_pairs={{0,16},{16,32},{32,48},{48,64},{64,80},{80,96},{96,112},{112,128},... | collective-permute-start | bytes 196616 | tf_op jit(solution)/shard_map/while/body/eval_jaxpr/ppermute | solution.py:16
  142.5 6.5 %collective-permute-start = (bf16[256,128]{1,0:T(8,128)(2,1)S(1)}, bf16[256,128]{1,0:T(8,128)(2,1)S(1)}, u32[]{:S(2)}, u32[]{:S(2)}) collective-permute-start(bf16[256,128]{1,0:T(8,128)(2,1)S(1)} %fusion.105), channel_id=1, source_target_pairs={{0,16},{16,32},{32,48},{48,64},{64,80},{80,96},{96,112},{112,128},... | collective-permute-start | bytes 196616 | tf_op jit(solution)/shard_map/while/body/eval_jaxpr/ppermute | solution.py:16
  149.1 6.5 %collective-permute-start = (bf16[256,128]{1,0:T(8,128)(2,1)S(1)}, bf16[256,128]{1,0:T(8,128)(2,1)S(1)}, u32[]{:S(2)}, u32[]{:S(2)}) collective-permute-start(bf16[256,128]{1,0:T(8,128)(2,1)S(1)} %fusion.105), channel_id=1, source_target_pairs={{0,16},{16,32},{32,48},{48,64},{64,80},{80,96},{96,112},{112,128},... | collective-permute-start | bytes 196616 | tf_op jit(solution)/shard_map/while/body/eval_jaxpr/ppermute | solution.py:16
  161.9 6.6 %collective-permute-start = (bf16[256,128]{1,0:T(8,128)(2,1)S(1)}, bf16[256,128]{1,0:T(8,128)(2,1)S(1)}, u32[]{:S(2)}, u32[]{:S(2)}) collective-permute-start(bf16[256,128]{1,0:T(8,128)(2,1)S(1)} %fusion.105), channel_id=1, source_target_pairs={{0,16},{16,32},{32,48},{48,64},{64,80},{80,96},{96,112},{112,128},... | collective-permute-start | bytes 196616 | tf_op jit(solution)/shard_map/while/body/eval_jaxpr/ppermute | solution.py:16
  181.4 7.0 %collective-permute-start = (bf16[256,128]{1,0:T(8,128)(2,1)S(1)}, bf16[256,128]{1,0:T(8,128)(2,1)S(1)}, u32[]{:S(2)}, u32[]{:S(2)}) collective-permute-start(bf16[256,128]{1,0:T(8,128)(2,1)S(1)} %fusion.105), channel_id=1, source_target_pairs={{0,16},{16,32},{32,48},{48,64},{64,80},{80,96},{96,112},{112,128},... | collective-permute-start | bytes 196616 | tf_op jit(solution)/shard_map/while/body/eval_jaxpr/ppermute | solution.py:16
  188.5 6.9 %collective-permute-start = (bf16[256,128]{1,0:T(8,128)(2,1)S(1)}, bf16[256,128]{1,0:T(8,128)(2,1)S(1)}, u32[]{:S(2)}, u32[]{:S(2)}) collective-permute-start(bf16[256,128]{1,0:T(8,128)(2,1)S(1)} %fusion.105), channel_id=1, source_target_pairs={{0,16},{16,32},{32,48},{48,64},{64,80},{80,96},{96,112},{112,128},... | collective-permute-start | bytes 196616 | tf_op jit(solution)/shard_map/while/body/eval_jaxpr/ppermute | solution.py:16
  195.5 7.3 %collective-permute-start = (bf16[256,128]{1,0:T(8,128)(2,1)S(1)}, bf16[256,128]{1,0:T(8,128)(2,1)S(1)}, u32[]{:S(2)}, u32[]{:S(2)}) collective-permute-start(bf16[256,128]{1,0:T(8,128)(2,1)S(1)} %fusion.105), channel_id=1, source_target_pairs={{0,16},{16,32},{32,48},{48,64},{64,80},{80,96},{96,112},{112,128},... | collective-permute-start | bytes 196616 | tf_op jit(solution)/shard_map/while/body/eval_jaxpr/ppermute | solution.py:16
  202.9 7.4 %collective-permute-start = (bf16[256,128]{1,0:T(8,128)(2,1)S(1)}, bf16[256,128]{1,0:T(8,128)(2,1)S(1)}, u32[]{:S(2)}, u32[]{:S(2)}) collective-permute-start(bf16[256,128]{1,0:T(8,128)(2,1)S(1)} %fusion.105), channel_id=1, source_target_pairs={{0,16},{16,32},{32,48},{48,64},{64,80},{80,96},{96,112},{112,128},... | collective-permute-start | bytes 196616 | tf_op jit(solution)/shard_map/while/body/eval_jaxpr/ppermute | solution.py:16
  210.4 7.3 %collective-permute-start = (bf16[256,128]{1,0:T(8,128)(2,1)S(1)}, bf16[256,128]{1,0:T(8,128)(2,1)S(1)}, u32[]{:S(2)}, u32[]{:S(2)}) collective-permute-start(bf16[256,128]{1,0:T(8,128)(2,1)S(1)} %fusion.105), channel_id=1, source_target_pairs={{0,16},{16,32},{32,48},{48,64},{64,80},{80,96},{96,112},{112,128},... | collective-permute-start | bytes 196616 | tf_op jit(solution)/shard_map/while/body/eval_jaxpr/ppermute | solution.py:16
  217.9 7.0 %collective-permute-start = (bf16[256,128]{1,0:T(8,128)(2,1)S(1)}, bf16[256,128]{1,0:T(8,128)(2,1)S(1)}, u32[]{:S(2)}, u32[]{:S(2)}) collective-permute-start(bf16[256,128]{1,0:T(8,128)(2,1)S(1)} %fusion.105), channel_id=1, source_target_pairs={{0,16},{16,32},{32,48},{48,64},{64,80},{80,96},{96,112},{112,128},... | collective-permute-start | bytes 196616 | tf_op jit(solution)/shard_map/while/body/eval_jaxpr/ppermute | solution.py:16
  225.1 6.9 %collective-permute-start = (bf16[256,128]{1,0:T(8,128)(2,1)S(1)}, bf16[256,128]{1,0:T(8,128)(2,1)S(1)}, u32[]{:S(2)}, u32[]{:S(2)}) collective-permute-start(bf16[256,128]{1,0:T(8,128)(2,1)S(1)} %fusion.105), channel_id=1, source_target_pairs={{0,16},{16,32},{32,48},{48,64},{64,80},{80,96},{96,112},{112,128},... | collective-permute-start | bytes 196616 | tf_op jit(solution)/shard_map/while/body/eval_jaxpr/ppermute | solution.py:16
  232.1 7.5 %collective-permute-start = (bf16[256,128]{1,0:T(8,128)(2,1)S(1)}, bf16[256,128]{1,0:T(8,128)(2,1)S(1)}, u32[]{:S(2)}, u32[]{:S(2)}) collective-permute-start(bf16[256,128]{1,0:T(8,128)(2,1)S(1)} %fusion.105), channel_id=1, source_target_pairs={{0,16},{16,32},{32,48},{48,64},{64,80},{80,96},{96,112},{112,128},... | collective-permute-start | bytes 196616 | tf_op jit(solution)/shard_map/while/body/eval_jaxpr/ppermute | solution.py:16
  239.7 6.9 %collective-permute-start = (bf16[256,128]{1,0:T(8,128)(2,1)S(1)}, bf16[256,128]{1,0:T(8,128)(2,1)S(1)}, u32[]{:S(2)}, u32[]{:S(2)}) collective-permute-start(bf16[256,128]{1,0:T(8,128)(2,1)S(1)} %fusion.105), channel_id=1, source_target_pairs={{0,16},{16,32},{32,48},{48,64},{64,80},{80,96},{96,112},{112,128},... | collective-permute-start | bytes 196616 | tf_op jit(solution)/shard_map/while/body/eval_jaxpr/ppermute | solution.py:16
  246.8 6.8 %collective-permute-start = (bf16[256,128]{1,0:T(8,128)(2,1)S(1)}, bf16[256,128]{1,0:T(8,128)(2,1)S(1)}, u32[]{:S(2)}, u32[]{:S(2)}) collective-permute-start(bf16[256,128]{1,0:T(8,128)(2,1)S(1)} %fusion.105), channel_id=1, source_target_pairs={{0,16},{16,32},{32,48},{48,64},{64,80},{80,96},{96,112},{112,128},... | collective-permute-start | bytes 196616 | tf_op jit(solution)/shard_map/while/body/eval_jaxpr/ppermute | solution.py:16
  253.7 7.6 %collective-permute-start = (bf16[256,128]{1,0:T(8,128)(2,1)S(1)}, bf16[256,128]{1,0:T(8,128)(2,1)S(1)}, u32[]{:S(2)}, u32[]{:S(2)}) collective-permute-start(bf16[256,128]{1,0:T(8,128)(2,1)S(1)} %fusion.105), channel_id=1, source_target_pairs={{0,16},{16,32},{32,48},{48,64},{64,80},{80,96},{96,112},{112,128},... | collective-permute-start | bytes 196616 | tf_op jit(solution)/shard_map/while/body/eval_jaxpr/ppermute | solution.py:16
  261.5 7.7 %collective-permute-start = (bf16[256,128]{1,0:T(8,128)(2,1)S(1)}, bf16[256,128]{1,0:T(8,128)(2,1)S(1)}, u32[]{:S(2)}, u32[]{:S(2)}) collective-permute-start(bf16[256,128]{1,0:T(8,128)(2,1)S(1)} %fusion.105), channel_id=1, source_target_pairs={{0,16},{16,32},{32,48},{48,64},{64,80},{80,96},{96,112},{112,128},... | collective-permute-start | bytes 196616 | tf_op jit(solution)/shard_map/while/body/eval_jaxpr/ppermute | solution.py:16
  (24 other events, 1010.7 us)
Sparse Core Ops, SparseCore 0:
  314.4 102.4 reduce-scatter.3
where the time goes:
time: 427 us; the launch traced here: 425 us
  starting transfers between devices  161 us (38%)
  waiting for transfers between devices  144 us (34%)
  blocking collectives  78.4 us (18%)
  between operations  14.9 us (3%)
  other arithmetic  10.8 us (3%)
  local copies, waits for them, and re-layouts  6.92 us (2%)
  matrix products  4.97 us (1%)
    ppermute x32, starting transfers between devices, shifted(): return lax.ppermute(array, axis, pairs)  161 us
    unnamed x2, waiting for transfers between devices  103 us
    psum x1, blocking collectives, shards(): squares = lax.psum(jnp.sum(attended * attended, axis=1), 'col')  42.8 us
    ppermute x32, waiting for transfers between devices, shifted(): return lax.ppermute(array, axis, pairs)  41.8 us
    all_gather x1, blocking collectives, shards(): whole = lax.all_gather(hidden_in, ('row', 'col'), axis=1, tiled=True)  35.7 us
  transfers between devices with their start and end apart: 33, of which 32 were waited for; matrix products, arithmetic and copies ran while one was open for 0% of the time, Pallas kernels for 0%

commit v1 on v0

v1 whole, which is shorter than its diff:
```python
import jax
import jax.numpy as jnp
from jax import lax
from jax.experimental import pallas as pl
from jax.experimental.pallas import tpu as pltpu
from jax.sharding import Mesh, PartitionSpec as P

F32 = jnp.float32
BF16 = jnp.bfloat16
HIGHEST = lax.Precision.HIGHEST
HEAD_V = 512
WIDTH = 2048
BLOCK = 128
HEAD_K = 256
CHUNK = 128
LAST = (((1,), (1,)), ((), ()))
FIRST = (((0,), (0,)), ((), ()))

SEQ = ("x", "y")
CHIPS = ("row", "zhi")
ROWS_X, ROWS_Y = 4, 8
PIECE = BLOCK // ROWS_Y


def local_call(kernel, outs, *args, scratch=(), scalars=0):
    vmem = pl.BlockSpec(memory_space=pltpu.VMEM)
    smem = pl.BlockSpec(memory_space=pltpu.SMEM)
    return pl.pallas_call(
        kernel,
        out_shape=[jax.ShapeDtypeStruct(s, t) for s, t in outs],
        in_specs=[smem] * scalars + [vmem] * (len(args) - scalars),
        out_specs=[vmem] * len(outs),
        scratch_shapes=list(scratch),
        name=kernel.__name__,
    )(*args)


def dot(a, b, dims=(((1,), (0,)), ((), ())), precision=None):
    return lax.dot_general(a, b, dims, precision=precision, preferred_element_type=F32)


def halves(value):
    high = value.astype(BF16)
    return high, (value - high.astype(F32)).astype(BF16)


def pair_rows(value):
    high, low = halves(value)
    shape = (8, value.shape[1])
    index = lax.broadcasted_iota(jnp.int32, shape, 0)
    both = jnp.where(
        index == 0,
        jnp.broadcast_to(high.astype(F32), shape),
        jnp.where(index == 1, jnp.broadcast_to(low.astype(F32), shape), 0.0),
    )
    return both.astype(BF16)


def silu(value):
    return value * jax.nn.sigmoid(value)


def project(
    whole, gain, w_query, w_key, w_value, w_gate, w_down, pre, gate_pre, rank_part, normed
):
    chunks = WIDTH // CHUNK
    squares = jnp.zeros((BLOCK, CHUNK), F32)
    for f in range(chunks):
        activ = whole[f % 2, f // 2].astype(F32)
        squares = squares + activ * activ
    scale = lax.rsqrt(jnp.sum(squares, axis=1, keepdims=True) / WIDTH + 1e-06)
    for f in range(chunks):
        span = slice(f * CHUNK, (f + 1) * CHUNK)
        activ = whole[f % 2, f // 2].astype(F32)
        normed[:, span] = (activ * scale * gain[:, span]).astype(BF16)
    rows = normed[...]
    pre[:, :HEAD_K] = dot(rows, w_query[...])
    pre[:, HEAD_K : 2 * HEAD_K] = dot(rows, w_key[...])
    pre[:, 2 * HEAD_K :] = dot(rows, w_value[...])
    gate_pre[...] = dot(rows, w_gate[...])
    rank_part[...] = dot(rows, w_down[...])


def gates(
    index, rank_part, w_up, bias, gate_pre, head_gain, seg_ids, cumulated, gate, columns, own_rows
):
    logits = dot(rank_part[...], w_up[...].astype(F32), precision=HIGHEST) + bias[...]
    log_decay = (jnp.minimum(logits, 0.0) - jnp.log(1.0 + jnp.exp(-jnp.abs(logits)))) / 16.0
    row_iota = lax.broadcasted_iota(jnp.int32, (BLOCK, BLOCK), 0)
    col_iota = lax.broadcasted_iota(jnp.int32, (BLOCK, BLOCK), 1)
    lower = jnp.where(row_iota >= col_iota, 1.0, 0.0).astype(F32)
    cumulated[...] = dot(lower, log_decay, precision=HIGHEST)
    gate[...] = silu(gate_pre[...]) * head_gain[...]
    at = index[0]
    own = seg_ids[pl.ds(at, 1), :].astype(F32)
    before = seg_ids[pl.ds(jnp.maximum(at - 1, 0), 1), :].astype(F32)
    before = jnp.where(at > 0, before, -1.0)
    own = jnp.broadcast_to(own, (8, BLOCK))
    before = jnp.broadcast_to(before, (8, BLOCK))
    lane = lax.broadcasted_iota(jnp.int32, (8, BLOCK), 1)
    parts = [own]
    for j in range(1, 4):
        parts.append(jnp.where(lane < j, pltpu.roll(before, j, 1), pltpu.roll(own, j, 1)))
    parts.append(jnp.broadcast_to(before[:, BLOCK - 1 :], (8, BLOCK)))
    parts.append(jnp.broadcast_to(own[:, BLOCK - 1 :], (8, BLOCK)))
    parts.append(jnp.zeros((BLOCK - 8 * len(parts), BLOCK), F32))
    columns[...] = jnp.transpose(jnp.concatenate(parts, axis=0))
    own_rows[...] = own


def span(
    pre, edge, taps_q, taps_k, taps_v, cumulated, columns, own_rows, intra, reach, pieces, extended
):
    extended[0:8, :] = edge[...]
    extended[8:, :] = pre[...]
    seg = columns[:, 0:1]

    def conv(lanes, taps):
        total = taps[0:1, :] * extended[8:, lanes]
        for j in range(1, 4):
            same = columns[:, 8 * j : 8 * j + 1] == seg
            total = total + jnp.where(
                same, taps[j : j + 1, :] * extended[8 - j : 8 - j + BLOCK, lanes], 0.0
            )
        return silu(total)

    queries = conv(slice(0, HEAD_K), taps_q) * HEAD_K ** (-0.5)
    keys = conv(slice(HEAD_K, 2 * HEAD_K), taps_k)
    values = conv(slice(2 * HEAD_K, 2 * HEAD_K + CHUNK), taps_v)
    cum = cumulated[...]
    row_iota = lax.broadcasted_iota(jnp.int32, (BLOCK, BLOCK), 0)
    col_iota = lax.broadcasted_iota(jnp.int32, (BLOCK, BLOCK), 1)
    weights = jnp.zeros((BLOCK, BLOCK), F32)
    for half in (8, 16, 32, 64):
        anchors = [
            jnp.broadcast_to(cum[b + half - 1 : b + half, :], (2 * half, HEAD_K))
            for b in range(0, BLOCK, 2 * half)
        ]
        anchor = jnp.concatenate(anchors, axis=0) if len(anchors) > 1 else anchors[0]
        factor = jnp.exp(-jnp.abs(cum - anchor))
        part = dot((queries * factor).astype(BF16), (keys * factor).astype(BF16), LAST)
        inside = (
            (row_iota // (2 * half) == col_iota // (2 * half))
            & (row_iota % (2 * half) >= half)
            & (col_iota % (2 * half) < half)
        )
        weights = jnp.where(inside, part, weights)
    groups = (BLOCK // 8, 8, HEAD_K)
    cum_g, keys_g = cum.reshape(groups), keys.reshape(groups)
    queries_g = queries.reshape(groups)
    for by in range(8):
        if by:
            spread = jnp.minimum(cum_g - pltpu.roll(cum_g, by, 1), 0.0)
            product = queries_g * pltpu.roll(keys_g, by, 1) * jnp.exp(spread)
        else:
            product = queries_g * keys_g
        sums = jnp.sum(product.reshape(BLOCK, HEAD_K), axis=1, keepdims=True)
        inside = (row_iota - col_iota == by) & (row_iota % 8 >= by)
        weights = jnp.where(inside, sums, weights)
    visible = (seg == own_rows[0:1, :]) & (row_iota >= col_iota)
    weights = jnp.where(visible, weights, 0.0)
    values_b = values.astype(BF16)
    intra[...] = dot(weights.astype(BF16), values_b)
    before, last = columns[:, 32:33], columns[:, 40:41]
    reach[...] = jnp.where(seg == before, queries * jnp.exp(cum), 0.0)
    final = cum[BLOCK - 1 :, :]
    pushed = jnp.where(seg == last, keys * jnp.exp(final - cum), 0.0)
    state = dot(values_b, pushed.astype(BF16), FIRST)
    keep = jnp.where(before[0:1, :] == last[0:1, :], jnp.exp(final), 0.0)
    keep_rows = pair_rows(keep)
    for j in range(ROWS_Y):
        pieces[j, 0:PIECE, :] = state[j * PIECE : (j + 1) * PIECE, :].astype(BF16)
        pieces[j, PIECE:, :] = keep_rows


def row_scan(pieces, entering, kept, totals):
    state = jnp.zeros((PIECE, HEAD_K), F32)
    keep = jnp.ones((1, HEAD_K), F32)
    for j in range(ROWS_Y):
        entering[j] = state
        kept[j] = jnp.broadcast_to(keep, (8, HEAD_K))
        pair = pieces[j, PIECE:, :].astype(F32)
        decay = pair[0:1, :] + pair[1:2, :]
        state = state * decay + pieces[j, 0:PIECE, :].astype(F32)
        keep = keep * decay
    totals[0:PIECE, :] = state
    totals[PIECE:, :] = jnp.broadcast_to(keep, (8, HEAD_K))


def carry(entering, kept, one_back, two_back, states):
    arriving = one_back[0:PIECE, :] + one_back[PIECE : PIECE + 1, :] * two_back[0:PIECE, :]
    for j in range(ROWS_Y):
        states[j] = (entering[j] + kept[j, 0:1, :] * arriving).astype(BF16)


def attend(index, intra, reach, incoming, gate, w_out, kept, kept_squares, sent):
    high, low = halves(reach[...])
    state = incoming[...]
    attended = intra[...] + dot(high, state, LAST) + dot(low, state, LAST)
    squares = dot(jnp.ones((8, CHUNK), F32), attended * attended, LAST, precision=HIGHEST)
    terms = dot((attended * gate[...]).astype(BF16), w_out[...])
    first = index[0] == 0
    for j in range(8):
        even = terms[:, (2 * j) * CHUNK : (2 * j + 1) * CHUNK]
        odd = terms[:, (2 * j + 1) * CHUNK : (2 * j + 2) * CHUNK]
        kept[j] = jnp.where(first, even, odd)
        sent[j * BLOCK : (j + 1) * BLOCK, :] = jnp.where(first, odd, even).astype(BF16)
    kept_squares[...] = squares
    sent[8 * BLOCK :, :] = pair_rows(squares[0:1, :])


def pair_sum(kept, kept_squares, received, sent):
    other = received[8 * BLOCK :, :].astype(F32)
    squares = pair_rows(kept_squares[0:1, :] + other[0:1, :] + other[1:2, :])
    for j in range(8):
        terms = kept[j] + received[j * BLOCK : (j + 1) * BLOCK, :].astype(F32)
        sent[j, 0:BLOCK, :] = terms.astype(BF16)
        sent[j, BLOCK:, :] = squares


def finish(received, hidden, mixed):
    parts = []
    for r in range(4):
        pair = received[2 * r, BLOCK:, :].astype(F32) + received[2 * r + 1, BLOCK:, :].astype(F32)
        squares = pair[0:1, :] + pair[1:2, :]
        scale = lax.rsqrt(squares / HEAD_V + 1e-05)
        parts.append(jnp.broadcast_to(scale, (8, BLOCK)))
    parts.append(jnp.zeros((BLOCK - 8 * len(parts), BLOCK), F32))
    columns = jnp.transpose(jnp.concatenate(parts, axis=0))
    total = hidden[...].astype(F32)
    for r in range(4):
        terms = received[2 * r, 0:BLOCK, :].astype(F32)
        terms = terms + received[2 * r + 1, 0:BLOCK, :].astype(F32)
        total = total + columns[:, 8 * r : 8 * r + 1] * terms
    mixed[...] = total.astype(BF16)


def shards(
    hidden_in,
    seg_ids,
    norm_gain,
    w_query,
    w_key,
    w_value,
    w_gate,
    w_decay_down,
    w_decay_up,
    decay_bias,
    conv_query,
    conv_key,
    conv_value,
    head_gain,
    w_out,
):
    block = lax.axis_index("x") * ROWS_Y + lax.axis_index("y")
    block_at = jnp.reshape(block, (1,)).astype(jnp.int32)
    core_at = jnp.reshape(lax.axis_index("core"), (1,)).astype(jnp.int32)
    blocks = ROWS_X * ROWS_Y

    copies = jnp.broadcast_to(hidden_in[None], (8, BLOCK, CHUNK))
    of_core = lax.all_to_all(copies, CHIPS, 0, 0)
    whole = lax.all_gather(of_core, "core", axis=0)

    pre, gate_pre, rank_part = local_call(
        project,
        [((BLOCK, 2 * HEAD_K + CHUNK), F32), ((BLOCK, CHUNK), F32), ((BLOCK, 16), F32)],
        whole,
        norm_gain.reshape(1, WIDTH),
        w_query,
        w_key,
        w_value,
        w_gate,
        w_decay_down,
        scratch=[pltpu.VMEM((BLOCK, WIDTH), BF16)],
    )
    edge = lax.ppermute(pre[BLOCK - 8 :], SEQ, [(i, i + 1) for i in range(blocks - 1)])
    cumulated, gate, columns, own_rows = local_call(
        gates,
        [
            ((BLOCK, HEAD_K), F32),
            ((BLOCK, CHUNK), F32),
            ((BLOCK, BLOCK), F32),
            ((8, BLOCK), F32),
        ],
        block_at,
        rank_part,
        w_decay_up,
        decay_bias.reshape(1, HEAD_K),
        gate_pre,
        head_gain.reshape(1, CHUNK),
        seg_ids.reshape(blocks, BLOCK),
        scalars=1,
    )
    intra, reach, pieces = local_call(
        span,
        [
            ((BLOCK, CHUNK), F32),
            ((BLOCK, HEAD_K), F32),
            ((ROWS_Y, PIECE + 8, HEAD_K), BF16),
        ],
        pre,
        edge,
        conv_query,
        conv_key,
        conv_value,
        cumulated,
        columns,
        own_rows,
        scratch=[pltpu.VMEM((BLOCK + 8, 2 * HEAD_K + CHUNK), F32)],
    )
    entering, kept, totals = local_call(
        row_scan,
        [
            ((ROWS_Y, PIECE, HEAD_K), F32),
            ((ROWS_Y, 8, HEAD_K), F32),
            ((PIECE + 8, HEAD_K), F32),
        ],
        lax.all_to_all(pieces, "y", 0, 0),
    )
    one_back = lax.ppermute(totals, "x", [(i, i + 1) for i in range(ROWS_X - 1)])
    two_back = lax.ppermute(totals, "x", [(i, i + 2) for i in range(ROWS_X - 2)])
    (states,) = local_call(
        carry, [((ROWS_Y, PIECE, HEAD_K), BF16)], entering, kept, one_back, two_back
    )
    incoming = lax.all_to_all(states, "y", 0, 0).reshape(CHUNK, HEAD_K)
    mine, my_squares, sent = local_call(
        attend,
        [((8, BLOCK, CHUNK), F32), ((8, BLOCK), F32), ((8 * BLOCK + 8, CHUNK), BF16)],
        core_at,
        intra,
        reach,
        incoming,
        gate,
        w_out,
        scalars=1,
    )
    theirs = lax.ppermute(sent, "core", [(0, 1), (1, 0)])
    (pairs,) = local_call(
        pair_sum, [((8, BLOCK + 8, CHUNK), BF16)], mine, my_squares, theirs
    )
    arrived = lax.all_to_all(pairs, CHIPS, 0, 0)
    (mixed,) = local_call(finish, [((BLOCK, CHUNK), BF16)], arrived, hidden_in)
    return mixed


def solution(mesh):
    finer = Mesh(mesh.devices.reshape(ROWS_X, ROWS_Y, 4, 2, 2), ("x", "y", "row", "zhi", "core"))
    part = ("row", "zhi", "core")
    return jax.shard_map(
        shards,
        mesh=finer,
        in_specs=(
            P(SEQ, part),
            P(),
            P(),
            P(None, "row"),
            P(None, "row"),
            P(None, part),
            P(None, part),
            P(),
            P(None, "row"),
            P("row"),
            P(None, "row"),
            P(None, "row"),
            P(None, part),
            P(("zhi", "core")),
            P(part, None),
        ),
        out_specs=P(SEQ, part),
        check_vma=False,
    )
```

time: 427 us -> 109 us (0.26)
  the two profiles are of different devices: /device:TPU:1 before, /device:TPU:2 now
where the time goes in v1:
time: 109 us; the launch traced here: 108 us
  blocking collectives  34.4 us (32%)
  starting transfers between devices  25.1 us (23%)
  waiting for transfers between devices  23.8 us (22%)
  Pallas kernels  18.5 us (17%)
  local copies, waits for them, and re-layouts  5.77 us (5%)
    pallas_call x8, Pallas kernels, local_call(): pl.pallas_call(kernel, out_shape=[jax.ShapeDtypeStruct(s, t) for s, t in...  18.5 us
    all_to_all x1, blocking collectives, shards(): arrived = lax.all_to_all(pairs, CHIPS, 0, 0)  17.1 us
    all_to_all x1, blocking collectives, shards(): lax.all_to_all(pieces, 'y', 0, 0)  15 us
    all_to_all x1, starting transfers between devices, shards(): of_core = lax.all_to_all(copies, CHIPS, 0, 0)  10.4 us
    all_to_all x1, waiting for transfers between devices, shards(): incoming = lax.all_to_all(states, 'y', 0, 0).reshape(CHUNK, HEAD_K)  8.29 us
    all_to_all x1, waiting for transfers between devices, shards(): of_core = lax.all_to_all(copies, CHIPS, 0, 0)  7.82 us
    ppermute x1, starting transfers between devices, shards(): lax.ppermute(totals, 'x', [(i, i + 2) for i in range(ROWS_X - 2)])  4.01 us
    ppermute x1, waiting for transfers between devices, shards(): lax.ppermute(totals, 'x', [(i, i + 1) for i in range(ROWS_X - 1)])  3.98 us
  transfers between devices with their start and end apart: 6, of which 5 were waited for; matrix products, arithmetic and copies ran while one was open for 1% of the time, Pallas kernels for 2%

profile of v1, /device:TPU:2, one launch (start us, length us, event | category | flops | bytes accessed | tf_op | source)
XLA Modules:
  0.0 107.7 jit_solution(10856791637967630658)
XLA Ops:
  0.0 1.5 %broadcast_in_dim.2 = bf16[8,128,128]{2,1,0:T(8,128)(2,1)} broadcast(bf16[128,128]{1,0:T(8,128)(2,1)} %hidden.1), dimensions={1,2} | broadcast | bytes 294912 | tf_op jit(solution)/shard_map/broadcast_in_dim | solution.py:260
  1.5 10.4 %all-to-all-start = ((bf16[8,128,128]{2,1,0:T(8,128)(2,1)}), bf16[8,128,128]{2,1,0:T(8,128)(2,1)S(1)}, u32[]{:S(2)}, u32[]{:S(2)}) async-start(bf16[8,128,128]{2,1,0:T(8,128)(2,1)} %broadcast_in_dim.2), calls=%async_computation | async-start | bytes 524288 | tf_op jit(solution)/shard_map/all_to_all | solution.py:261
  11.9 1.0 copy.17.w_down
  13.0 7.8 %all-to-all-done = bf16[8,128,128]{2,1,0:T(8,128)(2,1)S(1)} async-done(((bf16[8,128,128]{2,1,0:T(8,128)(2,1)}), bf16[8,128,128]{2,1,0:T(8,128)(2,1)S(1)}, u32[]{:S(2)}, u32[]{:S(2)}) %all-to-all-start) | async-done | bytes 262176 | tf_op jit(solution)/shard_map/all_to_all | solution.py:261
  20.8 2.3 %all-gather = bf16[16,128,128]{2,1,0:T(8,128)(2,1)} all-gather(bf16[8,128,128]{2,1,0:T(8,128)(2,1)S(1)} %all-to-all-done), channel_id=2, replica_groups=mesh['x'=4,'y'=8,'row'=4,'zhi'=2,'core'=2] {'core'}, dimensions={0}, use_global_device_ids=true | all-gather | bytes 786432 | tf_op jit(solution)/shard_map/all_gather | solution.py:262
  23.1 3.8 %project.1 = (f32[128,640]{1,0:T(8,128)}, f32[128,128]{1,0:T(8,128)}, f32[128,16]{1,0:T(8,128)}) custom-call(bf16[2,8,128,128]{3,2,1,0:T(8,128)(2,1)} %bitcast.8, f32[1,2048]{1,0:T(1,128)} %bitcast.11, bf16[2048,256]{1,0:T(8,128)(2,1)} %w_query.1, bf16[2048,256]{1,0:T(8,128)(2,1)} %w_key.1, bf16[2048,128]{1,0:T(8,128)(2,1)} %w_value.1, ...), custom_call_target="tpu_custom_call" | custom-call | tf_op jit(solution)/shard_map/project/pallas_call | solution.py:28
  27.6 3.5 %collective-permute-start = (f32[8,640]{1,0:T(8,128)S(1)}, f32[8,640]{1,0:T(8,128)S(1)}, u32[]{:S(2)}, u32[]{:S(2)}) collective-permute-start(f32[8,640]{1,0:T(8,128)S(1)} %slice.3), channel_id=1, source_target_pairs={{0,16},{16,32},{32,48},{48,64},{64,80},{80,96},{96,112},{112,128},... | collective-permute-start | bytes 61448 | tf_op jit(solution)/shard_map/ppermute | solution.py:276
  31.1 2.3 %gates.1 = (f32[128,256]{1,0:T(8,128)}, f32[128,128]{1,0:T(8,128)}, f32[128,128]{1,0:T(8,128)}, f32[8,128]{1,0:T(8,128)}) custom-call(s32[1]{0:T(128)} %bitcast.3.index, f32[128,16]{1,0:T(8,128)} %get-tuple-element.22.rank_part, bf16[16,256]{1,0:T(8,128)(2,1)} %w_up.1, f32[1,256]{1,0:T(1,128)} %bitcast.12, f32[128,128]{1,0:T(8,128)} %get-tuple-element.23.gate_pre, ...), custom_call_target="tpu_custom_call" | custom-call | tf_op jit(solution)/shard_map/gates/pallas_call | solution.py:28
  33.3 2.0 %collective-permute-done.edge = f32[8,640]{1,0:T(8,128)S(1)} collective-permute-done((f32[8,640]{1,0:T(8,128)S(1)}, f32[8,640]{1,0:T(8,128)S(1)}, u32[]{:S(2)}, u32[]{:S(2)}) %collective-permute-start) | collective-permute-done | bytes 20512 | tf_op jit(solution)/shard_map/ppermute | solution.py:276
  36.0 2.9 %span.1 = (f32[128,128]{1,0:T(8,128)}, f32[128,256]{1,0:T(8,128)}, bf16[8,24,256]{2,1,0:T(8,128)(2,1)}) custom-call(f32[128,640]{1,0:T(8,128)} %get-tuple-element.21.pre, f32[8,640]{1,0:T(8,128)} %copy-done.5, f32[4,256]{1,0:T(4,128)} %taps_q.1, f32[4,256]{1,0:T(4,128)} %taps_k.1, f32[4,128]{1,0:T(4,128)} %taps_v.1, f32[128,256]{1,0:T(8,128)} %get-tuple-element.24.cumulated, ...), custom_call_target="tpu_custom_call" | custom-call | tf_op jit(solution)/shard_map/span/pallas_call | solution.py:28
  38.9 15.0 %all_to_all.20.pieces = bf16[8,24,256]{2,1,0:T(8,128)(2,1)} all-to-all(bf16[8,24,256]{2,1,0:T(8,128)(2,1)} %get-tuple-element.29), channel_id=1, replica_groups=mesh['x'=4,'y'=8,'row'=4,'zhi'=2,'core'=2] {'y'}, dimensions={0} | all-to-all | bytes 196608 | tf_op jit(solution)/shard_map/all_to_all | solution.py:318
  53.9 1.6 %row_scan.1 = (f32[8,16,256]{2,1,0:T(8,128)}, f32[8,8,256]{2,1,0:T(8,128)}, f32[24,256]{1,0:T(8,128)}) custom-call(bf16[8,24,256]{2,1,0:T(8,128)(2,1)} %all_to_all.20.pieces), custom_call_target="tpu_custom_call" | custom-call | tf_op jit(solution)/shard_map/row_scan/pallas_call | solution.py:28
  55.5 4.0 %collective-permute-start.2 = (f32[24,256]{1,0:T(8,128)}, f32[24,256]{1,0:T(8,128)S(1)}, u32[]{:S(2)}, u32[]{:S(2)}) collective-permute-start(f32[24,256]{1,0:T(8,128)} %get-tuple-element.32), channel_id=1, source_target_pairs={{0,256},{128,384},{1,257},{129,385},{2,258},{130,386},{3,259},{131... | collective-permute-start | bytes 73736 | tf_op jit(solution)/shard_map/ppermute | solution.py:321
  59.5 1.9 %collective-permute-start.1 = (f32[24,256]{1,0:T(8,128)}, f32[24,256]{1,0:T(8,128)S(1)}, u32[]{:S(2)}, u32[]{:S(2)}) collective-permute-start(f32[24,256]{1,0:T(8,128)} %get-tuple-element.32), channel_id=1, source_target_pairs={{0,128},{128,256},{256,384},{1,129},{129,257},{257,385},{2,130},{1... | collective-permute-start | bytes 73736 | tf_op jit(solution)/shard_map/ppermute | solution.py:320
  61.5 4.0 %collective-permute-done.1.one_back = f32[24,256]{1,0:T(8,128)S(1)} collective-permute-done((f32[24,256]{1,0:T(8,128)}, f32[24,256]{1,0:T(8,128)S(1)}, u32[]{:S(2)}, u32[]{:S(2)}) %collective-permute-start.1) | collective-permute-done | bytes 24608 | tf_op jit(solution)/shard_map/ppermute | solution.py:320
  66.1 1.6 %carry.1 = bf16[8,16,256]{2,1,0:T(8,128)(2,1)} custom-call(f32[8,16,256]{2,1,0:T(8,128)} %get-tuple-element.30.entering, f32[8,8,256]{2,1,0:T(8,128)} %get-tuple-element.31.kept, f32[24,256]{1,0:T(8,128)} %copy-done.4, f32[24,256]{1,0:T(8,128)} %copy-done.3), custom_call_target="tpu_custom_call" | custom-call | tf_op jit(solution)/shard_map/carry/pallas_call | solution.py:28
  67.6 3.3 %all-to-all-start.2 = ((bf16[8,16,256]{2,1,0:T(8,128)(2,1)}), bf16[8,16,256]{2,1,0:T(8,128)(2,1)S(1)}, u32[]{:S(2)}, u32[]{:S(2)}) async-start(bf16[8,16,256]{2,1,0:T(8,128)(2,1)} %carry.1), calls=%async_computation.2 | async-start | bytes 131072 | tf_op jit(solution)/shard_map/all_to_all | solution.py:325
  71.0 8.3 %all-to-all-done.2 = bf16[8,16,256]{2,1,0:T(8,128)(2,1)S(1)} async-done(((bf16[8,16,256]{2,1,0:T(8,128)(2,1)}), bf16[8,16,256]{2,1,0:T(8,128)(2,1)S(1)}, u32[]{:S(2)}, u32[]{:S(2)}) %all-to-all-start.2) | async-done | bytes 65568 | tf_op jit(solution)/shard_map/all_to_all | solution.py:325
  79.9 2.7 %attend.1 = (f32[8,128,128]{2,1,0:T(8,128)}, f32[8,128]{1,0:T(8,128)}, bf16[1032,128]{1,0:T(8,128)(2,1)}) custom-call(s32[1]{0:T(128)} %bitcast.index, f32[128,128]{1,0:T(8,128)} %get-tuple-element.27.intra, f32[128,256]{1,0:T(8,128)} %get-tuple-element.28.reach, bf16[128,256]{1,0:T(8,128)(2,1)} %bitcast.9, f32[128,128]{1,0:T(8,128)} %get-tuple-element.33.gate, ...), custom_call_target="tpu_custom_call" | custom-call | tf_op jit(solution)/shard_map/attend/pallas_call | solution.py:28
  82.6 1.9 %collective-permute-start.3 = (bf16[1032,128]{1,0:T(8,128)(2,1)}, bf16[1032,128]{1,0:T(8,128)(2,1)S(1)}, u32[]{:S(2)}, u32[]{:S(2)}) collective-permute-start(bf16[1032,128]{1,0:T(8,128)(2,1)} %get-tuple-element.36), channel_id=1, source_target_pairs={{0,1},{1,0},{2,3},{3,2},{4,5},{5,4},{6,7},{7,6},{8,9},{9,8},{10,11... | collective-permute-start | bytes 792584 | tf_op jit(solution)/shard_map/ppermute | solution.py:337
  84.5 1.7 %collective-permute-done.3.received = bf16[1032,128]{1,0:T(8,128)(2,1)S(1)} collective-permute-done((bf16[1032,128]{1,0:T(8,128)(2,1)}, bf16[1032,128]{1,0:T(8,128)(2,1)S(1)}, u32[]{:S(2)}, u32[]{:S(2)}) %collective-permute-start.3) | collective-permute-done | bytes 264224 | tf_op jit(solution)/shard_map/ppermute | solution.py:337
  86.9 1.9 %pair_sum.1 = bf16[8,136,128]{2,1,0:T(8,128)(2,1)} custom-call(f32[8,128,128]{2,1,0:T(8,128)} %get-tuple-element.34.kept, f32[8,128]{1,0:T(8,128)} %get-tuple-element.35.kept_squares, bf16[1032,128]{1,0:T(8,128)(2,1)} %copy-done), custom_call_target="tpu_custom_call" | custom-call | tf_op jit(solution)/shard_map/pair_sum/pallas_call | solution.py:28
  88.8 17.1 %all_to_all.21.received = bf16[8,136,128]{2,1,0:T(8,128)(2,1)} all-to-all(bf16[8,136,128]{2,1,0:T(8,128)(2,1)} %pair_sum.1), channel_id=1, replica_groups=mesh['x'=4,'y'=8,'row'=4,'zhi'=2,'core'=2] {'row','zhi'}, dimensions={0} | all-to-all | bytes 557056 | tf_op jit(solution)/shard_map/all_to_all | solution.py:341
  105.9 1.8 %finish.1 = bf16[128,128]{1,0:T(8,128)(2,1)} custom-call(bf16[8,136,128]{2,1,0:T(8,128)(2,1)} %all_to_all.21.received, bf16[128,128]{1,0:T(8,128)(2,1)} %hidden.1), custom_call_target="tpu_custom_call" | custom-call | tf_op jit(solution)/shard_map/finish/pallas_call | solution.py:28
  (14 shorter events, 3.3 us)
Async XLA Ops:
  1.5 10.5 %copy-start.2 = (bf16[2048,16]{0,1:T(8,128)(2,1)S(1)}, bf16[2048,16]{0,1:T(8,128)(2,1)}, u32[]{:S(2)}) copy-start(bf16[2048,16]{0,1:T(8,128)(2,1)} %param.22) | copy-start | bytes 196612
  1.5 19.3 %all-to-all-start = ((bf16[8,128,128]{2,1,0:T(8,128)(2,1)}), bf16[8,128,128]{2,1,0:T(8,128)(2,1)S(1)}, u32[]{:S(2)}, u32[]{:S(2)}) async-start(bf16[8,128,128]{2,1,0:T(8,128)(2,1)} %broadcast_in_dim.2), calls=%async_computation | async-start | bytes 524288 | tf_op jit(solution)/shard_map/all_to_all | solution.py:261
  27.6 7.8 %collective-permute-start = (f32[8,640]{1,0:T(8,128)S(1)}, f32[8,640]{1,0:T(8,128)S(1)}, u32[]{:S(2)}, u32[]{:S(2)}) collective-permute-start(f32[8,640]{1,0:T(8,128)S(1)} %slice.3), channel_id=1, source_target_pairs={{0,16},{16,32},{32,48},{48,64},{64,80},{80,96},{96,112},{112,128},... | collective-permute-start | bytes 61448 | tf_op jit(solution)/shard_map/ppermute | solution.py:276
  35.4 0.6 copy-start.5
  55.5 6.0 %collective-permute-start.2 = (f32[24,256]{1,0:T(8,128)}, f32[24,256]{1,0:T(8,128)S(1)}, u32[]{:S(2)}, u32[]{:S(2)}) collective-permute-start(f32[24,256]{1,0:T(8,128)} %get-tuple-element.32), channel_id=1, source_target_pairs={{0,256},{128,384},{1,257},{129,385},{2,258},{130,386},{3,259},{131... | collective-permute-start | bytes 73736 | tf_op jit(solution)/shard_map/ppermute | solution.py:321
  59.5 5.9 %collective-permute-start.1 = (f32[24,256]{1,0:T(8,128)}, f32[24,256]{1,0:T(8,128)S(1)}, u32[]{:S(2)}, u32[]{:S(2)}) collective-permute-start(f32[24,256]{1,0:T(8,128)} %get-tuple-element.32), channel_id=1, source_target_pairs={{0,128},{128,256},{256,384},{1,129},{129,257},{257,385},{2,130},{1... | collective-permute-start | bytes 73736 | tf_op jit(solution)/shard_map/ppermute | solution.py:320
  61.5 4.0 %copy-start.3 = (f32[24,256]{1,0:T(8,128)}, f32[24,256]{1,0:T(8,128)S(1)}, u32[]{:S(2)}) copy-start(f32[24,256]{1,0:T(8,128)S(1)} %collective-permute-done.2.two_back) | copy-start | bytes 73732
  65.5 0.6 copy-start.4
  67.6 11.7 %all-to-all-start.2 = ((bf16[8,16,256]{2,1,0:T(8,128)(2,1)}), bf16[8,16,256]{2,1,0:T(8,128)(2,1)S(1)}, u32[]{:S(2)}, u32[]{:S(2)}) async-start(bf16[8,16,256]{2,1,0:T(8,128)(2,1)} %carry.1), calls=%async_computation.2 | async-start | bytes 131072 | tf_op jit(solution)/shard_map/all_to_all | solution.py:325
  79.3 0.6 copy-start.1
  82.6 3.6 %collective-permute-start.3 = (bf16[1032,128]{1,0:T(8,128)(2,1)}, bf16[1032,128]{1,0:T(8,128)(2,1)S(1)}, u32[]{:S(2)}, u32[]{:S(2)}) collective-permute-start(bf16[1032,128]{1,0:T(8,128)(2,1)} %get-tuple-element.36), channel_id=1, source_target_pairs={{0,1},{1,0},{2,3},{3,2},{4,5},{5,4},{6,7},{7,6},{8,9},{9,8},{10,11... | collective-permute-start | bytes 792584 | tf_op jit(solution)/shard_map/ppermute | solution.py:337
  86.2 0.7 copy-start

commit v2 on v1

--- a/solution.py
+++ b/solution.py
@@ -22,16 +22,21 @@
 PIECE = BLOCK // ROWS_Y
 
 
-def local_call(kernel, outs, *args, scratch=(), scalars=0):
+def local_call(kernel, outs, *args, scratch=(), scalars=0, plain=(), last=False):
     vmem = pl.BlockSpec(memory_space=pltpu.VMEM)
     smem = pl.BlockSpec(memory_space=pltpu.SMEM)
+    args = [
+        a if i < scalars or i in plain else pltpu.with_memory_space_constraint(a, pltpu.VMEM)
+        for i, a in enumerate(args)
+    ]
     return pl.pallas_call(
         kernel,
-        out_shape=[jax.ShapeDtypeStruct(s, t) for s, t in outs],
+        out_shape=[jax.ShapeDtypeStruct(s, t) if last else pltpu.VMEM(s, t) for s, t in outs],
         in_specs=[smem] * scalars + [vmem] * (len(args) - scalars),
         out_specs=[vmem] * len(outs),
         scratch_shapes=list(scratch),
         name=kernel.__name__,
+        compiler_params=pltpu.CompilerParams(vmem_limit_bytes=16 << 20),
     )(*args)
 
 
@@ -60,8 +65,13 @@
     return value * jax.nn.sigmoid(value)
 
 
+def spread_out(hidden, copies):
+    for j in range(8):
+        copies[j] = hidden[...]
+
+
 def project(
-    whole, gain, w_query, w_key, w_value, w_gate, w_down, pre, gate_pre, rank_part, normed
+    whole, gain, w_query, w_key, w_value, w_gate, w_down, pre, tail, gate_pre, rank_part, normed
 ):
     chunks = WIDTH // CHUNK
     squares = jnp.zeros((BLOCK, CHUNK), F32)
@@ -77,8 +87,9 @@
     pre[:, :HEAD_K] = dot(rows, w_query[...])
     pre[:, HEAD_K : 2 * HEAD_K] = dot(rows, w_key[...])
     pre[:, 2 * HEAD_K :] = dot(rows, w_value[...])
+    tail[...] = pre[BLOCK - 8 :, :]
     gate_pre[...] = dot(rows, w_gate[...])
-    rank_part[...] = dot(rows, w_down[...])
+    rank_part[...] = dot(rows, w_down[...], LAST)
 
 
 def gates(
@@ -209,7 +220,8 @@
     sent[8 * BLOCK :, :] = pair_rows(squares[0:1, :])
 
 
-def pair_sum(kept, kept_squares, received, sent):
+def pair_sum(index, kept, kept_squares, both, sent):
+    received = both.at[1 - index[0]]
     other = received[8 * BLOCK :, :].astype(F32)
     squares = pair_rows(kept_squares[0:1, :] + other[0:1, :] + other[1:2, :])
     for j in range(8):
@@ -257,23 +269,28 @@
     core_at = jnp.reshape(lax.axis_index("core"), (1,)).astype(jnp.int32)
     blocks = ROWS_X * ROWS_Y
 
-    copies = jnp.broadcast_to(hidden_in[None], (8, BLOCK, CHUNK))
+    (copies,) = local_call(spread_out, [((8, BLOCK, CHUNK), BF16)], hidden_in, plain=(0,))
     of_core = lax.all_to_all(copies, CHIPS, 0, 0)
     whole = lax.all_gather(of_core, "core", axis=0)
 
-    pre, gate_pre, rank_part = local_call(
+    pre, tail, gate_pre, rank_part = local_call(
         project,
-        [((BLOCK, 2 * HEAD_K + CHUNK), F32), ((BLOCK, CHUNK), F32), ((BLOCK, 16), F32)],
+        [
+            ((BLOCK, 2 * HEAD_K + CHUNK), F32),
+            ((8, 2 * HEAD_K + CHUNK), F32),
+            ((BLOCK, CHUNK), F32),
+            ((BLOCK, 16), F32),
+        ],
         whole,
         norm_gain.reshape(1, WIDTH),
         w_query,
         w_key,
         w_value,
         w_gate,
-        w_decay_down,
+        w_decay_down.T,
         scratch=[pltpu.VMEM((BLOCK, WIDTH), BF16)],
     )
-    edge = lax.ppermute(pre[BLOCK - 8 :], SEQ, [(i, i + 1) for i in range(blocks - 1)])
+    edge = lax.ppermute(tail, SEQ, [(i, i + 1) for i in range(blocks - 1)])
     cumulated, gate, columns, own_rows = local_call(
         gates,
         [
@@ -334,12 +351,14 @@
         w_out,
         scalars=1,
     )
-    theirs = lax.ppermute(sent, "core", [(0, 1), (1, 0)])
+    both = lax.all_gather(sent, "core", axis=0)
     (pairs,) = local_call(
-        pair_sum, [((8, BLOCK + 8, CHUNK), BF16)], mine, my_squares, theirs
+        pair_sum, [((8, BLOCK + 8, CHUNK), BF16)], core_at, mine, my_squares, both, scalars=1
     )
     arrived = lax.all_to_all(pairs, CHIPS, 0, 0)
-    (mixed,) = local_call(finish, [((BLOCK, CHUNK), BF16)], arrived, hidden_in)
+    (mixed,) = local_call(
+        finish, [((BLOCK, CHUNK), BF16)], arrived, hidden_in, plain=(1,), last=True
+    )
     return mixed
 
 

time: 109 us -> 93.4 us (0.86)
  blocking collectives: 34.4 us -> 54.4 us
  Pallas kernels: 18.5 us -> 5.07 us
  starting transfers between devices: 25.1 us -> 12.8 us
  waiting for transfers between devices: 23.8 us -> 15 us
    all_to_all x0 -> x1, blocking collectives: none -> 19 us  [shards(): of_core = lax.all_to_all(copies, CHIPS, 0, 0)]
    pallas_call x8 -> x9, Pallas kernels: 18.5 us -> 5.07 us  [local_call(): pl.pallas_call(kernel, out_shape=[jax.ShapeDtypeStruct(s, t) if last else...]
    all_to_all x1 -> x0, starting transfers between devices: 10.4 us -> none  [shards(): of_core = lax.all_to_all(copies, CHIPS, 0, 0)]
    all_to_all x1 -> x0, waiting for transfers between devices: 7.82 us -> none  [shards(): of_core = lax.all_to_all(copies, CHIPS, 0, 0)]
    all_gather x0 -> x1, blocking collectives: none -> 2.18 us  [shards(): both = lax.all_gather(sent, 'core', axis=0)]
    ppermute x2 -> x1, starting transfers between devices: 5.38 us -> 3.49 us  [shards(): edge = lax.ppermute(tail, SEQ, [(i, i + 1) for i in range(blocks - 1)])]
    unnamed x13 -> x32, local copies, waits for them, and re-layouts: 3.55 us -> 5.33 us
    broadcast_in_dim x1 -> x0, local copies, waits for them, and re-layouts: 1.49 us -> none  [shards(): copies = jnp.broadcast_to(hidden_in[None], (8, BLOCK, CHUNK))]
  transfers between devices with their start and end apart: 6 -> 4, of which waited for: 5 -> 3; matrix products, arithmetic and copies ran while one was open for 1% -> 0% of each run, Pallas kernels for 2% -> 1%
where the time goes in v2:
time: 93.4 us; the launch traced here: 92.7 us
  blocking collectives  54.4 us (58%)
  waiting for transfers between devices  15 us (16%)
  starting transfers between devices  12.8 us (14%)
  local copies, waits for them, and re-layouts  5.33 us (6%)
  Pallas kernels  5.07 us (5%)
    all_to_all x1, blocking collectives, shards(): of_core = lax.all_to_all(copies, CHIPS, 0, 0)  19 us
    all_to_all x1, blocking collectives, shards(): arrived = lax.all_to_all(pairs, CHIPS, 0, 0)  16.2 us
    all_to_all x1, blocking collectives, shards(): lax.all_to_all(pieces, 'y', 0, 0)  14.7 us
    all_to_all x1, waiting for transfers between devices, shards(): incoming = lax.all_to_all(states, 'y', 0, 0).reshape(CHUNK, HEAD_K)  8.3 us
    unnamed x32, local copies, waits for them, and re-layouts  5.33 us
    pallas_call x9, Pallas kernels, local_call(): pl.pallas_call(kernel, out_shape=[jax.ShapeDtypeStruct(s, t) if last else...  5.07 us
    ppermute x1, starting transfers between devices, shards(): lax.ppermute(totals, 'x', [(i, i + 2) for i in range(ROWS_X - 2)])  4.03 us
    ppermute x1, waiting for transfers between devices, shards(): lax.ppermute(totals, 'x', [(i, i + 1) for i in range(ROWS_X - 1)])  3.78 us
  transfers between devices with their start and end apart: 4, of which 3 were waited for; matrix products, arithmetic and copies ran while one was open for 0% of the time, Pallas kernels for 1%

profile of v2, /device:TPU:2, one launch (start us, length us, event | category | flops | bytes accessed | tf_op | source)
XLA Modules:
  0.0 92.7 jit_solution(6465866622885774599)
XLA Ops:
  0.0 0.8 copy-done.5
  0.9 19.0 %all_to_all.20 = bf16[8,128,128]{2,1,0:T(8,128)(2,1)S(1)} all-to-all(bf16[8,128,128]{2,1,0:T(8,128)(2,1)S(1)} %spread_out.1), channel_id=1, replica_groups=mesh['x'=4,'y'=8,'row'=4,'zhi'=2,'core'=2] {'row','zhi'}, dimensions={0} | all-to-all | bytes 524288 | tf_op jit(solution)/shard_map/all_to_all | solution.py:273
  19.9 2.3 %all-gather = bf16[16,128,128]{2,1,0:T(8,128)(2,1)S(1)} all-gather(bf16[8,128,128]{2,1,0:T(8,128)(2,1)S(1)} %all_to_all.20), channel_id=2, replica_groups=mesh['x'=4,'y'=8,'row'=4,'zhi'=2,'core'=2] {'core'}, dimensions={0}, use_global_device_ids=true | all-gather | bytes 786432 | tf_op jit(solution)/shard_map/all_gather | solution.py:274
  22.2 1.2 %copy-done.1 = bf16[2048,256]{1,0:T(8,128)(2,1)S(1)} copy-done((bf16[2048,256]{1,0:T(8,128)(2,1)S(1)}, bf16[2048,256]{1,0:T(8,128)(2,1)}, u32[]{:S(2)}) %copy-start.1) | copy-done | bytes 1048600
  23.4 1.0 %copy-done.3 = bf16[2048,128]{1,0:T(8,128)(2,1)S(1)} copy-done((bf16[2048,128]{1,0:T(8,128)(2,1)S(1)}, bf16[2048,128]{1,0:T(8,128)(2,1)}, u32[]{:S(2)}) %copy-start.3) | copy-done | bytes 524312
  24.4 0.8 copy-done.7
  25.3 1.0 %project.1 = (f32[128,640]{1,0:T(8,128)S(1)}, f32[8,640]{1,0:T(8,128)S(1)}, f32[128,128]{1,0:T(8,128)S(1)}, f32[128,16]{1,0:T(8,128)S(1)}) custom-call(bf16[2,8,128,128]{3,2,1,0:T(8,128)(2,1)S(1)} %bitcast.11, f32[1,2048]{1,0:T(1,128)S(1)} %bitcast.15, bf16[2048,256]{1,0:T(8,128)(2,1)S(1)} %copy-done, bf16[2048,256]{1,0:T(8,128)(2,1)S(1)} %copy-done.1, ...), custom_call_target="tpu_custom_call" | custom-call | tf_op jit(solution)/shard_map/project/pallas_call | solution.py:32
  26.3 3.5 %collective-permute-start = (f32[8,640]{1,0:T(8,128)S(1)}, f32[8,640]{1,0:T(8,128)S(1)}, u32[]{:S(2)}, u32[]{:S(2)}) collective-permute-start(f32[8,640]{1,0:T(8,128)S(1)} %get-tuple-element.23), channel_id=1, source_target_pairs={{0,16},{16,32},{32,48},{48,64},{64,80},{80,96},{96,112},{112,128},... | collective-permute-start | bytes 61448 | tf_op jit(solution)/shard_map/ppermute | solution.py:293
  29.9 0.7 copy-done.10
  30.5 0.7 gates.1
  31.2 2.9 %collective-permute-done.edge = f32[8,640]{1,0:T(8,128)S(1)} collective-permute-done((f32[8,640]{1,0:T(8,128)S(1)}, f32[8,640]{1,0:T(8,128)S(1)}, u32[]{:S(2)}, u32[]{:S(2)}) %collective-permute-start) | collective-permute-done | bytes 20512 | tf_op jit(solution)/shard_map/ppermute | solution.py:293
  34.1 0.7 copy-done.13
  34.8 1.1 %span.1 = (f32[128,128]{1,0:T(8,128)S(1)}, f32[128,256]{1,0:T(8,128)S(1)}, bf16[8,24,256]{2,1,0:T(8,128)(2,1)S(1)}) custom-call(f32[128,640]{1,0:T(8,128)S(1)} %get-tuple-element.22.pre, f32[8,640]{1,0:T(8,128)S(1)} %collective-permute-done.edge, f32[4,256]{1,0:T(4,128)S(1)} %copy-done.11, f32[4,256]{1,0:T(4,128)S(1)} %copy-done.12, ...), custom_call_target="tpu_custom_call" | custom-call | tf_op jit(solution)/shard_map/span/pallas_call | solution.py:32
  35.9 14.7 %all_to_all.21.pieces = bf16[8,24,256]{2,1,0:T(8,128)(2,1)S(1)} all-to-all(bf16[8,24,256]{2,1,0:T(8,128)(2,1)S(1)} %get-tuple-element.31), channel_id=1, replica_groups=mesh['x'=4,'y'=8,'row'=4,'zhi'=2,'core'=2] {'y'}, dimensions={0} | all-to-all | bytes 196608 | tf_op jit(solution)/shard_map/all_to_all | solution.py:335
  50.7 4.0 %collective-permute-start.2 = (f32[24,256]{1,0:T(8,128)S(1)}, f32[24,256]{1,0:T(8,128)S(1)}, u32[]{:S(2)}, u32[]{:S(2)}) collective-permute-start(f32[24,256]{1,0:T(8,128)S(1)} %get-tuple-element.34), channel_id=1, source_target_pairs={{0,256},{128,384},{1,257},{129,385},{2,258},{130,386},{3,259},{131... | collective-permute-start | bytes 73736 | tf_op jit(solution)/shard_map/ppermute | solution.py:338
  54.7 1.9 %collective-permute-start.1 = (f32[24,256]{1,0:T(8,128)S(1)}, f32[24,256]{1,0:T(8,128)S(1)}, u32[]{:S(2)}, u32[]{:S(2)}) collective-permute-start(f32[24,256]{1,0:T(8,128)S(1)} %get-tuple-element.34), channel_id=1, source_target_pairs={{0,128},{128,256},{256,384},{1,129},{129,257},{257,385},{2,130},{1... | collective-permute-start | bytes 73736 | tf_op jit(solution)/shard_map/ppermute | solution.py:337
  56.6 3.8 %collective-permute-done.1.one_back = f32[24,256]{1,0:T(8,128)S(1)} collective-permute-done((f32[24,256]{1,0:T(8,128)S(1)}, f32[24,256]{1,0:T(8,128)S(1)}, u32[]{:S(2)}, u32[]{:S(2)}) %collective-permute-start.1) | collective-permute-done | bytes 24608 | tf_op jit(solution)/shard_map/ppermute | solution.py:337
  60.4 0.6 carry.1
  61.1 3.3 %all-to-all-start.2 = ((bf16[8,16,256]{2,1,0:T(8,128)(2,1)}), bf16[8,16,256]{2,1,0:T(8,128)(2,1)S(1)}, u32[]{:S(2)}, u32[]{:S(2)}) async-start(bf16[8,16,256]{2,1,0:T(8,128)(2,1)} %carry.1), calls=%async_computation.2 | async-start | bytes 131072 | tf_op jit(solution)/shard_map/all_to_all | solution.py:342
  64.4 8.3 %all-to-all-done.2 = bf16[8,16,256]{2,1,0:T(8,128)(2,1)S(1)} async-done(((bf16[8,16,256]{2,1,0:T(8,128)(2,1)}), bf16[8,16,256]{2,1,0:T(8,128)(2,1)S(1)}, u32[]{:S(2)}, u32[]{:S(2)}) %all-to-all-start.2) | async-done | bytes 65568 | tf_op jit(solution)/shard_map/all_to_all | solution.py:342
  72.7 0.6 attend.1
  73.3 2.2 %all-gather.1 = bf16[2064,128]{1,0:T(8,128)(2,1)S(1)} all-gather(bf16[1032,128]{1,0:T(8,128)(2,1)S(1)} %get-tuple-element.38), channel_id=3, replica_groups=mesh['x'=4,'y'=8,'row'=4,'zhi'=2,'core'=2] {'core'}, dimensions={0}, use_global_device_ids=true | all-gather | bytes 792576 | tf_op jit(solution)/shard_map/all_gather | solution.py:354
  75.6 16.2 %all_to_all.22.received = bf16[8,136,128]{2,1,0:T(8,128)(2,1)S(1)} all-to-all(bf16[8,136,128]{2,1,0:T(8,128)(2,1)S(1)} %pair_sum.1), channel_id=1, replica_groups=mesh['x'=4,'y'=8,'row'=4,'zhi'=2,'core'=2] {'row','zhi'}, dimensions={0} | all-to-all | bytes 557056 | tf_op jit(solution)/shard_map/all_to_all | solution.py:358
  91.8 0.9 finish.1
  (30 shorter events, 0.2 us)
Async XLA Ops:
  0.0 22.2 %copy-start = (bf16[2048,256]{1,0:T(8,128)(2,1)S(1)}, bf16[2048,256]{1,0:T(8,128)(2,1)}, u32[]{:S(2)}) copy-start(bf16[2048,256]{1,0:T(8,128)(2,1)} %w_query.1) | copy-start | bytes 3145732
  0.0 0.8 copy-start.5
  19.8 2.3 %copy-start.2 = (bf16[2048,128]{1,0:T(8,128)(2,1)S(1)}, bf16[2048,128]{1,0:T(8,128)(2,1)}, u32[]{:S(2)}) copy-start(bf16[2048,128]{1,0:T(8,128)(2,1)} %w_value.1) | copy-start | bytes 1572868
  19.8 2.3 %copy-start.9 = (f32[2048]{0:T(1024)S(1)}, f32[2048]{0:T(1024)}, u32[]{:S(2)}) copy-start(f32[2048]{0:T(1024)} %param.17) | copy-start | bytes 24580
  22.2 1.2 %copy-start.1 = (bf16[2048,256]{1,0:T(8,128)(2,1)S(1)}, bf16[2048,256]{1,0:T(8,128)(2,1)}, u32[]{:S(2)}) copy-start(bf16[2048,256]{1,0:T(8,128)(2,1)} %w_key.1) | copy-start | bytes 3145732
  23.4 1.0 %copy-start.3 = (bf16[2048,128]{1,0:T(8,128)(2,1)S(1)}, bf16[2048,128]{1,0:T(8,128)(2,1)}, u32[]{:S(2)}) copy-start(bf16[2048,128]{1,0:T(8,128)(2,1)} %w_gate.1) | copy-start | bytes 1572868
  24.4 0.8 copy-start.7
  26.3 3.6 %copy-start.8 = (s32[4096]{0:T(1024)S(1)}, s32[4096]{0:T(1024)}, u32[]{:S(2)}) copy-start(s32[4096]{0:T(1024)} %param.16) | copy-start | bytes 49156
  26.3 7.8 %collective-permute-start = (f32[8,640]{1,0:T(8,128)S(1)}, f32[8,640]{1,0:T(8,128)S(1)}, u32[]{:S(2)}, u32[]{:S(2)}) collective-permute-start(f32[8,640]{1,0:T(8,128)S(1)} %get-tuple-element.23), channel_id=1, source_target_pairs={{0,16},{16,32},{32,48},{48,64},{64,80},{80,96},{96,112},{112,128},... | collective-permute-start | bytes 61448 | tf_op jit(solution)/shard_map/ppermute | solution.py:293
  29.8 0.7 copy-start.10
  29.8 0.7 copy-start.14
  29.9 0.7 copy-start.15
  30.5 3.6 %copy-start.12 = (f32[4,256]{1,0:T(4,128)S(1)}, f32[4,256]{1,0:T(4,128)}, u32[]{:S(2)}) copy-start(f32[4,256]{1,0:T(4,128)} %taps_k.1) | copy-start | bytes 12292
  31.2 2.9 %copy-start.11 = (f32[4,256]{1,0:T(4,128)S(1)}, f32[4,256]{1,0:T(4,128)}, u32[]{:S(2)}) copy-start(f32[4,256]{1,0:T(4,128)} %taps_q.1) | copy-start | bytes 12292
  34.1 0.7 copy-start.13
  34.8 37.9 %copy-start.4 = (bf16[128,2048]{1,0:T(8,128)(2,1)S(1)}, bf16[128,2048]{1,0:T(8,128)(2,1)}, u32[]{:S(2)}) copy-start(bf16[128,2048]{1,0:T(8,128)(2,1)} %w_out.1) | copy-start | bytes 1572868
  50.7 6.0 %collective-permute-start.2 = (f32[24,256]{1,0:T(8,128)S(1)}, f32[24,256]{1,0:T(8,128)S(1)}, u32[]{:S(2)}, u32[]{:S(2)}) collective-permute-start(f32[24,256]{1,0:T(8,128)S(1)} %get-tuple-element.34), channel_id=1, source_target_pairs={{0,256},{128,384},{1,257},{129,385},{2,258},{130,386},{3,259},{131... | collective-permute-start | bytes 73736 | tf_op jit(solution)/shard_map/ppermute | solution.py:338
  54.7 5.7 %collective-permute-start.1 = (f32[24,256]{1,0:T(8,128)S(1)}, f32[24,256]{1,0:T(8,128)S(1)}, u32[]{:S(2)}, u32[]{:S(2)}) collective-permute-start(f32[24,256]{1,0:T(8,128)S(1)} %get-tuple-element.34), channel_id=1, source_target_pairs={{0,128},{128,256},{256,384},{1,129},{129,257},{257,385},{2,130},{1... | collective-permute-start | bytes 73736 | tf_op jit(solution)/shard_map/ppermute | solution.py:337
  61.1 11.7 %all-to-all-start.2 = ((bf16[8,16,256]{2,1,0:T(8,128)(2,1)}), bf16[8,16,256]{2,1,0:T(8,128)(2,1)S(1)}, u32[]{:S(2)}, u32[]{:S(2)}) async-start(bf16[8,16,256]{2,1,0:T(8,128)(2,1)} %carry.1), calls=%async_computation.2 | async-start | bytes 131072 | tf_op jit(solution)/shard_map/all_to_all | solution.py:342
  75.6 16.2 %copy-start.6 = (bf16[128,128]{1,0:T(8,128)(2,1)S(1)}, bf16[128,128]{1,0:T(8,128)(2,1)}, u32[]{:S(2)}) copy-start(bf16[128,128]{1,0:T(8,128)(2,1)} %hidden.3) | copy-start | bytes 98308

commit v3 on v2

--- a/solution.py
+++ b/solution.py
@@ -22,17 +22,23 @@
 PIECE = BLOCK // ROWS_Y
 
 
-def local_call(kernel, outs, *args, scratch=(), scalars=0, plain=(), last=False):
+def local_call(kernel, outs, *args, scratch=(), scalars=0, plain=(), anywhere=(), last=False):
+    elsewhere = (*range(scalars), *plain, *anywhere)
     vmem = pl.BlockSpec(memory_space=pltpu.VMEM)
     smem = pl.BlockSpec(memory_space=pltpu.SMEM)
     args = [
-        a if i < scalars or i in plain else pltpu.with_memory_space_constraint(a, pltpu.VMEM)
+        pltpu.with_memory_space_constraint(a, pltpu.HBM if i in anywhere else pltpu.VMEM)
+        if i in anywhere or i not in elsewhere
+        else a
         for i, a in enumerate(args)
     ]
     return pl.pallas_call(
         kernel,
         out_shape=[jax.ShapeDtypeStruct(s, t) if last else pltpu.VMEM(s, t) for s, t in outs],
-        in_specs=[smem] * scalars + [vmem] * (len(args) - scalars),
+        in_specs=[
+            smem if i < scalars else pl.BlockSpec(memory_space=pltpu.HBM) if i in anywhere else vmem
+            for i in range(len(args))
+        ],
         out_specs=[vmem] * len(outs),
         scratch_shapes=list(scratch),
         name=kernel.__name__,
@@ -71,8 +77,31 @@
 
 
 def project(
-    whole, gain, w_query, w_key, w_value, w_gate, w_down, pre, tail, gate_pre, rank_part, normed
+    whole,
+    gain,
+    w_query,
+    w_value,
+    key_hbm,
+    gate_hbm,
+    down_hbm,
+    pre,
+    tail,
+    gate_pre,
+    rank_part,
+    normed,
+    w_key,
+    w_gate,
+    w_down,
+    arrived,
 ):
+    copies = [
+        pltpu.make_async_copy(source, target, arrived.at[i])
+        for i, (source, target) in enumerate(
+            ((key_hbm, w_key), (gate_hbm, w_gate), (down_hbm, w_down))
+        )
+    ]
+    for copy in copies:
+        copy.start()
     chunks = WIDTH // CHUNK
     squares = jnp.zeros((BLOCK, CHUNK), F32)
     for f in range(chunks):
@@ -85,16 +114,38 @@
         normed[:, span] = (activ * scale * gain[:, span]).astype(BF16)
     rows = normed[...]
     pre[:, :HEAD_K] = dot(rows, w_query[...])
+    pre[:, 2 * HEAD_K :] = dot(rows, w_value[...])
+    copies[0].wait()
     pre[:, HEAD_K : 2 * HEAD_K] = dot(rows, w_key[...])
-    pre[:, 2 * HEAD_K :] = dot(rows, w_value[...])
     tail[...] = pre[BLOCK - 8 :, :]
+    copies[1].wait()
     gate_pre[...] = dot(rows, w_gate[...])
+    copies[2].wait()
     rank_part[...] = dot(rows, w_down[...], LAST)
 
 
 def gates(
-    index, rank_part, w_up, bias, gate_pre, head_gain, seg_ids, cumulated, gate, columns, own_rows
+    index,
+    core,
+    rank_part,
+    w_up,
+    bias,
+    gate_pre,
+    head_gain,
+    seg_ids,
+    taps_q,
+    taps_k,
+    taps_v,
+    cumulated,
+    gate,
+    columns,
+    own_rows,
+    taps,
 ):
+    del core
+    taps[:, :HEAD_K] = taps_q[...]
+    taps[:, HEAD_K : 2 * HEAD_K] = taps_k[...]
+    taps[:, 2 * HEAD_K :] = taps_v[...]
     logits = dot(rank_part[...], w_up[...].astype(F32), precision=HIGHEST) + bias[...]
     log_decay = (jnp.minimum(logits, 0.0) - jnp.log(1.0 + jnp.exp(-jnp.abs(logits)))) / 16.0
     row_iota = lax.broadcasted_iota(jnp.int32, (BLOCK, BLOCK), 0)
@@ -120,24 +171,24 @@
 
 
 def span(
-    pre, edge, taps_q, taps_k, taps_v, cumulated, columns, own_rows, intra, reach, pieces, extended
+    pre, edge, taps, cumulated, columns, own_rows, intra, reach, pieces, extended
 ):
     extended[0:8, :] = edge[...]
     extended[8:, :] = pre[...]
     seg = columns[:, 0:1]
 
-    def conv(lanes, taps):
-        total = taps[0:1, :] * extended[8:, lanes]
+    def conv(lanes):
+        total = taps[0:1, lanes] * extended[8:, lanes]
         for j in range(1, 4):
             same = columns[:, 8 * j : 8 * j + 1] == seg
             total = total + jnp.where(
-                same, taps[j : j + 1, :] * extended[8 - j : 8 - j + BLOCK, lanes], 0.0
+                same, taps[j : j + 1, lanes] * extended[8 - j : 8 - j + BLOCK, lanes], 0.0
             )
         return silu(total)
 
-    queries = conv(slice(0, HEAD_K), taps_q) * HEAD_K ** (-0.5)
-    keys = conv(slice(HEAD_K, 2 * HEAD_K), taps_k)
-    values = conv(slice(2 * HEAD_K, 2 * HEAD_K + CHUNK), taps_v)
+    queries = conv(slice(0, HEAD_K)) * HEAD_K ** (-0.5)
+    keys = conv(slice(HEAD_K, 2 * HEAD_K))
+    values = conv(slice(2 * HEAD_K, 2 * HEAD_K + CHUNK))
     cum = cumulated[...]
     row_iota = lax.broadcasted_iota(jnp.int32, (BLOCK, BLOCK), 0)
     col_iota = lax.broadcasted_iota(jnp.int32, (BLOCK, BLOCK), 1)
@@ -284,29 +335,42 @@
         whole,
         norm_gain.reshape(1, WIDTH),
         w_query,
+        w_value,
         w_key,
-        w_value,
         w_gate,
         w_decay_down.T,
-        scratch=[pltpu.VMEM((BLOCK, WIDTH), BF16)],
+        scratch=[
+            pltpu.VMEM((BLOCK, WIDTH), BF16),
+            pltpu.VMEM((WIDTH, HEAD_K), BF16),
+            pltpu.VMEM((WIDTH, CHUNK), BF16),
+            pltpu.VMEM((16, WIDTH), BF16),
+            pltpu.SemaphoreType.DMA((3,)),
+        ],
+        anywhere=(4, 5, 6),
     )
     edge = lax.ppermute(tail, SEQ, [(i, i + 1) for i in range(blocks - 1)])
-    cumulated, gate, columns, own_rows = local_call(
+    cumulated, gate, columns, own_rows, taps = local_call(
         gates,
         [
             ((BLOCK, HEAD_K), F32),
             ((BLOCK, CHUNK), F32),
             ((BLOCK, BLOCK), F32),
             ((8, BLOCK), F32),
+            ((4, 2 * HEAD_K + CHUNK), F32),
         ],
         block_at,
+        core_at,
         rank_part,
         w_decay_up,
         decay_bias.reshape(1, HEAD_K),
         gate_pre,
         head_gain.reshape(1, CHUNK),
         seg_ids.reshape(blocks, BLOCK),
-        scalars=1,
+        conv_query,
+        conv_key,
+        conv_value,
+        scalars=2,
+        plain=(3, 4, 6, 7, 8, 9, 10),
     )
     intra, reach, pieces = local_call(
         span,
@@ -317,9 +381,7 @@
         ],
         pre,
         edge,
-        conv_query,
-        conv_key,
-        conv_value,
+        taps,
         cumulated,
         columns,
         own_rows,

time: 93.4 us -> 89.6 us (0.959)
  blocking collectives: 54.4 us -> 65.1 us
  waiting for transfers between devices: 15 us -> 6.64 us
  local copies, waits for them, and re-layouts: 5.33 us -> 1.56 us
  starting transfers between devices: 12.8 us -> 9.44 us
  Pallas kernels: 5.07 us -> 6.18 us
    all_to_all x0 -> x1, blocking collectives: none -> 10.8 us  [shards(): incoming = lax.all_to_all(states, 'y', 0, 0).reshape(CHUNK, HEAD_K)]
    all_to_all x1 -> x0, waiting for transfers between devices: 8.3 us -> none  [shards(): incoming = lax.all_to_all(states, 'y', 0, 0).reshape(CHUNK, HEAD_K)]
    unnamed x32 -> x26, local copies, waits for them, and re-layouts: 5.33 us -> 1.56 us
    all_to_all x1 -> x0, starting transfers between devices: 3.35 us -> none  [shards(): incoming = lax.all_to_all(states, 'y', 0, 0).reshape(CHUNK, HEAD_K)]
    pallas_call x9, Pallas kernels: 5.07 us -> 6.18 us  [local_call(): pl.pallas_call(kernel, out_shape=[jax.ShapeDtypeStruct(s, t) if last else...]
  transfers between devices with their start and end apart: 4 -> 3, of which waited for: 3 -> 2; matrix products, arithmetic and copies ran while one was open for 0% -> 0% of each run, Pallas kernels for 1% -> 1%
where the time goes in v3:
time: 89.6 us; the launch traced here: 89.1 us
  blocking collectives  65.1 us (73%)
  starting transfers between devices  9.44 us (11%)
  waiting for transfers between devices  6.64 us (7%)
  Pallas kernels  6.18 us (7%)
  local copies, waits for them, and re-layouts  1.56 us (2%)
    all_to_all x1, blocking collectives, shards(): of_core = lax.all_to_all(copies, CHIPS, 0, 0)  19 us
    all_to_all x1, blocking collectives, shards(): arrived = lax.all_to_all(pairs, CHIPS, 0, 0)  16.2 us
    all_to_all x1, blocking collectives, shards(): lax.all_to_all(pieces, 'y', 0, 0)  14.7 us
    all_to_all x1, blocking collectives, shards(): incoming = lax.all_to_all(states, 'y', 0, 0).reshape(CHUNK, HEAD_K)  10.8 us
    pallas_call x9, Pallas kernels, local_call(): pl.pallas_call(kernel, out_shape=[jax.ShapeDtypeStruct(s, t) if last else...  6.18 us
    ppermute x1, starting transfers between devices, shards(): lax.ppermute(totals, 'x', [(i, i + 2) for i in range(ROWS_X - 2)])  4.03 us
    ppermute x1, waiting for transfers between devices, shards(): lax.ppermute(totals, 'x', [(i, i + 1) for i in range(ROWS_X - 1)])  3.78 us
    ppermute x1, starting transfers between devices, shards(): edge = lax.ppermute(tail, SEQ, [(i, i + 1) for i in range(blocks - 1)])  3.48 us
  transfers between devices with their start and end apart: 3, of which 2 were waited for; matrix products, arithmetic and copies ran while one was open for 0% of the time, Pallas kernels for 1%

profile of v3, /device:TPU:2, one launch (start us, length us, event | category | flops | bytes accessed | tf_op | source)
XLA Modules:
  0.0 89.1 jit_solution(5148936600997899936)
XLA Ops:
  0.0 0.8 copy-done.3
  0.9 19.0 %all_to_all.20 = bf16[8,128,128]{2,1,0:T(8,128)(2,1)S(1)} all-to-all(bf16[8,128,128]{2,1,0:T(8,128)(2,1)S(1)} %spread_out.1), channel_id=1, replica_groups=mesh['x'=4,'y'=8,'row'=4,'zhi'=2,'core'=2] {'row','zhi'}, dimensions={0} | all-to-all | bytes 524288 | tf_op jit(solution)/shard_map/all_to_all | solution.py:324
  19.9 2.3 %all-gather = bf16[16,128,128]{2,1,0:T(8,128)(2,1)S(1)} all-gather(bf16[8,128,128]{2,1,0:T(8,128)(2,1)S(1)} %all_to_all.20), channel_id=2, replica_groups=mesh['x'=4,'y'=8,'row'=4,'zhi'=2,'core'=2] {'core'}, dimensions={0}, use_global_device_ids=true | all-gather | bytes 786432 | tf_op jit(solution)/shard_map/all_gather | solution.py:325
  22.2 0.0 copy-start.12
  22.2 2.8 %project.1 = (f32[128,640]{1,0:T(8,128)S(1)}, f32[8,640]{1,0:T(8,128)S(1)}, f32[128,128]{1,0:T(8,128)S(1)}, f32[128,16]{1,0:T(8,128)S(1)}) custom-call(bf16[2,8,128,128]{3,2,1,0:T(8,128)(2,1)S(1)} %bitcast.11, f32[1,2048]{1,0:T(1,128)S(1)} %bitcast.14, bf16[2048,256]{1,0:T(8,128)(2,1)S(1)} %copy-done, bf16[2048,128]{1,0:T(8,128)(2,1)S(1)} %copy-done.1, ...), custom_call_target="tpu_custom_call" | custom-call | tf_op jit(solution)/shard_map/project/pallas_call | solution.py:35
  25.0 3.5 %collective-permute-start = (f32[8,640]{1,0:T(8,128)S(1)}, f32[8,640]{1,0:T(8,128)S(1)}, u32[]{:S(2)}, u32[]{:S(2)}) collective-permute-start(f32[8,640]{1,0:T(8,128)S(1)} %get-tuple-element.24), channel_id=1, source_target_pairs={{0,16},{16,32},{32,48},{48,64},{64,80},{80,96},{96,112},{112,128},... | collective-permute-start | bytes 61448 | tf_op jit(solution)/shard_map/ppermute | solution.py:351
  28.4 0.0 copy-start.5
  28.5 0.0 copy-start.7
  28.5 0.6 copy-done.5
  29.2 0.0 copy-done.8
  29.2 0.0 copy-done.11
  29.2 0.7 gates.1
  29.9 2.9 %collective-permute-done.edge = f32[8,640]{1,0:T(8,128)S(1)} collective-permute-done((f32[8,640]{1,0:T(8,128)S(1)}, f32[8,640]{1,0:T(8,128)S(1)}, u32[]{:S(2)}, u32[]{:S(2)}) %collective-permute-start) | collective-permute-done | bytes 20512 | tf_op jit(solution)/shard_map/ppermute | solution.py:351
  32.7 1.1 %span.1 = (f32[128,128]{1,0:T(8,128)S(1)}, f32[128,256]{1,0:T(8,128)S(1)}, bf16[8,24,256]{2,1,0:T(8,128)(2,1)S(1)}) custom-call(f32[128,640]{1,0:T(8,128)S(1)} %get-tuple-element.23.pre, f32[8,640]{1,0:T(8,128)S(1)} %collective-permute-done.edge, f32[4,640]{1,0:T(4,128)S(1)} %get-tuple-element.27.taps, f32[128,256]{1,0:T(8,128)S(1)} %get-tuple-element.28.cumulated, ...), custom_call_target="tpu_custom_call" | custom-call | tf_op jit(solution)/shard_map/span/pallas_call | solution.py:35
  33.9 14.7 %all_to_all.21.pieces = bf16[8,24,256]{2,1,0:T(8,128)(2,1)S(1)} all-to-all(bf16[8,24,256]{2,1,0:T(8,128)(2,1)S(1)} %get-tuple-element.33), channel_id=1, replica_groups=mesh['x'=4,'y'=8,'row'=4,'zhi'=2,'core'=2] {'y'}, dimensions={0} | all-to-all | bytes 196608 | tf_op jit(solution)/shard_map/all_to_all | solution.py:397
  48.6 4.0 %collective-permute-start.2 = (f32[24,256]{1,0:T(8,128)S(1)}, f32[24,256]{1,0:T(8,128)S(1)}, u32[]{:S(2)}, u32[]{:S(2)}) collective-permute-start(f32[24,256]{1,0:T(8,128)S(1)} %get-tuple-element.36), channel_id=1, source_target_pairs={{0,256},{128,384},{1,257},{129,385},{2,258},{130,386},{3,259},{131... | collective-permute-start | bytes 73736 | tf_op jit(solution)/shard_map/ppermute | solution.py:400
  52.7 1.9 %collective-permute-start.1 = (f32[24,256]{1,0:T(8,128)S(1)}, f32[24,256]{1,0:T(8,128)S(1)}, u32[]{:S(2)}, u32[]{:S(2)}) collective-permute-start(f32[24,256]{1,0:T(8,128)S(1)} %get-tuple-element.36), channel_id=1, source_target_pairs={{0,128},{128,256},{256,384},{1,129},{129,257},{257,385},{2,130},{1... | collective-permute-start | bytes 73736 | tf_op jit(solution)/shard_map/ppermute | solution.py:399
  54.6 3.8 %collective-permute-done.1.one_back = f32[24,256]{1,0:T(8,128)S(1)} collective-permute-done((f32[24,256]{1,0:T(8,128)S(1)}, f32[24,256]{1,0:T(8,128)S(1)}, u32[]{:S(2)}, u32[]{:S(2)}) %collective-permute-start.1) | collective-permute-done | bytes 24608 | tf_op jit(solution)/shard_map/ppermute | solution.py:399
  58.4 10.8 %all_to_all.22 = bf16[8,16,256]{2,1,0:T(8,128)(2,1)S(1)} all-to-all(bf16[8,16,256]{2,1,0:T(8,128)(2,1)S(1)} %carry.1), channel_id=1, replica_groups=mesh['x'=4,'y'=8,'row'=4,'zhi'=2,'core'=2] {'y'}, dimensions={0} | all-to-all | bytes 131072 | tf_op jit(solution)/shard_map/all_to_all | solution.py:404
  69.2 0.6 attend.1
  69.8 2.2 %all-gather.1 = bf16[2064,128]{1,0:T(8,128)(2,1)S(1)} all-gather(bf16[1032,128]{1,0:T(8,128)(2,1)S(1)} %get-tuple-element.40), channel_id=3, replica_groups=mesh['x'=4,'y'=8,'row'=4,'zhi'=2,'core'=2] {'core'}, dimensions={0}, use_global_device_ids=true | all-gather | bytes 792576 | tf_op jit(solution)/shard_map/all_gather | solution.py:416
  71.9 0.1 pair_sum.1
  72.0 16.2 %all_to_all.23.received = bf16[8,136,128]{2,1,0:T(8,128)(2,1)S(1)} all-to-all(bf16[8,136,128]{2,1,0:T(8,128)(2,1)S(1)} %pair_sum.1), channel_id=1, replica_groups=mesh['x'=4,'y'=8,'row'=4,'zhi'=2,'core'=2] {'row','zhi'}, dimensions={0} | all-to-all | bytes 557056 | tf_op jit(solution)/shard_map/all_to_all | solution.py:420
  88.3 0.9 finish.1
  (23 shorter events, 0.1 us)
Async XLA Ops:
  0.0 22.2 %copy-start = (bf16[2048,256]{1,0:T(8,128)(2,1)S(1)}, bf16[2048,256]{1,0:T(8,128)(2,1)}, u32[]{:S(2)}) copy-start(bf16[2048,256]{1,0:T(8,128)(2,1)} %w_query.1) | copy-start | bytes 3145732
  0.0 0.8 copy-start.3
  19.8 2.3 %copy-start.1 = (bf16[2048,128]{1,0:T(8,128)(2,1)S(1)}, bf16[2048,128]{1,0:T(8,128)(2,1)}, u32[]{:S(2)}) copy-start(bf16[2048,128]{1,0:T(8,128)(2,1)} %w_value.1) | copy-start | bytes 1572868
  19.8 2.3 %copy-start.6 = (f32[2048]{0:T(1024)S(1)}, f32[2048]{0:T(1024)}, u32[]{:S(2)}) copy-start(f32[2048]{0:T(1024)} %param.17) | copy-start | bytes 24580
  22.2 6.4 %copy-start.9 = (f32[4,256]{1,0:T(4,128)S(1)}, f32[4,256]{1,0:T(4,128)}, u32[]{:S(2)}) copy-start(f32[4,256]{1,0:T(4,128)} %taps_k.1) | copy-start | bytes 12292
  22.2 6.3 %copy-start.12 = (f32[128]{0:T(128)S(1)}, f32[128]{0:T(128)}, u32[]{:S(2)}) copy-start(f32[128]{0:T(128)} %param.28) | copy-start | bytes 1540
  25.0 7.8 %collective-permute-start = (f32[8,640]{1,0:T(8,128)S(1)}, f32[8,640]{1,0:T(8,128)S(1)}, u32[]{:S(2)}, u32[]{:S(2)}) collective-permute-start(f32[8,640]{1,0:T(8,128)S(1)} %get-tuple-element.24), channel_id=1, source_target_pairs={{0,16},{16,32},{32,48},{48,64},{64,80},{80,96},{96,112},{112,128},... | collective-permute-start | bytes 61448 | tf_op jit(solution)/shard_map/ppermute | solution.py:351
  28.4 0.7 copy-start.5
  28.5 0.7 copy-start.7
  28.5 0.7 copy-start.8
  28.5 0.7 copy-start.10
  28.5 0.7 copy-start.11
  32.7 36.4 %copy-start.2 = (bf16[128,2048]{1,0:T(8,128)(2,1)S(1)}, bf16[128,2048]{1,0:T(8,128)(2,1)}, u32[]{:S(2)}) copy-start(bf16[128,2048]{1,0:T(8,128)(2,1)} %w_out.1) | copy-start | bytes 1572868
  48.6 6.0 %collective-permute-start.2 = (f32[24,256]{1,0:T(8,128)S(1)}, f32[24,256]{1,0:T(8,128)S(1)}, u32[]{:S(2)}, u32[]{:S(2)}) collective-permute-start(f32[24,256]{1,0:T(8,128)S(1)} %get-tuple-element.36), channel_id=1, source_target_pairs={{0,256},{128,384},{1,257},{129,385},{2,258},{130,386},{3,259},{131... | collective-permute-start | bytes 73736 | tf_op jit(solution)/shard_map/ppermute | solution.py:400
  52.7 5.7 %collective-permute-start.1 = (f32[24,256]{1,0:T(8,128)S(1)}, f32[24,256]{1,0:T(8,128)S(1)}, u32[]{:S(2)}, u32[]{:S(2)}) collective-permute-start(f32[24,256]{1,0:T(8,128)S(1)} %get-tuple-element.36), channel_id=1, source_target_pairs={{0,128},{128,256},{256,384},{1,129},{129,257},{257,385},{2,130},{1... | collective-permute-start | bytes 73736 | tf_op jit(solution)/shard_map/ppermute | solution.py:399
  72.0 16.2 %copy-start.4 = (bf16[128,128]{1,0:T(8,128)(2,1)S(1)}, bf16[128,128]{1,0:T(8,128)(2,1)}, u32[]{:S(2)}) copy-start(bf16[128,128]{1,0:T(8,128)(2,1)} %hidden.3) | copy-start | bytes 98308

commit v4 on v2

--- a/solution.py
+++ b/solution.py
@@ -22,17 +22,23 @@
 PIECE = BLOCK // ROWS_Y
 
 
-def local_call(kernel, outs, *args, scratch=(), scalars=0, plain=(), last=False):
+def local_call(kernel, outs, *args, scratch=(), scalars=0, plain=(), anywhere=(), last=False):
+    elsewhere = (*range(scalars), *plain, *anywhere)
     vmem = pl.BlockSpec(memory_space=pltpu.VMEM)
     smem = pl.BlockSpec(memory_space=pltpu.SMEM)
     args = [
-        a if i < scalars or i in plain else pltpu.with_memory_space_constraint(a, pltpu.VMEM)
+        pltpu.with_memory_space_constraint(a, pltpu.HBM if i in anywhere else pltpu.VMEM)
+        if i in anywhere or i not in elsewhere
+        else a
         for i, a in enumerate(args)
     ]
     return pl.pallas_call(
         kernel,
         out_shape=[jax.ShapeDtypeStruct(s, t) if last else pltpu.VMEM(s, t) for s, t in outs],
-        in_specs=[smem] * scalars + [vmem] * (len(args) - scalars),
+        in_specs=[
+            smem if i < scalars else pl.BlockSpec(memory_space=pltpu.HBM) if i in anywhere else vmem
+            for i in range(len(args))
+        ],
         out_specs=[vmem] * len(outs),
         scratch_shapes=list(scratch),
         name=kernel.__name__,
@@ -65,43 +71,82 @@
     return value * jax.nn.sigmoid(value)
 
 
-def spread_out(hidden, copies):
+def take(index, core, hidden, kept, tail):
+    del index, core
+    kept[...] = hidden[...]
+    tail[...] = hidden[BLOCK - 8 :, :]
+
+
+def fetch(tail, key_hbm, gate_hbm, w_key, w_gate, arrived):
+    del tail
+    copies = [
+        pltpu.make_async_copy(key_hbm, w_key, arrived.at[0]),
+        pltpu.make_async_copy(gate_hbm, w_gate, arrived.at[1]),
+    ]
+    for copy in copies:
+        copy.start()
+    for copy in copies:
+        copy.wait()
+
+
+def spread_out(hidden, edge, w_key, copies):
+    del w_key
     for j in range(8):
-        copies[j] = hidden[...]
-
-
-def project(
-    whole, gain, w_query, w_key, w_value, w_gate, w_down, pre, tail, gate_pre, rank_part, normed
+        copies[j, 0:BLOCK, :] = hidden[...]
+        copies[j, BLOCK:, :] = edge[...]
+
+
+def local_work(
+    index,
+    core,
+    whole,
+    gain,
+    w_query,
+    w_key,
+    w_value,
+    w_gate,
+    w_down,
+    w_up,
+    bias,
+    head_gain,
+    seg_ids,
+    taps_q,
+    taps_k,
+    taps_v,
+    intra,
+    reach,
+    pieces,
+    gate,
+    normed,
+    extended,
 ):
+    del core
     chunks = WIDTH // CHUNK
-    squares = jnp.zeros((BLOCK, CHUNK), F32)
+    squares = jnp.zeros((BLOCK + 8, CHUNK), F32)
     for f in range(chunks):
         activ = whole[f % 2, f // 2].astype(F32)
         squares = squares + activ * activ
     scale = lax.rsqrt(jnp.sum(squares, axis=1, keepdims=True) / WIDTH + 1e-06)
     for f in range(chunks):
-        span = slice(f * CHUNK, (f + 1) * CHUNK)
+        lanes = slice(f * CHUNK, (f + 1) * CHUNK)
         activ = whole[f % 2, f // 2].astype(F32)
-        normed[:, span] = (activ * scale * gain[:, span]).astype(BF16)
+        normed[:, lanes] = (activ * scale * gain[:, lanes]).astype(BF16)
     rows = normed[...]
-    pre[:, :HEAD_K] = dot(rows, w_query[...])
-    pre[:, HEAD_K : 2 * HEAD_K] = dot(rows, w_key[...])
-    pre[:, 2 * HEAD_K :] = dot(rows, w_value[...])
-    tail[...] = pre[BLOCK - 8 :, :]
-    gate_pre[...] = dot(rows, w_gate[...])
-    rank_part[...] = dot(rows, w_down[...], LAST)
-
-
-def gates(
-    index, rank_part, w_up, bias, gate_pre, head_gain, seg_ids, cumulated, gate, columns, own_rows
-):
-    logits = dot(rank_part[...], w_up[...].astype(F32), precision=HIGHEST) + bias[...]
-    log_decay = (jnp.minimum(logits, 0.0) - jnp.log(1.0 + jnp.exp(-jnp.abs(logits)))) / 16.0
-    row_iota = lax.broadcasted_iota(jnp.int32, (BLOCK, BLOCK), 0)
-    col_iota = lax.broadcasted_iota(jnp.int32, (BLOCK, BLOCK), 1)
-    lower = jnp.where(row_iota >= col_iota, 1.0, 0.0).astype(F32)
-    cumulated[...] = dot(lower, log_decay, precision=HIGHEST)
-    gate[...] = silu(gate_pre[...]) * head_gain[...]
+    rank_part = dot(rows, w_down[...], LAST)[0:BLOCK, :]
+    gate_pre = dot(rows, w_gate[...])[0:BLOCK, :]
+
+    def conv(weight, taps, lanes):
+        pre = dot(rows, weight[...])
+        extended[0:8, lanes] = pre[BLOCK:, :]
+        extended[8:, lanes] = pre[0:BLOCK, :]
+        total = taps[0:1, :] * pre[0:BLOCK, :]
+        for j in range(1, 4):
+            same = columns[:, 8 * j : 8 * j + 1] == seg
+            total = total + jnp.where(
+                same, taps[j : j + 1, :] * extended[8 - j : 8 - j + BLOCK, lanes], 0.0
+            )
+        return silu(total)
+
     at = index[0]
     own = seg_ids[pl.ds(at, 1), :].astype(F32)
     before = seg_ids[pl.ds(jnp.maximum(at - 1, 0), 1), :].astype(F32)
@@ -112,35 +157,34 @@
     parts = [own]
     for j in range(1, 4):
         parts.append(jnp.where(lane < j, pltpu.roll(before, j, 1), pltpu.roll(own, j, 1)))
-    parts.append(jnp.broadcast_to(before[:, BLOCK - 1 :], (8, BLOCK)))
-    parts.append(jnp.broadcast_to(own[:, BLOCK - 1 :], (8, BLOCK)))
+    before = jnp.broadcast_to(before[:, BLOCK - 1 :], (8, BLOCK))
+    last = jnp.broadcast_to(own[:, BLOCK - 1 :], (8, BLOCK))
+    parts += [before, last]
     parts.append(jnp.zeros((BLOCK - 8 * len(parts), BLOCK), F32))
-    columns[...] = jnp.transpose(jnp.concatenate(parts, axis=0))
-    own_rows[...] = own
-
-
-def span(
-    pre, edge, taps_q, taps_k, taps_v, cumulated, columns, own_rows, intra, reach, pieces, extended
-):
-    extended[0:8, :] = edge[...]
-    extended[8:, :] = pre[...]
+    columns = jnp.transpose(jnp.concatenate(parts, axis=0))
     seg = columns[:, 0:1]
 
-    def conv(lanes, taps):
-        total = taps[0:1, :] * extended[8:, lanes]
-        for j in range(1, 4):
-            same = columns[:, 8 * j : 8 * j + 1] == seg
-            total = total + jnp.where(
-                same, taps[j : j + 1, :] * extended[8 - j : 8 - j + BLOCK, lanes], 0.0
-            )
-        return silu(total)
-
-    queries = conv(slice(0, HEAD_K), taps_q) * HEAD_K ** (-0.5)
-    keys = conv(slice(HEAD_K, 2 * HEAD_K), taps_k)
-    values = conv(slice(2 * HEAD_K, 2 * HEAD_K + CHUNK), taps_v)
-    cum = cumulated[...]
+    logits = dot(rank_part, w_up[...].astype(F32), precision=HIGHEST) + bias[...]
+    log_decay = (jnp.minimum(logits, 0.0) - jnp.log(1.0 + jnp.exp(-jnp.abs(logits)))) / 16.0
     row_iota = lax.broadcasted_iota(jnp.int32, (BLOCK, BLOCK), 0)
     col_iota = lax.broadcasted_iota(jnp.int32, (BLOCK, BLOCK), 1)
+    lower = jnp.where(row_iota >= col_iota, 1.0, 0.0).astype(F32)
+    cum = dot(lower, log_decay, precision=HIGHEST)
+
+    keys = conv(w_key, taps_k, slice(HEAD_K, 2 * HEAD_K))
+    values = conv(w_value, taps_v, slice(2 * HEAD_K, 2 * HEAD_K + CHUNK)).astype(BF16)
+    final = cum[BLOCK - 1 :, :]
+    pushed = jnp.where(seg == columns[:, 40:41], keys * jnp.exp(final - cum), 0.0)
+    state = dot(values, pushed.astype(BF16), FIRST)
+    keep = jnp.where(before[0:1, 0:1] == last[0:1, 0:1], jnp.exp(final), 0.0)
+    keep_rows = pair_rows(keep)
+    for j in range(ROWS_Y):
+        pieces[j, 0:PIECE, :] = state[j * PIECE : (j + 1) * PIECE, :].astype(BF16)
+        pieces[j, PIECE:, :] = keep_rows
+
+    gate[...] = silu(gate_pre) * head_gain[...]
+    queries = conv(w_query, taps_q, slice(0, HEAD_K)) * HEAD_K ** (-0.5)
+    reach[...] = jnp.where(seg == columns[:, 32:33], queries * jnp.exp(cum), 0.0)
     weights = jnp.zeros((BLOCK, BLOCK), F32)
     for half in (8, 16, 32, 64):
         anchors = [
@@ -168,20 +212,9 @@
         sums = jnp.sum(product.reshape(BLOCK, HEAD_K), axis=1, keepdims=True)
         inside = (row_iota - col_iota == by) & (row_iota % 8 >= by)
         weights = jnp.where(inside, sums, weights)
-    visible = (seg == own_rows[0:1, :]) & (row_iota >= col_iota)
+    visible = (seg == own[0:1, :]) & (row_iota >= col_iota)
     weights = jnp.where(visible, weights, 0.0)
-    values_b = values.astype(BF16)
-    intra[...] = dot(weights.astype(BF16), values_b)
-    before, last = columns[:, 32:33], columns[:, 40:41]
-    reach[...] = jnp.where(seg == before, queries * jnp.exp(cum), 0.0)
-    final = cum[BLOCK - 1 :, :]
-    pushed = jnp.where(seg == last, keys * jnp.exp(final - cum), 0.0)
-    state = dot(values_b, pushed.astype(BF16), FIRST)
-    keep = jnp.where(before[0:1, :] == last[0:1, :], jnp.exp(final), 0.0)
-    keep_rows = pair_rows(keep)
-    for j in range(ROWS_Y):
-        pieces[j, 0:PIECE, :] = state[j * PIECE : (j + 1) * PIECE, :].astype(BF16)
-        pieces[j, PIECE:, :] = keep_rows
+    intra[...] = dot(weights.astype(BF16), values)
 
 
 def row_scan(pieces, entering, kept, totals):
@@ -269,61 +302,64 @@
     core_at = jnp.reshape(lax.axis_index("core"), (1,)).astype(jnp.int32)
     blocks = ROWS_X * ROWS_Y
 
-    (copies,) = local_call(spread_out, [((8, BLOCK, CHUNK), BF16)], hidden_in, plain=(0,))
+    onward = [(i, i + 1) for i in range(blocks - 1)]
+    hidden, tail = local_call(
+        take,
+        [((BLOCK, CHUNK), BF16), ((8, CHUNK), BF16)],
+        block_at,
+        core_at,
+        hidden_in,
+        scalars=2,
+        plain=(2,),
+    )
+    edge = lax.ppermute(tail, SEQ, onward)
+    key_here, gate_here = local_call(
+        fetch,
+        [((WIDTH, HEAD_K), BF16), ((WIDTH, CHUNK), BF16)],
+        tail,
+        w_key,
+        w_gate,
+        scratch=[pltpu.SemaphoreType.DMA((2,))],
+        anywhere=(1, 2),
+    )
+    (copies,) = local_call(
+        spread_out,
+        [((8, BLOCK + 8, CHUNK), BF16)],
+        hidden,
+        edge,
+        key_here,
+    )
     of_core = lax.all_to_all(copies, CHIPS, 0, 0)
     whole = lax.all_gather(of_core, "core", axis=0)
-
-    pre, tail, gate_pre, rank_part = local_call(
-        project,
-        [
-            ((BLOCK, 2 * HEAD_K + CHUNK), F32),
-            ((8, 2 * HEAD_K + CHUNK), F32),
-            ((BLOCK, CHUNK), F32),
-            ((BLOCK, 16), F32),
-        ],
-        whole,
-        norm_gain.reshape(1, WIDTH),
-        w_query,
-        w_key,
-        w_value,
-        w_gate,
-        w_decay_down.T,
-        scratch=[pltpu.VMEM((BLOCK, WIDTH), BF16)],
-    )
-    edge = lax.ppermute(tail, SEQ, [(i, i + 1) for i in range(blocks - 1)])
-    cumulated, gate, columns, own_rows = local_call(
-        gates,
-        [
-            ((BLOCK, HEAD_K), F32),
-            ((BLOCK, CHUNK), F32),
-            ((BLOCK, BLOCK), F32),
-            ((8, BLOCK), F32),
-        ],
-        block_at,
-        rank_part,
-        w_decay_up,
-        decay_bias.reshape(1, HEAD_K),
-        gate_pre,
-        head_gain.reshape(1, CHUNK),
-        seg_ids.reshape(blocks, BLOCK),
-        scalars=1,
-    )
-    intra, reach, pieces = local_call(
-        span,
+    intra, reach, pieces, gate = local_call(
+        local_work,
         [
             ((BLOCK, CHUNK), F32),
             ((BLOCK, HEAD_K), F32),
             ((ROWS_Y, PIECE + 8, HEAD_K), BF16),
+            ((BLOCK, CHUNK), F32),
         ],
-        pre,
-        edge,
+        block_at,
+        core_at,
+        whole,
+        norm_gain.reshape(1, WIDTH),
+        w_query,
+        key_here,
+        w_value,
+        gate_here,
+        w_decay_down.T,
+        w_decay_up,
+        decay_bias.reshape(1, HEAD_K),
+        head_gain.reshape(1, CHUNK),
+        seg_ids.reshape(blocks, BLOCK),
         conv_query,
         conv_key,
         conv_value,
-        cumulated,
-        columns,
-        own_rows,
-        scratch=[pltpu.VMEM((BLOCK + 8, 2 * HEAD_K + CHUNK), F32)],
+        scratch=[
+            pltpu.VMEM((BLOCK + 8, WIDTH), BF16),
+            pltpu.VMEM((BLOCK + 8, 2 * HEAD_K + CHUNK), F32),
+        ],
+        scalars=2,
     )
     entering, kept, totals = local_call(
         row_scan,
@@ -357,7 +393,7 @@
     )
     arrived = lax.all_to_all(pairs, CHIPS, 0, 0)
     (mixed,) = local_call(
-        finish, [((BLOCK, CHUNK), BF16)], arrived, hidden_in, plain=(1,), last=True
+        finish, [((BLOCK, CHUNK), BF16)], arrived, hidden, last=True
     )
     return mixed
 

time: 93.4 us -> 88.8 us (0.951)
  the two profiles are of different devices: /device:TPU:2 before, /device:TPU:1 now
where the time goes in v4:
time: 88.8 us; the launch traced here: 87 us
  blocking collectives  68.1 us (77%)
  starting transfers between devices  10.9 us (12%)
  Pallas kernels  5.52 us (6%)
  local copies, waits for them, and re-layouts  1.43 us (2%)
  waiting for transfers between devices  0.92 us (1%)
    all_to_all x1, blocking collectives, shards(): of_core = lax.all_to_all(copies, CHIPS, 0, 0)  19.7 us
    all_to_all x1, blocking collectives, shards(): lax.all_to_all(pieces, 'y', 0, 0)  15.1 us
    all_to_all x1, blocking collectives, shards(): arrived = lax.all_to_all(pairs, CHIPS, 0, 0)  12.9 us
    all_to_all x1, blocking collectives, shards(): incoming = lax.all_to_all(states, 'y', 0, 0).reshape(CHUNK, HEAD_K)  9.6 us
    all_gather x1, blocking collectives, shards(): both = lax.all_gather(sent, 'core', axis=0)  6.09 us
    pallas_call x9, Pallas kernels, local_call(): pl.pallas_call(kernel, out_shape=[jax.ShapeDtypeStruct(s, t) if last else...  5.52 us
    all_gather x1, blocking collectives, shards(): whole = lax.all_gather(of_core, 'core', axis=0)  4.66 us
    ppermute x1, starting transfers between devices, shards(): lax.ppermute(totals, 'x', [(i, i + 2) for i in range(ROWS_X - 2)])  4.65 us
  transfers between devices with their start and end apart: 3, of which 1 were waited for; matrix products, arithmetic and copies ran while one was open for 0% of the time, Pallas kernels for 2%

profile of v4, /device:TPU:1, one launch (start us, length us, event | category | flops | bytes accessed | tf_op | source)
XLA Modules:
  0.0 87.0 jit_solution(8513265644982487929)
XLA Ops:
  0.0 0.8 copy-done.4
  0.8 4.0 %collective-permute-start = (bf16[8,128]{1,0:T(8,128)(2,1)S(1)}, bf16[8,128]{1,0:T(8,128)(2,1)S(1)}, u32[]{:S(2)}, u32[]{:S(2)}) collective-permute-start(bf16[8,128]{1,0:T(8,128)(2,1)S(1)} %get-tuple-element.20.tail), channel_id=1, source_target_pairs={{0,16},{16,32},{32,48},{48,64},{64,80},{80,96},{96,112},{112,128},... | collective-permute-start | bytes 6152 | tf_op jit(solution)/shard_map/ppermute | solution.py:315
  4.8 1.4 %fetch.1 = (bf16[2048,256]{1,0:T(8,128)(2,1)S(1)}, bf16[2048,128]{1,0:T(8,128)(2,1)S(1)}) custom-call(bf16[8,128]{1,0:T(8,128)(2,1)S(1)} %get-tuple-element.20.tail, bf16[2048,256]{1,0:T(8,128)(2,1)} %key_hbm.1, bf16[2048,128]{1,0:T(8,128)(2,1)} %gate_hbm.1), custom_call_target="tpu_custom_call" | custom-call | tf_op jit(solution)/shard_map/fetch/pallas_call | solution.py:35
  6.2 0.0 collective-permute-done.edge
  6.2 0.0 copy-start
  6.2 19.7 %all_to_all.20 = bf16[8,136,128]{2,1,0:T(8,128)(2,1)S(1)} all-to-all(bf16[8,136,128]{2,1,0:T(8,128)(2,1)S(1)} %spread_out.1), channel_id=1, replica_groups=mesh['x'=4,'y'=8,'row'=4,'zhi'=2,'core'=2] {'row','zhi'}, dimensions={0} | all-to-all | bytes 557056 | tf_op jit(solution)/shard_map/all_to_all | solution.py:332
  26.0 0.0 copy-start.9
  26.0 0.0 copy-start.10
  26.0 0.0 copy-start.12
  26.0 4.7 %all-gather = bf16[16,136,128]{2,1,0:T(8,128)(2,1)S(1)} all-gather(bf16[8,136,128]{2,1,0:T(8,128)(2,1)S(1)} %all_to_all.20), channel_id=2, replica_groups=mesh['x'=4,'y'=8,'row'=4,'zhi'=2,'core'=2] {'core'}, dimensions={0}, use_global_device_ids=true | all-gather | bytes 835584 | tf_op jit(solution)/shard_map/all_gather | solution.py:333
  30.8 0.6 copy-done.6
  31.4 0.0 copy-done.8
  31.4 0.0 copy-done.11
  31.4 2.5 %local_work.1 = (f32[128,128]{1,0:T(8,128)S(1)}, f32[128,256]{1,0:T(8,128)S(1)}, bf16[8,24,256]{2,1,0:T(8,128)(2,1)S(1)}, f32[128,128]{1,0:T(8,128)S(1)}) custom-call(s32[1]{0:T(128)} %bitcast.1.index, s32[1]{0:T(128)} %bitcast.core.index, bf16[2,8,136,128]{3,2,1,0:T(8,128)(2,1)S(1)} %bitcast.10, f32[1,2048]{1,0:T(1,128)S(1)} %bitcast.15, ...), custom_call_target="tpu_custom_call" | custom-call | tf_op jit(solution)/shard_map/local_work/pallas_call | solution.py:35
  33.9 15.1 %all_to_all.21.pieces = bf16[8,24,256]{2,1,0:T(8,128)(2,1)S(1)} all-to-all(bf16[8,24,256]{2,1,0:T(8,128)(2,1)S(1)} %get-tuple-element.25), channel_id=1, replica_groups=mesh['x'=4,'y'=8,'row'=4,'zhi'=2,'core'=2] {'y'}, dimensions={0} | all-to-all | bytes 196608 | tf_op jit(solution)/shard_map/all_to_all | solution.py:371
  49.0 4.6 %collective-permute-start.2 = (f32[24,256]{1,0:T(8,128)S(1)}, f32[24,256]{1,0:T(8,128)S(1)}, u32[]{:S(2)}, u32[]{:S(2)}) collective-permute-start(f32[24,256]{1,0:T(8,128)S(1)} %get-tuple-element.28), channel_id=1, source_target_pairs={{0,256},{128,384},{1,257},{129,385},{2,258},{130,386},{3,259},{131... | collective-permute-start | bytes 73736 | tf_op jit(solution)/shard_map/ppermute | solution.py:374
  53.7 2.2 %collective-permute-start.1 = (f32[24,256]{1,0:T(8,128)S(1)}, f32[24,256]{1,0:T(8,128)S(1)}, u32[]{:S(2)}, u32[]{:S(2)}) collective-permute-start(f32[24,256]{1,0:T(8,128)S(1)} %get-tuple-element.28), channel_id=1, source_target_pairs={{0,128},{128,256},{256,384},{1,129},{129,257},{257,385},{2,130},{1... | collective-permute-start | bytes 73736 | tf_op jit(solution)/shard_map/ppermute | solution.py:373
  55.9 0.9 %collective-permute-done.1.one_back = f32[24,256]{1,0:T(8,128)S(1)} collective-permute-done((f32[24,256]{1,0:T(8,128)S(1)}, f32[24,256]{1,0:T(8,128)S(1)}, u32[]{:S(2)}, u32[]{:S(2)}) %collective-permute-start.1) | collective-permute-done | bytes 24608 | tf_op jit(solution)/shard_map/ppermute | solution.py:373
  56.9 9.6 %all_to_all.22 = bf16[8,16,256]{2,1,0:T(8,128)(2,1)S(1)} all-to-all(bf16[8,16,256]{2,1,0:T(8,128)(2,1)S(1)} %carry.1), channel_id=1, replica_groups=mesh['x'=4,'y'=8,'row'=4,'zhi'=2,'core'=2] {'y'}, dimensions={0} | all-to-all | bytes 131072 | tf_op jit(solution)/shard_map/all_to_all | solution.py:378
  66.5 0.6 attend.1
  67.1 6.1 %all-gather.1 = bf16[2064,128]{1,0:T(8,128)(2,1)S(1)} all-gather(bf16[1032,128]{1,0:T(8,128)(2,1)S(1)} %get-tuple-element.32), channel_id=3, replica_groups=mesh['x'=4,'y'=8,'row'=4,'zhi'=2,'core'=2] {'core'}, dimensions={0}, use_global_device_ids=true | all-gather | bytes 792576 | tf_op jit(solution)/shard_map/all_gather | solution.py:390
  73.2 0.1 pair_sum.1
  73.2 12.9 %all_to_all.23.received = bf16[8,136,128]{2,1,0:T(8,128)(2,1)S(1)} all-to-all(bf16[8,136,128]{2,1,0:T(8,128)(2,1)S(1)} %pair_sum.1), channel_id=1, replica_groups=mesh['x'=4,'y'=8,'row'=4,'zhi'=2,'core'=2] {'row','zhi'}, dimensions={0} | all-to-all | bytes 557056 | tf_op jit(solution)/shard_map/all_to_all | solution.py:394
  86.2 0.9 %finish.1 = bf16[128,128]{1,0:T(8,128)(2,1)} custom-call(bf16[8,136,128]{2,1,0:T(8,128)(2,1)S(1)} %all_to_all.23.received, bf16[128,128]{1,0:T(8,128)(2,1)S(1)} %get-tuple-element.19.hidden), custom_call_target="tpu_custom_call" | custom-call | tf_op jit(solution)/shard_map/finish/pallas_call | solution.py:35
  (23 shorter events, 0.1 us)
Async XLA Ops:
  0.0 0.8 copy-start.4
  0.8 5.4 %collective-permute-start = (bf16[8,128]{1,0:T(8,128)(2,1)S(1)}, bf16[8,128]{1,0:T(8,128)(2,1)S(1)}, u32[]{:S(2)}, u32[]{:S(2)}) collective-permute-start(bf16[8,128]{1,0:T(8,128)(2,1)S(1)} %get-tuple-element.20.tail), channel_id=1, source_target_pairs={{0,16},{16,32},{32,48},{48,64},{64,80},{80,96},{96,112},{112,128},... | collective-permute-start | bytes 6152 | tf_op jit(solution)/shard_map/ppermute | solution.py:315
  6.2 24.5 %copy-start = (bf16[2048,256]{1,0:T(8,128)(2,1)S(1)}, bf16[2048,256]{1,0:T(8,128)(2,1)}, u32[]{:S(2)}) copy-start(bf16[2048,256]{1,0:T(8,128)(2,1)} %w_query.1) | copy-start | bytes 3145732
  26.0 4.7 %copy-start.1 = (bf16[2048,128]{1,0:T(8,128)(2,1)S(1)}, bf16[2048,128]{1,0:T(8,128)(2,1)}, u32[]{:S(2)}) copy-start(bf16[2048,128]{1,0:T(8,128)(2,1)} %w_value.1) | copy-start | bytes 1572868
  26.0 4.7 %copy-start.3 = (bf16[2048,16]{0,1:T(8,128)(2,1)S(1)}, bf16[2048,16]{0,1:T(8,128)(2,1)}, u32[]{:S(2)}) copy-start(bf16[2048,16]{0,1:T(8,128)(2,1)} %param.22) | copy-start | bytes 196612
  26.0 4.7 %copy-start.5 = (s32[4096]{0:T(1024)S(1)}, s32[4096]{0:T(1024)}, u32[]{:S(2)}) copy-start(s32[4096]{0:T(1024)} %param.16) | copy-start | bytes 49156
  26.0 4.7 %copy-start.7 = (bf16[16,256]{1,0:T(8,128)(2,1)S(1)}, bf16[16,256]{1,0:T(8,128)(2,1)}, u32[]{:S(2)}) copy-start(bf16[16,256]{1,0:T(8,128)(2,1)} %w_up.1) | copy-start | bytes 24580
  26.0 4.8 %copy-start.9 = (f32[4,256]{1,0:T(4,128)S(1)}, f32[4,256]{1,0:T(4,128)}, u32[]{:S(2)}) copy-start(f32[4,256]{1,0:T(4,128)} %taps_k.1) | copy-start | bytes 12292
  26.0 4.8 %copy-start.10 = (f32[4,128]{1,0:T(4,128)S(1)}, f32[4,128]{1,0:T(4,128)}, u32[]{:S(2)}) copy-start(f32[4,128]{1,0:T(4,128)} %taps_v.1) | copy-start | bytes 6148
  26.0 4.7 %copy-start.12 = (f32[128]{0:T(128)S(1)}, f32[128]{0:T(128)}, u32[]{:S(2)}) copy-start(f32[128]{0:T(128)} %param.28) | copy-start | bytes 1540
  30.7 0.7 copy-start.6
  30.7 0.7 copy-start.8
  30.7 0.7 copy-start.11
  33.9 32.6 %copy-start.2 = (bf16[128,2048]{1,0:T(8,128)(2,1)S(1)}, bf16[128,2048]{1,0:T(8,128)(2,1)}, u32[]{:S(2)}) copy-start(bf16[128,2048]{1,0:T(8,128)(2,1)} %w_out.1) | copy-start | bytes 1572868
  49.0 6.9 %collective-permute-start.2 = (f32[24,256]{1,0:T(8,128)S(1)}, f32[24,256]{1,0:T(8,128)S(1)}, u32[]{:S(2)}, u32[]{:S(2)}) collective-permute-start(f32[24,256]{1,0:T(8,128)S(1)} %get-tuple-element.28), channel_id=1, source_target_pairs={{0,256},{128,384},{1,257},{129,385},{2,258},{130,386},{3,259},{131... | collective-permute-start | bytes 73736 | tf_op jit(solution)/shard_map/ppermute | solution.py:374
  53.7 3.2 %collective-permute-start.1 = (f32[24,256]{1,0:T(8,128)S(1)}, f32[24,256]{1,0:T(8,128)S(1)}, u32[]{:S(2)}, u32[]{:S(2)}) collective-permute-start(f32[24,256]{1,0:T(8,128)S(1)} %get-tuple-element.28), channel_id=1, source_target_pairs={{0,128},{128,256},{256,384},{1,129},{129,257},{257,385},{2,130},{1... | collective-permute-start | bytes 73736 | tf_op jit(solution)/shard_map/ppermute | solution.py:373

commit v5 on v4

--- a/solution.py
+++ b/solution.py
@@ -71,17 +71,12 @@
     return value * jax.nn.sigmoid(value)
 
 
-def take(index, core, hidden, kept, tail):
+def fetch(index, core, *refs):
     del index, core
-    kept[...] = hidden[...]
-    tail[...] = hidden[BLOCK - 8 :, :]
-
-
-def fetch(tail, key_hbm, gate_hbm, w_key, w_gate, arrived):
-    del tail
+    count = (len(refs) - 1) // 2
+    arrived = refs[-1]
     copies = [
-        pltpu.make_async_copy(key_hbm, w_key, arrived.at[0]),
-        pltpu.make_async_copy(gate_hbm, w_gate, arrived.at[1]),
+        pltpu.make_async_copy(refs[i], refs[count + i], arrived.at[i]) for i in range(count)
     ]
     for copy in copies:
         copy.start()
@@ -89,38 +84,49 @@
         copy.wait()
 
 
-def spread_out(hidden, edge, w_key, copies):
+def spread_out(hidden, neighbour, w_key, copies):
     del w_key
+    edge = neighbour[BLOCK - 8 :, :]
     for j in range(8):
         copies[j, 0:BLOCK, :] = hidden[...]
-        copies[j, BLOCK:, :] = edge[...]
-
-
-def local_work(
+        copies[j, BLOCK:, :] = edge
+
+
+def conv(pre, taps, extended, columns):
+    extended[0:8, :] = pre[BLOCK:, :]
+    extended[8:, :] = pre[0:BLOCK, :]
+    seg = columns[:, 0:1]
+    total = taps[0:1, :] * pre[0:BLOCK, :]
+    for j in range(1, 4):
+        same = columns[:, 8 * j : 8 * j + 1] == seg
+        total = total + jnp.where(
+            same, taps[j : j + 1, :] * extended[8 - j : 8 - j + BLOCK, :], 0.0
+        )
+    return silu(total)
+
+
+def block_state(
     index,
-    core,
     whole,
     gain,
-    w_query,
     w_key,
     w_value,
-    w_gate,
     w_down,
     w_up,
     bias,
-    head_gain,
     seg_ids,
-    taps_q,
     taps_k,
     taps_v,
-    intra,
-    reach,
     pieces,
-    gate,
     normed,
-    extended,
+    keys_out,
+    values_out,
+    cumulated,
+    columns_out,
+    own_rows,
+    extended_k,
+    extended_v,
 ):
-    del core
     chunks = WIDTH // CHUNK
     squares = jnp.zeros((BLOCK + 8, CHUNK), F32)
     for f in range(chunks):
@@ -133,19 +139,6 @@
         normed[:, lanes] = (activ * scale * gain[:, lanes]).astype(BF16)
     rows = normed[...]
     rank_part = dot(rows, w_down[...], LAST)[0:BLOCK, :]
-    gate_pre = dot(rows, w_gate[...])[0:BLOCK, :]
-
-    def conv(weight, taps, lanes):
-        pre = dot(rows, weight[...])
-        extended[0:8, lanes] = pre[BLOCK:, :]
-        extended[8:, lanes] = pre[0:BLOCK, :]
-        total = taps[0:1, :] * pre[0:BLOCK, :]
-        for j in range(1, 4):
-            same = columns[:, 8 * j : 8 * j + 1] == seg
-            total = total + jnp.where(
-                same, taps[j : j + 1, :] * extended[8 - j : 8 - j + BLOCK, lanes], 0.0
-            )
-        return silu(total)
 
     at = index[0]
     own = seg_ids[pl.ds(at, 1), :].astype(F32)
@@ -162,7 +155,8 @@
     parts += [before, last]
     parts.append(jnp.zeros((BLOCK - 8 * len(parts), BLOCK), F32))
     columns = jnp.transpose(jnp.concatenate(parts, axis=0))
-    seg = columns[:, 0:1]
+    columns_out[...] = columns
+    own_rows[...] = own
 
     logits = dot(rank_part, w_up[...].astype(F32), precision=HIGHEST) + bias[...]
     log_decay = (jnp.minimum(logits, 0.0) - jnp.log(1.0 + jnp.exp(-jnp.abs(logits)))) / 16.0
@@ -170,11 +164,14 @@
     col_iota = lax.broadcasted_iota(jnp.int32, (BLOCK, BLOCK), 1)
     lower = jnp.where(row_iota >= col_iota, 1.0, 0.0).astype(F32)
     cum = dot(lower, log_decay, precision=HIGHEST)
-
-    keys = conv(w_key, taps_k, slice(HEAD_K, 2 * HEAD_K))
-    values = conv(w_value, taps_v, slice(2 * HEAD_K, 2 * HEAD_K + CHUNK)).astype(BF16)
+    cumulated[...] = cum
+
+    keys = conv(dot(rows, w_key[...]), taps_k, extended_k, columns)
+    values = conv(dot(rows, w_value[...]), taps_v, extended_v, columns).astype(BF16)
+    keys_out[...] = keys
+    values_out[...] = values
     final = cum[BLOCK - 1 :, :]
-    pushed = jnp.where(seg == columns[:, 40:41], keys * jnp.exp(final - cum), 0.0)
+    pushed = jnp.where(columns[:, 0:1] == columns[:, 40:41], keys * jnp.exp(final - cum), 0.0)
     state = dot(values, pushed.astype(BF16), FIRST)
     keep = jnp.where(before[0:1, 0:1] == last[0:1, 0:1], jnp.exp(final), 0.0)
     keep_rows = pair_rows(keep)
@@ -182,8 +179,31 @@
         pieces[j, 0:PIECE, :] = state[j * PIECE : (j + 1) * PIECE, :].astype(BF16)
         pieces[j, PIECE:, :] = keep_rows
 
-    gate[...] = silu(gate_pre) * head_gain[...]
-    queries = conv(w_query, taps_q, slice(0, HEAD_K)) * HEAD_K ** (-0.5)
+
+def block_attention(
+    normed,
+    w_query,
+    w_gate,
+    taps_q,
+    head_gain,
+    keys_in,
+    values,
+    cumulated,
+    columns,
+    own_rows,
+    totals,
+    intra,
+    reach,
+    gate,
+    extended,
+):
+    del totals
+    rows = normed[...]
+    gate[...] = silu(dot(rows, w_gate[...])[0:BLOCK, :]) * head_gain[...]
+    queries = conv(dot(rows, w_query[...]), taps_q, extended, columns) * HEAD_K ** (-0.5)
+    keys, cum, seg = keys_in[...], cumulated[...], columns[:, 0:1]
+    row_iota = lax.broadcasted_iota(jnp.int32, (BLOCK, BLOCK), 0)
+    col_iota = lax.broadcasted_iota(jnp.int32, (BLOCK, BLOCK), 1)
     reach[...] = jnp.where(seg == columns[:, 32:33], queries * jnp.exp(cum), 0.0)
     weights = jnp.zeros((BLOCK, BLOCK), F32)
     for half in (8, 16, 32, 64):
@@ -212,9 +232,9 @@
         sums = jnp.sum(product.reshape(BLOCK, HEAD_K), axis=1, keepdims=True)
         inside = (row_iota - col_iota == by) & (row_iota % 8 >= by)
         weights = jnp.where(inside, sums, weights)
-    visible = (seg == own[0:1, :]) & (row_iota >= col_iota)
+    visible = (seg == own_rows[0:1, :]) & (row_iota >= col_iota)
     weights = jnp.where(visible, weights, 0.0)
-    intra[...] = dot(weights.astype(BF16), values)
+    intra[...] = dot(weights.astype(BF16), values[...])
 
 
 def row_scan(pieces, entering, kept, totals):
@@ -227,12 +247,15 @@
         decay = pair[0:1, :] + pair[1:2, :]
         state = state * decay + pieces[j, 0:PIECE, :].astype(F32)
         keep = keep * decay
-    totals[0:PIECE, :] = state
-    totals[PIECE:, :] = jnp.broadcast_to(keep, (8, HEAD_K))
-
-
-def carry(entering, kept, one_back, two_back, states):
-    arriving = one_back[0:PIECE, :] + one_back[PIECE : PIECE + 1, :] * two_back[0:PIECE, :]
+    totals[0:PIECE, :] = state.astype(BF16)
+    totals[PIECE:, :] = pair_rows(keep)
+
+
+def carry(entering, kept, one_back, two_back, reach, states):
+    del reach
+    pair = one_back[PIECE:, :].astype(F32)
+    decay = pair[0:1, :] + pair[1:2, :]
+    arriving = one_back[0:PIECE, :].astype(F32) + decay * two_back[0:PIECE, :].astype(F32)
     for j in range(ROWS_Y):
         states[j] = (entering[j] + kept[j, 0:1, :] * arriving).astype(BF16)
 
@@ -303,77 +326,87 @@
     blocks = ROWS_X * ROWS_Y
 
     onward = [(i, i + 1) for i in range(blocks - 1)]
-    hidden, tail = local_call(
-        take,
-        [((BLOCK, CHUNK), BF16), ((8, CHUNK), BF16)],
-        block_at,
-        core_at,
-        hidden_in,
-        scalars=2,
-        plain=(2,),
-    )
-    edge = lax.ppermute(tail, SEQ, onward)
-    key_here, gate_here = local_call(
-        fetch,
-        [((WIDTH, HEAD_K), BF16), ((WIDTH, CHUNK), BF16)],
-        tail,
+    neighbour = lax.ppermute(hidden_in, SEQ, onward)
+    needed = (
         w_key,
-        w_gate,
-        scratch=[pltpu.SemaphoreType.DMA((2,))],
-        anywhere=(1, 2),
-    )
-    (copies,) = local_call(
-        spread_out,
-        [((8, BLOCK + 8, CHUNK), BF16)],
-        hidden,
-        edge,
-        key_here,
-    )
-    of_core = lax.all_to_all(copies, CHIPS, 0, 0)
-    whole = lax.all_gather(of_core, "core", axis=0)
-    intra, reach, pieces, gate = local_call(
-        local_work,
-        [
-            ((BLOCK, CHUNK), F32),
-            ((BLOCK, HEAD_K), F32),
-            ((ROWS_Y, PIECE + 8, HEAD_K), BF16),
-            ((BLOCK, CHUNK), F32),
-        ],
-        block_at,
-        core_at,
-        whole,
         norm_gain.reshape(1, WIDTH),
-        w_query,
-        key_here,
-        w_value,
-        gate_here,
         w_decay_down.T,
         w_decay_up,
         decay_bias.reshape(1, HEAD_K),
-        head_gain.reshape(1, CHUNK),
         seg_ids.reshape(blocks, BLOCK),
-        conv_query,
         conv_key,
         conv_value,
-        scratch=[
-            pltpu.VMEM((BLOCK + 8, WIDTH), BF16),
-            pltpu.VMEM((BLOCK + 8, 2 * HEAD_K + CHUNK), F32),
+        hidden_in,
+    )
+    key_here, gain, down, up, bias, segs, taps_k, taps_v, hidden = local_call(
+        fetch,
+        [(a.shape, a.dtype) for a in needed],
+        block_at,
+        core_at,
+        *needed,
+        scratch=[pltpu.SemaphoreType.DMA((len(needed),))],
+        scalars=2,
+        anywhere=range(2, 2 + len(needed)),
+    )
+    (copies,) = local_call(
+        spread_out, [((8, BLOCK + 8, CHUNK), BF16)], hidden, neighbour, key_here
+    )
+    of_core = lax.all_to_all(copies, CHIPS, 0, 0)
+    whole = lax.all_gather(of_core, "core", axis=0)
+    pieces, normed, keys, values, cumulated, columns, own_rows = local_call(
+        block_state,
+        [
+            ((ROWS_Y, PIECE + 8, HEAD_K), BF16),
+            ((BLOCK + 8, WIDTH), BF16),
+            ((BLOCK, HEAD_K), F32),
+            ((BLOCK, CHUNK), BF16),
+            ((BLOCK, HEAD_K), F32),
+            ((BLOCK, BLOCK), F32),
+            ((8, BLOCK), F32),
         ],
-        scalars=2,
+        block_at,
+        whole,
+        gain,
+        key_here,
+        w_value,
+        down,
+        up,
+        bias,
+        segs,
+        taps_k,
+        taps_v,
+        scratch=[pltpu.VMEM((BLOCK + 8, HEAD_K), F32), pltpu.VMEM((BLOCK + 8, CHUNK), F32)],
+        scalars=1,
     )
     entering, kept, totals = local_call(
         row_scan,
         [
             ((ROWS_Y, PIECE, HEAD_K), F32),
             ((ROWS_Y, 8, HEAD_K), F32),
-            ((PIECE + 8, HEAD_K), F32),
+            ((PIECE + 8, HEAD_K), BF16),
         ],
         lax.all_to_all(pieces, "y", 0, 0),
     )
     one_back = lax.ppermute(totals, "x", [(i, i + 1) for i in range(ROWS_X - 1)])
     two_back = lax.ppermute(totals, "x", [(i, i + 2) for i in range(ROWS_X - 2)])
+    intra, reach, gate = local_call(
+        block_attention,
+        [((BLOCK, CHUNK), F32), ((BLOCK, HEAD_K), F32), ((BLOCK, CHUNK), F32)],
+        normed,
+        w_query,
+        w_gate,
+        conv_query,
+        head_gain.reshape(1, CHUNK),
+        keys,
+        values,
+        cumulated,
+        columns,
+        own_rows,
+        totals,
+        scratch=[pltpu.VMEM((BLOCK + 8, HEAD_K), F32)],
+    )
     (states,) = local_call(
-        carry, [((ROWS_Y, PIECE, HEAD_K), BF16)], entering, kept, one_back, two_back
+        carry, [((ROWS_Y, PIECE, HEAD_K), BF16)], entering, kept, one_back, two_back, reach
     )
     incoming = lax.all_to_all(states, "y", 0, 0).reshape(CHUNK, HEAD_K)
     mine, my_squares, sent = local_call(

time: 88.8 us -> 86.7 us (0.976)
  waiting for transfers between devices: 0.92 us -> 0.01 us
    ppermute x1, waiting for transfers between devices: 0.92 us -> 0.01 us  [shards(): lax.ppermute(totals, 'x', [(i, i + 1) for i in range(ROWS_X - 1)])]
  transfers between devices with their start and end apart: 3 -> 3, of which waited for: 1 -> 0; matrix products, arithmetic and copies ran while one was open for 0% -> 0% of each run, Pallas kernels for 2% -> 3%
where the time goes in v5:
time: 86.7 us; the launch traced here: 85.8 us
  blocking collectives  68 us (78%)
  starting transfers between devices  10.9 us (13%)
  Pallas kernels  6.15 us (7%)
    all_to_all x1, blocking collectives, shards(): of_core = lax.all_to_all(copies, CHIPS, 0, 0)  19.5 us
    all_to_all x1, blocking collectives, shards(): lax.all_to_all(pieces, 'y', 0, 0)  15.6 us
    all_to_all x1, blocking collectives, shards(): arrived = lax.all_to_all(pairs, CHIPS, 0, 0)  12.9 us
    all_to_all x1, blocking collectives, shards(): incoming = lax.all_to_all(states, 'y', 0, 0).reshape(CHUNK, HEAD_K)  9.73 us
    pallas_call x9, Pallas kernels, local_call(): pl.pallas_call(kernel, out_shape=[jax.ShapeDtypeStruct(s, t) if last else...  6.15 us
    all_gather x1, blocking collectives, shards(): both = lax.all_gather(sent, 'core', axis=0)  5.51 us
    all_gather x1, blocking collectives, shards(): whole = lax.all_gather(of_core, 'core', axis=0)  4.7 us
    ppermute x1, starting transfers between devices, shards(): lax.ppermute(totals, 'x', [(i, i + 2) for i in range(ROWS_X - 2)])  4.65 us
  transfers between devices with their start and end apart: 3, of which 0 were waited for; matrix products, arithmetic and copies ran while one was open for 0% of the time, Pallas kernels for 3%

profile of v5, /device:TPU:1, one launch (start us, length us, event | category | flops | bytes accessed | tf_op | source)
XLA Modules:
  0.0 85.8 jit_solution(10793532983938575784)
XLA Ops:
  0.0 4.0 %collective-permute-start = (bf16[128,128]{1,0:T(8,128)(2,1)}, bf16[128,128]{1,0:T(8,128)(2,1)S(1)}, u32[]{:S(2)}, u32[]{:S(2)}) collective-permute-start(bf16[128,128]{1,0:T(8,128)(2,1)} %refs_8_.1), channel_id=1, source_target_pairs={{0,16},{16,32},{32,48},{48,64},{64,80},{80,96},{96,112},{112,128},... | collective-permute-start | bytes 98312 | tf_op jit(solution)/shard_map/ppermute | solution.py:329
  4.0 1.3 %fetch.1 = (bf16[2048,256]{1,0:T(8,128)(2,1)S(1)}, f32[1,2048]{1,0:T(1,128)S(1)}, bf16[16,2048]{1,0:T(8,128)(2,1)S(1)}, bf16[16,256]{1,0:T(8,128)(2,1)S(1)}, f32...) custom-call(s32[1]{0:T(128)} %bitcast.1.index, ...), custom_call_target="tpu_custom_call" | custom-call | tf_op jit(solution)/shard_map/fetch/pallas_call | solution.py:35
  5.4 0.0 collective-permute-done.neighbour
  5.4 19.5 %all_to_all.20 = bf16[8,136,128]{2,1,0:T(8,128)(2,1)S(1)} all-to-all(bf16[8,136,128]{2,1,0:T(8,128)(2,1)S(1)} %spread_out.1), channel_id=1, replica_groups=mesh['x'=4,'y'=8,'row'=4,'zhi'=2,'core'=2] {'row','zhi'}, dimensions={0} | all-to-all | bytes 557056 | tf_op jit(solution)/shard_map/all_to_all | solution.py:354
  24.9 4.7 %all-gather = bf16[16,136,128]{2,1,0:T(8,128)(2,1)S(1)} all-gather(bf16[8,136,128]{2,1,0:T(8,128)(2,1)S(1)} %all_to_all.20), channel_id=2, replica_groups=mesh['x'=4,'y'=8,'row'=4,'zhi'=2,'core'=2] {'core'}, dimensions={0}, use_global_device_ids=true | all-gather | bytes 835584 | tf_op jit(solution)/shard_map/all_gather | solution.py:355
  29.6 0.0 copy-done.2
  29.7 1.9 %block_state.1 = (bf16[8,24,256]{2,1,0:T(8,128)(2,1)S(1)}, bf16[136,2048]{1,0:T(8,128)(2,1)S(1)}, f32[128,256]{1,0:T(8,128)S(1)}, bf16[128,128]{1,0:T(8,128)(2,1...) custom-call(s32[1]{0:T(128)} %bitcast.1.index, ...), custom_call_target="tpu_custom_call" | custom-call | tf_op jit(solution)/shard_map/block_state/pallas_call | solution.py:35
  31.5 15.6 %all_to_all.21.pieces = bf16[8,24,256]{2,1,0:T(8,128)(2,1)S(1)} all-to-all(bf16[8,24,256]{2,1,0:T(8,128)(2,1)S(1)} %get-tuple-element.45), channel_id=1, replica_groups=mesh['x'=4,'y'=8,'row'=4,'zhi'=2,'core'=2] {'y'}, dimensions={0} | all-to-all | bytes 196608 | tf_op jit(solution)/shard_map/all_to_all | solution.py:388
  47.1 4.6 %collective-permute-start.2 = (bf16[24,256]{1,0:T(8,128)(2,1)S(1)}, bf16[24,256]{1,0:T(8,128)(2,1)S(1)}, u32[]{:S(2)}, u32[]{:S(2)}) collective-permute-start(bf16[24,256]{1,0:T(8,128)(2,1)S(1)} %get-tuple-element.46.totals), channel_id=1, source_target_pairs={{0,256},{128,384},{1,257},{129,385},{2,258},{130,386},{3,259},{131... | collective-permute-start | bytes 36872 | tf_op jit(solution)/shard_map/ppermute | solution.py:391
  51.8 2.2 %collective-permute-start.1 = (bf16[24,256]{1,0:T(8,128)(2,1)S(1)}, bf16[24,256]{1,0:T(8,128)(2,1)S(1)}, u32[]{:S(2)}, u32[]{:S(2)}) collective-permute-start(bf16[24,256]{1,0:T(8,128)(2,1)S(1)} %get-tuple-element.46.totals), channel_id=1, source_target_pairs={{0,128},{128,256},{256,384},{1,129},{129,257},{257,385},{2,130},{1... | collective-permute-start | bytes 36872 | tf_op jit(solution)/shard_map/ppermute | solution.py:390
  54.0 0.0 copy-start.4
  54.0 0.0 copy-start.5
  54.0 0.0 copy-done
  54.1 0.0 copy-done.3
  54.1 0.6 copy-done.4
  54.7 1.3 %block_attention.1 = (f32[128,128]{1,0:T(8,128)S(1)}, f32[128,256]{1,0:T(8,128)S(1)}, f32[128,128]{1,0:T(8,128)S(1)}) custom-call(bf16[136,2048]{1,0:T(8,128)(2,1)S(1)} %get-tuple-element.39.normed, bf16[2048,256]{1,0:T(8,128)(2,1)S(1)} %copy-done, bf16[2048,128]{1,0:T(8,128)(2,1)S(1)} %copy-done.3, f32[4,256]{1,0:T(4,128)S(1)} %copy-done.4, ...), custom_call_target="tpu_custom_call" | custom-call | tf_op jit(solution)/shard_map/block_attention/pallas_call | solution.py:35
  56.0 0.0 collective-permute-done.2.two_back
  56.0 0.0 collective-permute-done.1.one_back
  56.1 9.7 %all_to_all.22 = bf16[8,16,256]{2,1,0:T(8,128)(2,1)S(1)} all-to-all(bf16[8,16,256]{2,1,0:T(8,128)(2,1)S(1)} %carry.1), channel_id=1, replica_groups=mesh['x'=4,'y'=8,'row'=4,'zhi'=2,'core'=2] {'y'}, dimensions={0} | all-to-all | bytes 131072 | tf_op jit(solution)/shard_map/all_to_all | solution.py:411
  65.8 0.6 attend.1
  66.4 5.5 %all-gather.1 = bf16[2064,128]{1,0:T(8,128)(2,1)S(1)} all-gather(bf16[1032,128]{1,0:T(8,128)(2,1)S(1)} %get-tuple-element.54), channel_id=3, replica_groups=mesh['x'=4,'y'=8,'row'=4,'zhi'=2,'core'=2] {'core'}, dimensions={0}, use_global_device_ids=true | all-gather | bytes 792576 | tf_op jit(solution)/shard_map/all_gather | solution.py:423
  71.9 0.1 pair_sum.1
  72.0 12.9 %all_to_all.23.received = bf16[8,136,128]{2,1,0:T(8,128)(2,1)S(1)} all-to-all(bf16[8,136,128]{2,1,0:T(8,128)(2,1)S(1)} %pair_sum.1), channel_id=1, replica_groups=mesh['x'=4,'y'=8,'row'=4,'zhi'=2,'core'=2] {'row','zhi'}, dimensions={0} | all-to-all | bytes 557056 | tf_op jit(solution)/shard_map/all_to_all | solution.py:427
  84.9 0.9 %finish.1 = bf16[128,128]{1,0:T(8,128)(2,1)} custom-call(bf16[8,136,128]{2,1,0:T(8,128)(2,1)S(1)} %all_to_all.23.received, bf16[128,128]{1,0:T(8,128)(2,1)S(1)} %get-tuple-element.30.hidden), custom_call_target="tpu_custom_call" | custom-call | tf_op jit(solution)/shard_map/finish/pallas_call | solution.py:35
  (9 shorter events, 0.1 us)
Async XLA Ops:
  0.0 5.4 %collective-permute-start = (bf16[128,128]{1,0:T(8,128)(2,1)}, bf16[128,128]{1,0:T(8,128)(2,1)S(1)}, u32[]{:S(2)}, u32[]{:S(2)}) collective-permute-start(bf16[128,128]{1,0:T(8,128)(2,1)} %refs_8_.1), channel_id=1, source_target_pairs={{0,16},{16,32},{32,48},{48,64},{64,80},{80,96},{96,112},{112,128},... | collective-permute-start | bytes 98312 | tf_op jit(solution)/shard_map/ppermute | solution.py:329
  24.9 4.7 %copy-start.2 = (bf16[2048,128]{1,0:T(8,128)(2,1)S(1)}, bf16[2048,128]{1,0:T(8,128)(2,1)}, u32[]{:S(2)}) copy-start(bf16[2048,128]{1,0:T(8,128)(2,1)} %w_value.1) | copy-start | bytes 1572868
  29.7 24.4 %copy-start = (bf16[2048,256]{1,0:T(8,128)(2,1)S(1)}, bf16[2048,256]{1,0:T(8,128)(2,1)}, u32[]{:S(2)}) copy-start(bf16[2048,256]{1,0:T(8,128)(2,1)} %w_query.1) | copy-start | bytes 3145732
  29.7 24.4 %copy-start.3 = (bf16[2048,128]{1,0:T(8,128)(2,1)S(1)}, bf16[2048,128]{1,0:T(8,128)(2,1)}, u32[]{:S(2)}) copy-start(bf16[2048,128]{1,0:T(8,128)(2,1)} %w_gate.1) | copy-start | bytes 1572868
  47.1 8.9 %collective-permute-start.2 = (bf16[24,256]{1,0:T(8,128)(2,1)S(1)}, bf16[24,256]{1,0:T(8,128)(2,1)S(1)}, u32[]{:S(2)}, u32[]{:S(2)}) collective-permute-start(bf16[24,256]{1,0:T(8,128)(2,1)S(1)} %get-tuple-element.46.totals), channel_id=1, source_target_pairs={{0,256},{128,384},{1,257},{129,385},{2,258},{130,386},{3,259},{131... | collective-permute-start | bytes 36872 | tf_op jit(solution)/shard_map/ppermute | solution.py:391
  51.8 4.2 %collective-permute-start.1 = (bf16[24,256]{1,0:T(8,128)(2,1)S(1)}, bf16[24,256]{1,0:T(8,128)(2,1)S(1)}, u32[]{:S(2)}, u32[]{:S(2)}) collective-permute-start(bf16[24,256]{1,0:T(8,128)(2,1)S(1)} %get-tuple-element.46.totals), channel_id=1, source_target_pairs={{0,128},{128,256},{256,384},{1,129},{129,257},{257,385},{2,130},{1... | collective-permute-start | bytes 36872 | tf_op jit(solution)/shard_map/ppermute | solution.py:390
  54.0 0.7 copy-start.4
  54.0 0.7 copy-start.5
  56.0 9.8 %copy-start.1 = (bf16[128,2048]{1,0:T(8,128)(2,1)S(1)}, bf16[128,2048]{1,0:T(8,128)(2,1)}, u32[]{:S(2)}) copy-start(bf16[128,2048]{1,0:T(8,128)(2,1)} %w_out.1) | copy-start | bytes 1572868

commit v6 on v5

--- a/solution.py
+++ b/solution.py
@@ -19,6 +19,7 @@
 SEQ = ("x", "y")
 CHIPS = ("row", "zhi")
 ROWS_X, ROWS_Y = 4, 8
+LANES = 128
 PIECE = BLOCK // ROWS_Y
 
 
@@ -65,6 +66,25 @@
         jnp.where(index == 1, jnp.broadcast_to(low.astype(F32), shape), 0.0),
     )
     return both.astype(BF16)
+
+
+def pair_lanes(value):
+    shape = (8, LANES)
+    index = lax.broadcasted_iota(jnp.int32, shape, 0)
+    out = jnp.zeros(shape, F32)
+    for i, part in enumerate(halves(value)):
+        for j in range(2):
+            row = part.astype(F32)[:, j * LANES : (j + 1) * LANES]
+            out = jnp.where(index == 2 * i + j, jnp.broadcast_to(row, shape), out)
+    return out.astype(BF16)
+
+
+def unpaired(piece):
+    wide = piece.astype(F32)
+    state = jnp.concatenate([wide[0:PIECE], wide[PIECE : 2 * PIECE]], axis=1)
+    rows = wide[2 * PIECE :]
+    decay = jnp.concatenate([rows[0:1] + rows[2:3], rows[1:2] + rows[3:4]], axis=1)
+    return state, decay
 
 
 def silu(value):
@@ -174,10 +194,12 @@
     pushed = jnp.where(columns[:, 0:1] == columns[:, 40:41], keys * jnp.exp(final - cum), 0.0)
     state = dot(values, pushed.astype(BF16), FIRST)
     keep = jnp.where(before[0:1, 0:1] == last[0:1, 0:1], jnp.exp(final), 0.0)
-    keep_rows = pair_rows(keep)
+    keep_rows = pair_lanes(keep)
     for j in range(ROWS_Y):
-        pieces[j, 0:PIECE, :] = state[j * PIECE : (j + 1) * PIECE, :].astype(BF16)
-        pieces[j, PIECE:, :] = keep_rows
+        piece = state[j * PIECE : (j + 1) * PIECE, :].astype(BF16)
+        pieces[j, 0:PIECE, :] = piece[:, :LANES]
+        pieces[j, PIECE : 2 * PIECE, :] = piece[:, LANES:]
+        pieces[j, 2 * PIECE :, :] = keep_rows
 
 
 def block_attention(
@@ -243,19 +265,18 @@
     for j in range(ROWS_Y):
         entering[j] = state
         kept[j] = jnp.broadcast_to(keep, (8, HEAD_K))
-        pair = pieces[j, PIECE:, :].astype(F32)
-        decay = pair[0:1, :] + pair[1:2, :]
-        state = state * decay + pieces[j, 0:PIECE, :].astype(F32)
+        both, decay = unpaired(pieces[j])
+        state = state * decay + both
         keep = keep * decay
-    totals[0:PIECE, :] = state.astype(BF16)
-    totals[PIECE:, :] = pair_rows(keep)
-
-
-def carry(entering, kept, one_back, two_back, reach, states):
+    totals[0:PIECE, :] = state[:, :LANES].astype(BF16)
+    totals[PIECE : 2 * PIECE, :] = state[:, LANES:].astype(BF16)
+    totals[2 * PIECE :, :] = pair_lanes(keep)
+
+
+def carry(entering, kept, two_back, one_back, reach, states):
     del reach
-    pair = one_back[PIECE:, :].astype(F32)
-    decay = pair[0:1, :] + pair[1:2, :]
-    arriving = one_back[0:PIECE, :].astype(F32) + decay * two_back[0:PIECE, :].astype(F32)
+    near, decay = unpaired(one_back[...])
+    arriving = near + decay * unpaired(two_back[...])[0]
     for j in range(ROWS_Y):
         states[j] = (entering[j] + kept[j, 0:1, :] * arriving).astype(BF16)
 
@@ -356,7 +377,7 @@
     pieces, normed, keys, values, cumulated, columns, own_rows = local_call(
         block_state,
         [
-            ((ROWS_Y, PIECE + 8, HEAD_K), BF16),
+            ((ROWS_Y, 2 * PIECE + 8, LANES), BF16),
             ((BLOCK + 8, WIDTH), BF16),
             ((BLOCK, HEAD_K), F32),
             ((BLOCK, CHUNK), BF16),
@@ -383,7 +404,7 @@
         [
             ((ROWS_Y, PIECE, HEAD_K), F32),
             ((ROWS_Y, 8, HEAD_K), F32),
-            ((PIECE + 8, HEAD_K), BF16),
+            ((2 * PIECE + 8, LANES), BF16),
         ],
         lax.all_to_all(pieces, "y", 0, 0),
     )
@@ -406,7 +427,7 @@
         scratch=[pltpu.VMEM((BLOCK + 8, HEAD_K), F32)],
     )
     (states,) = local_call(
-        carry, [((ROWS_Y, PIECE, HEAD_K), BF16)], entering, kept, one_back, two_back, reach
+        carry, [((ROWS_Y, PIECE, HEAD_K), BF16)], entering, kept, two_back, one_back, reach
     )
     incoming = lax.all_to_all(states, "y", 0, 0).reshape(CHUNK, HEAD_K)
     mine, my_squares, sent = local_call(

time: 86.7 us -> 87 us (level)
    ppermute x1, starting transfers between devices: 2.22 us -> 3.12 us  [shards(): lax.ppermute(totals, 'x', [(i, i + 1) for i in range(ROWS_X - 1)])]
where the time goes in v6:
time: 87 us; the launch traced here: 86.2 us
  blocking collectives  67.7 us (78%)
  starting transfers between devices  11.5 us (13%)
  Pallas kernels  6.15 us (7%)
    all_to_all x1, blocking collectives, shards(): of_core = lax.all_to_all(copies, CHIPS, 0, 0)  19.5 us
    all_to_all x1, blocking collectives, shards(): lax.all_to_all(pieces, 'y', 0, 0)  15.4 us
    all_to_all x1, blocking collectives, shards(): arrived = lax.all_to_all(pairs, CHIPS, 0, 0)  12.9 us
    all_to_all x1, blocking collectives, shards(): incoming = lax.all_to_all(states, 'y', 0, 0).reshape(CHUNK, HEAD_K)  9.73 us
    pallas_call x9, Pallas kernels, local_call(): pl.pallas_call(kernel, out_shape=[jax.ShapeDtypeStruct(s, t) if last else...  6.15 us
    all_gather x1, blocking collectives, shards(): both = lax.all_gather(sent, 'core', axis=0)  5.42 us
    all_gather x1, blocking collectives, shards(): whole = lax.all_gather(of_core, 'core', axis=0)  4.7 us
    ppermute x1, starting transfers between devices, shards(): lax.ppermute(totals, 'x', [(i, i + 2) for i in range(ROWS_X - 2)])  4.35 us
  transfers between devices with their start and end apart: 3, of which 0 were waited for; matrix products, arithmetic and copies ran while one was open for 0% of the time, Pallas kernels for 3%

profile of v6, /device:TPU:1, one launch (start us, length us, event | category | flops | bytes accessed | tf_op | source)
XLA Modules:
  0.0 86.2 jit_solution(9623438334948785679)
XLA Ops:
  0.0 4.0 %collective-permute-start = (bf16[128,128]{1,0:T(8,128)(2,1)}, bf16[128,128]{1,0:T(8,128)(2,1)S(1)}, u32[]{:S(2)}, u32[]{:S(2)}) collective-permute-start(bf16[128,128]{1,0:T(8,128)(2,1)} %refs_8_.1), channel_id=1, source_target_pairs={{0,16},{16,32},{32,48},{48,64},{64,80},{80,96},{96,112},{112,128},... | collective-permute-start | bytes 98312 | tf_op jit(solution)/shard_map/ppermute | solution.py:350
  4.0 1.3 %fetch.1 = (bf16[2048,256]{1,0:T(8,128)(2,1)S(1)}, f32[1,2048]{1,0:T(1,128)S(1)}, bf16[16,2048]{1,0:T(8,128)(2,1)S(1)}, bf16[16,256]{1,0:T(8,128)(2,1)S(1)}, f32...) custom-call(s32[1]{0:T(128)} %bitcast.1.index, ...), custom_call_target="tpu_custom_call" | custom-call | tf_op jit(solution)/shard_map/fetch/pallas_call | solution.py:36
  5.4 0.0 collective-permute-done.neighbour
  5.4 19.5 %all_to_all.20 = bf16[8,136,128]{2,1,0:T(8,128)(2,1)S(1)} all-to-all(bf16[8,136,128]{2,1,0:T(8,128)(2,1)S(1)} %spread_out.1), channel_id=1, replica_groups=mesh['x'=4,'y'=8,'row'=4,'zhi'=2,'core'=2] {'row','zhi'}, dimensions={0} | all-to-all | bytes 557056 | tf_op jit(solution)/shard_map/all_to_all | solution.py:375
  24.9 4.7 %all-gather = bf16[16,136,128]{2,1,0:T(8,128)(2,1)S(1)} all-gather(bf16[8,136,128]{2,1,0:T(8,128)(2,1)S(1)} %all_to_all.20), channel_id=2, replica_groups=mesh['x'=4,'y'=8,'row'=4,'zhi'=2,'core'=2] {'core'}, dimensions={0}, use_global_device_ids=true | all-gather | bytes 835584 | tf_op jit(solution)/shard_map/all_gather | solution.py:376
  29.6 0.0 copy-done.2
  29.7 1.9 %block_state.1 = (bf16[8,40,128]{2,1,0:T(8,128)(2,1)S(1)}, bf16[136,2048]{1,0:T(8,128)(2,1)S(1)}, f32[128,256]{1,0:T(8,128)S(1)}, bf16[128,128]{1,0:T(8,128)(2,1...) custom-call(s32[1]{0:T(128)} %bitcast.1.index, ...), custom_call_target="tpu_custom_call" | custom-call | tf_op jit(solution)/shard_map/block_state/pallas_call | solution.py:36
  31.5 15.4 %all_to_all.21.pieces = bf16[8,40,128]{2,1,0:T(8,128)(2,1)S(1)} all-to-all(bf16[8,40,128]{2,1,0:T(8,128)(2,1)S(1)} %get-tuple-element.45), channel_id=1, replica_groups=mesh['x'=4,'y'=8,'row'=4,'zhi'=2,'core'=2] {'y'}, dimensions={0} | all-to-all | bytes 163840 | tf_op jit(solution)/shard_map/all_to_all | solution.py:409
  47.0 3.1 %collective-permute-start.2 = (bf16[40,128]{1,0:T(8,128)(2,1)S(1)}, bf16[40,128]{1,0:T(8,128)(2,1)S(1)}, u32[]{:S(2)}, u32[]{:S(2)}) collective-permute-start(bf16[40,128]{1,0:T(8,128)(2,1)S(1)} %get-tuple-element.46.totals), channel_id=1, source_target_pairs={{0,128},{128,256},{256,384},{1,129},{129,257},{257,385},{2,130},{1... | collective-permute-start | bytes 30728 | tf_op jit(solution)/shard_map/ppermute | solution.py:411
  50.1 4.4 %collective-permute-start.1 = (bf16[40,128]{1,0:T(8,128)(2,1)S(1)}, bf16[40,128]{1,0:T(8,128)(2,1)S(1)}, u32[]{:S(2)}, u32[]{:S(2)}) collective-permute-start(bf16[40,128]{1,0:T(8,128)(2,1)S(1)} %get-tuple-element.46.totals), channel_id=1, source_target_pairs={{0,256},{128,384},{1,257},{129,385},{2,258},{130,386},{3,259},{131... | collective-permute-start | bytes 30728 | tf_op jit(solution)/shard_map/ppermute | solution.py:412
  54.5 0.0 copy-start.4
  54.5 0.0 copy-start.5
  54.5 0.0 copy-done
  54.5 0.6 copy-done.4
  55.2 0.0 copy-done.5
  55.2 1.3 %block_attention.1 = (f32[128,128]{1,0:T(8,128)S(1)}, f32[128,256]{1,0:T(8,128)S(1)}, f32[128,128]{1,0:T(8,128)S(1)}) custom-call(bf16[136,2048]{1,0:T(8,128)(2,1)S(1)} %get-tuple-element.39.normed, bf16[2048,256]{1,0:T(8,128)(2,1)S(1)} %copy-done, bf16[2048,128]{1,0:T(8,128)(2,1)S(1)} %copy-done.3, f32[4,256]{1,0:T(4,128)S(1)} %copy-done.4, ...), custom_call_target="tpu_custom_call" | custom-call | tf_op jit(solution)/shard_map/block_attention/pallas_call | solution.py:36
  56.5 0.0 collective-permute-done.2.one_back
  56.5 0.0 collective-permute-done.1.two_back
  56.5 9.7 %all_to_all.22 = bf16[8,16,256]{2,1,0:T(8,128)(2,1)S(1)} all-to-all(bf16[8,16,256]{2,1,0:T(8,128)(2,1)S(1)} %carry.1), channel_id=1, replica_groups=mesh['x'=4,'y'=8,'row'=4,'zhi'=2,'core'=2] {'y'}, dimensions={0} | all-to-all | bytes 131072 | tf_op jit(solution)/shard_map/all_to_all | solution.py:432
  66.3 0.6 attend.1
  66.9 5.4 %all-gather.1 = bf16[2064,128]{1,0:T(8,128)(2,1)S(1)} all-gather(bf16[1032,128]{1,0:T(8,128)(2,1)S(1)} %get-tuple-element.54), channel_id=3, replica_groups=mesh['x'=4,'y'=8,'row'=4,'zhi'=2,'core'=2] {'core'}, dimensions={0}, use_global_device_ids=true | all-gather | bytes 792576 | tf_op jit(solution)/shard_map/all_gather | solution.py:444
  72.3 0.1 pair_sum.1
  72.4 12.9 %all_to_all.23.received = bf16[8,136,128]{2,1,0:T(8,128)(2,1)S(1)} all-to-all(bf16[8,136,128]{2,1,0:T(8,128)(2,1)S(1)} %pair_sum.1), channel_id=1, replica_groups=mesh['x'=4,'y'=8,'row'=4,'zhi'=2,'core'=2] {'row','zhi'}, dimensions={0} | all-to-all | bytes 557056 | tf_op jit(solution)/shard_map/all_to_all | solution.py:448
  85.3 0.9 %finish.1 = bf16[128,128]{1,0:T(8,128)(2,1)} custom-call(bf16[8,136,128]{2,1,0:T(8,128)(2,1)S(1)} %all_to_all.23.received, bf16[128,128]{1,0:T(8,128)(2,1)S(1)} %get-tuple-element.30.hidden), custom_call_target="tpu_custom_call" | custom-call | tf_op jit(solution)/shard_map/finish/pallas_call | solution.py:36
  (9 shorter events, 0.1 us)
Async XLA Ops:
  0.0 5.4 %collective-permute-start = (bf16[128,128]{1,0:T(8,128)(2,1)}, bf16[128,128]{1,0:T(8,128)(2,1)S(1)}, u32[]{:S(2)}, u32[]{:S(2)}) collective-permute-start(bf16[128,128]{1,0:T(8,128)(2,1)} %refs_8_.1), channel_id=1, source_target_pairs={{0,16},{16,32},{32,48},{48,64},{64,80},{80,96},{96,112},{112,128},... | collective-permute-start | bytes 98312 | tf_op jit(solution)/shard_map/ppermute | solution.py:350
  24.9 4.7 %copy-start.2 = (bf16[2048,128]{1,0:T(8,128)(2,1)S(1)}, bf16[2048,128]{1,0:T(8,128)(2,1)}, u32[]{:S(2)}) copy-start(bf16[2048,128]{1,0:T(8,128)(2,1)} %w_value.1) | copy-start | bytes 1572868
  29.7 24.9 %copy-start = (bf16[2048,256]{1,0:T(8,128)(2,1)S(1)}, bf16[2048,256]{1,0:T(8,128)(2,1)}, u32[]{:S(2)}) copy-start(bf16[2048,256]{1,0:T(8,128)(2,1)} %w_query.1) | copy-start | bytes 3145732
  29.7 24.9 %copy-start.3 = (bf16[2048,128]{1,0:T(8,128)(2,1)S(1)}, bf16[2048,128]{1,0:T(8,128)(2,1)}, u32[]{:S(2)}) copy-start(bf16[2048,128]{1,0:T(8,128)(2,1)} %w_gate.1) | copy-start | bytes 1572868
  47.0 9.5 %collective-permute-start.2 = (bf16[40,128]{1,0:T(8,128)(2,1)S(1)}, bf16[40,128]{1,0:T(8,128)(2,1)S(1)}, u32[]{:S(2)}, u32[]{:S(2)}) collective-permute-start(bf16[40,128]{1,0:T(8,128)(2,1)S(1)} %get-tuple-element.46.totals), channel_id=1, source_target_pairs={{0,128},{128,256},{256,384},{1,129},{129,257},{257,385},{2,130},{1... | collective-permute-start | bytes 30728 | tf_op jit(solution)/shard_map/ppermute | solution.py:411
  50.1 6.4 %collective-permute-start.1 = (bf16[40,128]{1,0:T(8,128)(2,1)S(1)}, bf16[40,128]{1,0:T(8,128)(2,1)S(1)}, u32[]{:S(2)}, u32[]{:S(2)}) collective-permute-start(bf16[40,128]{1,0:T(8,128)(2,1)S(1)} %get-tuple-element.46.totals), channel_id=1, source_target_pairs={{0,256},{128,384},{1,257},{129,385},{2,258},{130,386},{3,259},{131... | collective-permute-start | bytes 30728 | tf_op jit(solution)/shard_map/ppermute | solution.py:412
  54.5 0.7 copy-start.4
  54.5 0.7 copy-start.5
  56.5 9.8 %copy-start.1 = (bf16[128,2048]{1,0:T(8,128)(2,1)S(1)}, bf16[128,2048]{1,0:T(8,128)(2,1)}, u32[]{:S(2)}) copy-start(bf16[128,2048]{1,0:T(8,128)(2,1)} %w_out.1) | copy-start | bytes 1572868

commit v7 on v6

--- a/solution.py
+++ b/solution.py
@@ -268,15 +268,23 @@
         both, decay = unpaired(pieces[j])
         state = state * decay + both
         keep = keep * decay
-    totals[0:PIECE, :] = state[:, :LANES].astype(BF16)
-    totals[PIECE : 2 * PIECE, :] = state[:, LANES:].astype(BF16)
-    totals[2 * PIECE :, :] = pair_lanes(keep)
-
-
-def carry(entering, kept, two_back, one_back, reach, states):
+    last = pair_lanes(keep)
+    for x in range(ROWS_X):
+        totals[x, 0:PIECE, :] = state[:, :LANES].astype(BF16)
+        totals[x, PIECE : 2 * PIECE, :] = state[:, LANES:].astype(BF16)
+        totals[x, 2 * PIECE :, :] = last
+
+
+def carry(index, rows, entering, kept, reach, states):
     del reach
-    near, decay = unpaired(one_back[...])
-    arriving = near + decay * unpaired(two_back[...])[0]
+    row = index[0] // ROWS_Y
+
+    def back(by):
+        state, decay = unpaired(rows[jnp.maximum(row - by, 0)])
+        return jnp.where(row >= by, state, 0.0), decay
+
+    near, decay = back(1)
+    arriving = near + decay * back(2)[0]
     for j in range(ROWS_Y):
         states[j] = (entering[j] + kept[j, 0:1, :] * arriving).astype(BF16)
 
@@ -404,12 +412,11 @@
         [
             ((ROWS_Y, PIECE, HEAD_K), F32),
             ((ROWS_Y, 8, HEAD_K), F32),
-            ((2 * PIECE + 8, LANES), BF16),
+            ((ROWS_X, 2 * PIECE + 8, LANES), BF16),
         ],
         lax.all_to_all(pieces, "y", 0, 0),
     )
-    one_back = lax.ppermute(totals, "x", [(i, i + 1) for i in range(ROWS_X - 1)])
-    two_back = lax.ppermute(totals, "x", [(i, i + 2) for i in range(ROWS_X - 2)])
+    rows = lax.all_to_all(totals, "x", 0, 0)
     intra, reach, gate = local_call(
         block_attention,
         [((BLOCK, CHUNK), F32), ((BLOCK, HEAD_K), F32), ((BLOCK, CHUNK), F32)],
@@ -427,7 +434,14 @@
         scratch=[pltpu.VMEM((BLOCK + 8, HEAD_K), F32)],
     )
     (states,) = local_call(
-        carry, [((ROWS_Y, PIECE, HEAD_K), BF16)], entering, kept, two_back, one_back, reach
+        carry,
+        [((ROWS_Y, PIECE, HEAD_K), BF16)],
+        block_at,
+        rows,
+        entering,
+        kept,
+        reach,
+        scalars=1,
     )
     incoming = lax.all_to_all(states, "y", 0, 0).reshape(CHUNK, HEAD_K)
     mine, my_squares, sent = local_call(

time: 87 us -> 86.8 us (level)
  starting transfers between devices: 11.5 us -> 8.03 us
  waiting for transfers between devices: 0.01 us -> 1.55 us
  Pallas kernels: 6.15 us -> 7.54 us
    ppermute x2 -> x0, starting transfers between devices: 7.47 us -> none  [the longest x1 4.35 us: shards(): lax.ppermute(totals, 'x', [(i, i + 2) for i in range(ROWS_X - 2)])]
    all_to_all x0 -> x1, starting transfers between devices: none -> 4.01 us  [shards(): rows = lax.all_to_all(totals, 'x', 0, 0)]
    all_to_all x0 -> x1, waiting for transfers between devices: none -> 1.55 us  [shards(): rows = lax.all_to_all(totals, 'x', 0, 0)]
    pallas_call x9, Pallas kernels: 6.15 us -> 7.54 us  [local_call(): pl.pallas_call(kernel, out_shape=[jax.ShapeDtypeStruct(s, t) if last else...]
    all_gather x1, blocking collectives: 5.42 us -> 6.29 us  [shards(): both = lax.all_gather(sent, 'core', axis=0)]
  transfers between devices with their start and end apart: 3 -> 2, of which waited for: 0 -> 1; matrix products, arithmetic and copies ran while one was open for 0% -> 0% of each run, Pallas kernels for 3% -> 4%
where the time goes in v7:
time: 86.8 us; the launch traced here: 86.4 us
  blocking collectives  68.5 us (79%)
  starting transfers between devices  8.03 us (9%)
  Pallas kernels  7.54 us (9%)
  waiting for transfers between devices  1.55 us (2%)
    all_to_all x1, blocking collectives, shards(): of_core = lax.all_to_all(copies, CHIPS, 0, 0)  19.5 us
    all_to_all x1, blocking collectives, shards(): lax.all_to_all(pieces, 'y', 0, 0)  15.4 us
    all_to_all x1, blocking collectives, shards(): arrived = lax.all_to_all(pairs, CHIPS, 0, 0)  12.9 us
    all_to_all x1, blocking collectives, shards(): incoming = lax.all_to_all(states, 'y', 0, 0).reshape(CHUNK, HEAD_K)  9.6 us
    pallas_call x9, Pallas kernels, local_call(): pl.pallas_call(kernel, out_shape=[jax.ShapeDtypeStruct(s, t) if last else...  7.54 us
    all_gather x1, blocking collectives, shards(): both = lax.all_gather(sent, 'core', axis=0)  6.29 us
    all_gather x1, blocking collectives, shards(): whole = lax.all_gather(of_core, 'core', axis=0)  4.7 us
    ppermute x1, starting transfers between devices, shards(): neighbour = lax.ppermute(hidden_in, SEQ, onward)  4.02 us
  transfers between devices with their start and end apart: 2, of which 1 were waited for; matrix products, arithmetic and copies ran while one was open for 0% of the time, Pallas kernels for 4%

profile of v7, /device:TPU:1, one launch (start us, length us, event | category | flops | bytes accessed | tf_op | source)
XLA Modules:
  0.0 86.4 jit_solution(8646152519509707504)
XLA Ops:
  0.0 4.0 %collective-permute-start = (bf16[128,128]{1,0:T(8,128)(2,1)}, bf16[128,128]{1,0:T(8,128)(2,1)S(1)}, u32[]{:S(2)}, u32[]{:S(2)}) collective-permute-start(bf16[128,128]{1,0:T(8,128)(2,1)} %refs_8_.1), channel_id=1, source_target_pairs={{0,16},{16,32},{32,48},{48,64},{64,80},{80,96},{96,112},{112,128},... | collective-permute-start | bytes 98312 | tf_op jit(solution)/shard_map/ppermute | solution.py:358
  4.0 1.3 %fetch.1 = (bf16[2048,256]{1,0:T(8,128)(2,1)S(1)}, f32[1,2048]{1,0:T(1,128)S(1)}, bf16[16,2048]{1,0:T(8,128)(2,1)S(1)}, bf16[16,256]{1,0:T(8,128)(2,1)S(1)}, f32...) custom-call(s32[1]{0:T(128)} %bitcast.1.index, ...), custom_call_target="tpu_custom_call" | custom-call | tf_op jit(solution)/shard_map/fetch/pallas_call | solution.py:36
  5.4 0.0 collective-permute-done.neighbour
  5.4 19.5 %all_to_all.25 = bf16[8,136,128]{2,1,0:T(8,128)(2,1)S(1)} all-to-all(bf16[8,136,128]{2,1,0:T(8,128)(2,1)S(1)} %spread_out.1), channel_id=1, replica_groups=mesh['x'=4,'y'=8,'row'=4,'zhi'=2,'core'=2] {'row','zhi'}, dimensions={0} | all-to-all | bytes 557056 | tf_op jit(solution)/shard_map/all_to_all | solution.py:383
  24.9 0.0 copy-start.2
  25.0 4.7 %all-gather = bf16[16,136,128]{2,1,0:T(8,128)(2,1)S(1)} all-gather(bf16[8,136,128]{2,1,0:T(8,128)(2,1)S(1)} %all_to_all.25), channel_id=2, replica_groups=mesh['x'=4,'y'=8,'row'=4,'zhi'=2,'core'=2] {'core'}, dimensions={0}, use_global_device_ids=true | all-gather | bytes 835584 | tf_op jit(solution)/shard_map/all_gather | solution.py:384
  29.7 0.0 copy-done.2
  29.7 1.9 %block_state.1 = (bf16[8,40,128]{2,1,0:T(8,128)(2,1)S(1)}, bf16[136,2048]{1,0:T(8,128)(2,1)S(1)}, f32[128,256]{1,0:T(8,128)S(1)}, bf16[128,128]{1,0:T(8,128)(2,1...) custom-call(s32[1]{0:T(128)} %bitcast.1.index, ...), custom_call_target="tpu_custom_call" | custom-call | tf_op jit(solution)/shard_map/block_state/pallas_call | solution.py:36
  31.5 15.4 %all_to_all.26.pieces = bf16[8,40,128]{2,1,0:T(8,128)(2,1)S(1)} all-to-all(bf16[8,40,128]{2,1,0:T(8,128)(2,1)S(1)} %get-tuple-element.45), channel_id=1, replica_groups=mesh['x'=4,'y'=8,'row'=4,'zhi'=2,'core'=2] {'y'}, dimensions={0} | all-to-all | bytes 163840 | tf_op jit(solution)/shard_map/all_to_all | solution.py:417
  47.0 0.6 row_scan.1
  47.6 4.0 %all-to-all-start.2 = ((bf16[4,40,128]{2,1,0:T(8,128)(2,1)}), bf16[4,40,128]{2,1,0:T(8,128)(2,1)S(1)}, u32[]{:S(2)}, u32[]{:S(2)}) async-start(bf16[4,40,128]{2,1,0:T(8,128)(2,1)} %get-tuple-element.46.totals), calls=%async_computation.2 | async-start | bytes 81920 | tf_op jit(solution)/shard_map/all_to_all | solution.py:419
  51.6 0.0 copy-done
  51.6 0.0 copy-done.3
  51.6 0.7 copy-done.4
  52.3 0.0 copy-done.5
  52.3 2.1 %block_attention.1 = (f32[128,128]{1,0:T(8,128)S(1)}, f32[128,256]{1,0:T(8,128)S(1)}, f32[128,128]{1,0:T(8,128)S(1)}) custom-call(bf16[136,2048]{1,0:T(8,128)(2,1)S(1)} %get-tuple-element.39.normed, bf16[2048,256]{1,0:T(8,128)(2,1)S(1)} %copy-done, bf16[2048,128]{1,0:T(8,128)(2,1)S(1)} %copy-done.3, f32[4,256]{1,0:T(4,128)S(1)} %copy-done.4, ...), custom_call_target="tpu_custom_call" | custom-call | tf_op jit(solution)/shard_map/block_attention/pallas_call | solution.py:36
  54.4 1.5 %all-to-all-done.2.rows = bf16[4,40,128]{2,1,0:T(8,128)(2,1)S(1)} async-done(((bf16[4,40,128]{2,1,0:T(8,128)(2,1)}), bf16[4,40,128]{2,1,0:T(8,128)(2,1)S(1)}, u32[]{:S(2)}, u32[]{:S(2)}) %all-to-all-start.2) | async-done | bytes 40992 | tf_op jit(solution)/shard_map/all_to_all | solution.py:419
  56.0 9.6 %all_to_all.27 = bf16[8,16,256]{2,1,0:T(8,128)(2,1)S(1)} all-to-all(bf16[8,16,256]{2,1,0:T(8,128)(2,1)S(1)} %carry.1), channel_id=1, replica_groups=mesh['x'=4,'y'=8,'row'=4,'zhi'=2,'core'=2] {'y'}, dimensions={0} | all-to-all | bytes 131072 | tf_op jit(solution)/shard_map/all_to_all | solution.py:446
  65.6 0.0 copy-done.1
  65.6 0.6 attend.1
  66.2 6.3 %all-gather.1 = bf16[2064,128]{1,0:T(8,128)(2,1)S(1)} all-gather(bf16[1032,128]{1,0:T(8,128)(2,1)S(1)} %get-tuple-element.54), channel_id=3, replica_groups=mesh['x'=4,'y'=8,'row'=4,'zhi'=2,'core'=2] {'core'}, dimensions={0}, use_global_device_ids=true | all-gather | bytes 792576 | tf_op jit(solution)/shard_map/all_gather | solution.py:458
  72.5 0.1 pair_sum.1
  72.6 12.9 %all_to_all.28.received = bf16[8,136,128]{2,1,0:T(8,128)(2,1)S(1)} all-to-all(bf16[8,136,128]{2,1,0:T(8,128)(2,1)S(1)} %pair_sum.1), channel_id=1, replica_groups=mesh['x'=4,'y'=8,'row'=4,'zhi'=2,'core'=2] {'row','zhi'}, dimensions={0} | all-to-all | bytes 557056 | tf_op jit(solution)/shard_map/all_to_all | solution.py:462
  85.5 0.9 %finish.1 = bf16[128,128]{1,0:T(8,128)(2,1)} custom-call(bf16[8,136,128]{2,1,0:T(8,128)(2,1)S(1)} %all_to_all.28.received, bf16[128,128]{1,0:T(8,128)(2,1)S(1)} %get-tuple-element.30.hidden), custom_call_target="tpu_custom_call" | custom-call | tf_op jit(solution)/shard_map/finish/pallas_call | solution.py:36
  (7 shorter events, 0.1 us)
Async XLA Ops:
  0.0 5.4 %collective-permute-start = (bf16[128,128]{1,0:T(8,128)(2,1)}, bf16[128,128]{1,0:T(8,128)(2,1)S(1)}, u32[]{:S(2)}, u32[]{:S(2)}) collective-permute-start(bf16[128,128]{1,0:T(8,128)(2,1)} %refs_8_.1), channel_id=1, source_target_pairs={{0,16},{16,32},{32,48},{48,64},{64,80},{80,96},{96,112},{112,128},... | collective-permute-start | bytes 98312 | tf_op jit(solution)/shard_map/ppermute | solution.py:358
  24.9 4.7 %copy-start.2 = (bf16[2048,128]{1,0:T(8,128)(2,1)S(1)}, bf16[2048,128]{1,0:T(8,128)(2,1)}, u32[]{:S(2)}) copy-start(bf16[2048,128]{1,0:T(8,128)(2,1)} %w_value.1) | copy-start | bytes 1572868
  29.7 22.0 %copy-start = (bf16[2048,256]{1,0:T(8,128)(2,1)S(1)}, bf16[2048,256]{1,0:T(8,128)(2,1)}, u32[]{:S(2)}) copy-start(bf16[2048,256]{1,0:T(8,128)(2,1)} %w_query.1) | copy-start | bytes 3145732
  29.7 22.0 %copy-start.3 = (bf16[2048,128]{1,0:T(8,128)(2,1)S(1)}, bf16[2048,128]{1,0:T(8,128)(2,1)}, u32[]{:S(2)}) copy-start(bf16[2048,128]{1,0:T(8,128)(2,1)} %w_gate.1) | copy-start | bytes 1572868
  47.6 8.4 %all-to-all-start.2 = ((bf16[4,40,128]{2,1,0:T(8,128)(2,1)}), bf16[4,40,128]{2,1,0:T(8,128)(2,1)S(1)}, u32[]{:S(2)}, u32[]{:S(2)}) async-start(bf16[4,40,128]{2,1,0:T(8,128)(2,1)} %get-tuple-element.46.totals), calls=%async_computation.2 | async-start | bytes 81920 | tf_op jit(solution)/shard_map/all_to_all | solution.py:419
  51.6 0.7 copy-start.4
  51.6 0.7 copy-start.5
  54.4 11.2 %copy-start.1 = (bf16[128,2048]{1,0:T(8,128)(2,1)S(1)}, bf16[128,2048]{1,0:T(8,128)(2,1)}, u32[]{:S(2)}) copy-start(bf16[128,2048]{1,0:T(8,128)(2,1)} %w_out.1) | copy-start | bytes 1572868

commit v8 on v5

--- a/solution.py
+++ b/solution.py
@@ -17,9 +17,12 @@
 FIRST = (((0,), (0,)), ((), ()))
 
 SEQ = ("x", "y")
+GRID = ("y", "x")
 CHIPS = ("row", "zhi")
 ROWS_X, ROWS_Y = 4, 8
-PIECE = BLOCK // ROWS_Y
+LANES = 128
+BLOCKS = ROWS_X * ROWS_Y
+PIECE = 2 * CHUNK // BLOCKS
 
 
 def local_call(kernel, outs, *args, scratch=(), scalars=0, plain=(), anywhere=(), last=False):
@@ -174,10 +177,13 @@
     pushed = jnp.where(columns[:, 0:1] == columns[:, 40:41], keys * jnp.exp(final - cum), 0.0)
     state = dot(values, pushed.astype(BF16), FIRST)
     keep = jnp.where(before[0:1, 0:1] == last[0:1, 0:1], jnp.exp(final), 0.0)
-    keep_rows = pair_rows(keep)
-    for j in range(ROWS_Y):
-        pieces[j, 0:PIECE, :] = state[j * PIECE : (j + 1) * PIECE, :].astype(BF16)
-        pieces[j, PIECE:, :] = keep_rows
+    for h in range(2):
+        lanes = slice(h * LANES, (h + 1) * LANES)
+        keep_rows = pair_rows(keep[:, lanes])
+        for j in range(BLOCKS // 2):
+            piece = state[j * PIECE : (j + 1) * PIECE, lanes]
+            pieces[h * BLOCKS // 2 + j, 0:PIECE, :] = piece.astype(BF16)
+            pieces[h * BLOCKS // 2 + j, PIECE:, :] = keep_rows
 
 
 def block_attention(
@@ -191,13 +197,11 @@
     cumulated,
     columns,
     own_rows,
-    totals,
     intra,
     reach,
     gate,
     extended,
 ):
-    del totals
     rows = normed[...]
     gate[...] = silu(dot(rows, w_gate[...])[0:BLOCK, :]) * head_gain[...]
     queries = conv(dot(rows, w_query[...]), taps_q, extended, columns) * HEAD_K ** (-0.5)
@@ -237,32 +241,19 @@
     intra[...] = dot(weights.astype(BF16), values[...])
 
 
-def row_scan(pieces, entering, kept, totals):
-    state = jnp.zeros((PIECE, HEAD_K), F32)
-    keep = jnp.ones((1, HEAD_K), F32)
-    for j in range(ROWS_Y):
-        entering[j] = state
-        kept[j] = jnp.broadcast_to(keep, (8, HEAD_K))
-        pair = pieces[j, PIECE:, :].astype(F32)
-        decay = pair[0:1, :] + pair[1:2, :]
-        state = state * decay + pieces[j, 0:PIECE, :].astype(F32)
-        keep = keep * decay
-    totals[0:PIECE, :] = state.astype(BF16)
-    totals[PIECE:, :] = pair_rows(keep)
-
-
-def carry(entering, kept, one_back, two_back, reach, states):
+def scan_blocks(pieces, reach, states):
     del reach
-    pair = one_back[PIECE:, :].astype(F32)
-    decay = pair[0:1, :] + pair[1:2, :]
-    arriving = one_back[0:PIECE, :].astype(F32) + decay * two_back[0:PIECE, :].astype(F32)
-    for j in range(ROWS_Y):
-        states[j] = (entering[j] + kept[j, 0:1, :] * arriving).astype(BF16)
+    state = jnp.zeros((PIECE, LANES), F32)
+    for block in range(BLOCKS):
+        at = (block % ROWS_Y) * ROWS_X + block // ROWS_Y
+        states[at] = state.astype(BF16)
+        pair = pieces[at, PIECE:, :].astype(F32)
+        state = state * (pair[0:1, :] + pair[1:2, :]) + pieces[at, 0:PIECE, :].astype(F32)
 
 
 def attend(index, intra, reach, incoming, gate, w_out, kept, kept_squares, sent):
     high, low = halves(reach[...])
-    state = incoming[...]
+    state = jnp.concatenate([incoming[0], incoming[1]], axis=1)
     attended = intra[...] + dot(high, state, LAST) + dot(low, state, LAST)
     squares = dot(jnp.ones((8, CHUNK), F32), attended * attended, LAST, precision=HIGHEST)
     terms = dot((attended * gate[...]).astype(BF16), w_out[...])
@@ -323,9 +314,8 @@
     block = lax.axis_index("x") * ROWS_Y + lax.axis_index("y")
     block_at = jnp.reshape(block, (1,)).astype(jnp.int32)
     core_at = jnp.reshape(lax.axis_index("core"), (1,)).astype(jnp.int32)
-    blocks = ROWS_X * ROWS_Y
-
-    onward = [(i, i + 1) for i in range(blocks - 1)]
+
+    onward = [(i, i + 1) for i in range(BLOCKS - 1)]
     neighbour = lax.ppermute(hidden_in, SEQ, onward)
     needed = (
         w_key,
@@ -333,7 +323,7 @@
         w_decay_down.T,
         w_decay_up,
         decay_bias.reshape(1, HEAD_K),
-        seg_ids.reshape(blocks, BLOCK),
+        seg_ids.reshape(BLOCKS, BLOCK),
         conv_key,
         conv_value,
         hidden_in,
@@ -356,7 +346,7 @@
     pieces, normed, keys, values, cumulated, columns, own_rows = local_call(
         block_state,
         [
-            ((ROWS_Y, PIECE + 8, HEAD_K), BF16),
+            ((BLOCKS, PIECE + 8, LANES), BF16),
             ((BLOCK + 8, WIDTH), BF16),
             ((BLOCK, HEAD_K), F32),
             ((BLOCK, CHUNK), BF16),
@@ -378,17 +368,7 @@
         scratch=[pltpu.VMEM((BLOCK + 8, HEAD_K), F32), pltpu.VMEM((BLOCK + 8, CHUNK), F32)],
         scalars=1,
     )
-    entering, kept, totals = local_call(
-        row_scan,
-        [
-            ((ROWS_Y, PIECE, HEAD_K), F32),
-            ((ROWS_Y, 8, HEAD_K), F32),
-            ((PIECE + 8, HEAD_K), BF16),
-        ],
-        lax.all_to_all(pieces, "y", 0, 0),
-    )
-    one_back = lax.ppermute(totals, "x", [(i, i + 1) for i in range(ROWS_X - 1)])
-    two_back = lax.ppermute(totals, "x", [(i, i + 2) for i in range(ROWS_X - 2)])
+    owned = lax.all_to_all(pieces, GRID, 0, 0)
     intra, reach, gate = local_call(
         block_attention,
         [((BLOCK, CHUNK), F32), ((BLOCK, HEAD_K), F32), ((BLOCK, CHUNK), F32)],
@@ -402,13 +382,12 @@
         cumulated,
         columns,
         own_rows,
-        totals,
         scratch=[pltpu.VMEM((BLOCK + 8, HEAD_K), F32)],
     )
     (states,) = local_call(
-        carry, [((ROWS_Y, PIECE, HEAD_K), BF16)], entering, kept, one_back, two_back, reach
-    )
-    incoming = lax.all_to_all(states, "y", 0, 0).reshape(CHUNK, HEAD_K)
+        scan_blocks, [((BLOCKS, PIECE, LANES), BF16)], owned, reach
+    )
+    incoming = lax.all_to_all(states, GRID, 0, 0).reshape(2, CHUNK, LANES)
     mine, my_squares, sent = local_call(
         attend,
         [((8, BLOCK, CHUNK), F32), ((8, BLOCK), F32), ((8 * BLOCK + 8, CHUNK), BF16)],

time: 86.7 us -> 84.8 us (0.978)
  blocking collectives: 68 us -> 54.3 us
  waiting for transfers between devices: 0.01 us -> 7.34 us
  starting transfers between devices: 10.9 us -> 15.2 us
    all_to_all x2 -> x1, blocking collectives: 25.3 us -> 12.6 us  [shards(): incoming = lax.all_to_all(states, GRID, 0, 0).reshape(2, CHUNK, LANES)]
    all_to_all x0 -> x1, starting transfers between devices: none -> 11.2 us  [shards(): owned = lax.all_to_all(pieces, GRID, 0, 0)]
    all_to_all x0 -> x1, waiting for transfers between devices: none -> 7.34 us  [shards(): owned = lax.all_to_all(pieces, GRID, 0, 0)]
    ppermute x2 -> x0, starting transfers between devices: 6.87 us -> none  [the longest x1 4.65 us: shards(): lax.ppermute(totals, 'x', [(i, i + 2) for i in range(ROWS_X - 2)])]
    all_gather x1, blocking collectives: 5.51 us -> 4.6 us  [shards(): both = lax.all_gather(sent, 'core', axis=0)]
    pallas_call x9 -> x8, Pallas kernels: 6.15 us -> 6.81 us  [local_call(): pl.pallas_call(kernel, out_shape=[jax.ShapeDtypeStruct(s, t) if last else...]
  transfers between devices with their start and end apart: 3 -> 2, of which waited for: 0 -> 1; matrix products, arithmetic and copies ran while one was open for 0% -> 0% of each run, Pallas kernels for 3% -> 3%
where the time goes in v8:
time: 84.8 us; the launch traced here: 84.4 us
  blocking collectives  54.3 us (64%)
  starting transfers between devices  15.2 us (18%)
  waiting for transfers between devices  7.34 us (9%)
  Pallas kernels  6.81 us (8%)
    all_to_all x1, blocking collectives, shards(): of_core = lax.all_to_all(copies, CHIPS, 0, 0)  19.5 us
    all_to_all x1, blocking collectives, shards(): arrived = lax.all_to_all(pairs, CHIPS, 0, 0)  12.9 us
    all_to_all x1, blocking collectives, shards(): incoming = lax.all_to_all(states, GRID, 0, 0).reshape(2, CHUNK, LANES)  12.6 us
    all_to_all x1, starting transfers between devices, shards(): owned = lax.all_to_all(pieces, GRID, 0, 0)  11.2 us
    all_to_all x1, waiting for transfers between devices, shards(): owned = lax.all_to_all(pieces, GRID, 0, 0)  7.34 us
    pallas_call x8, Pallas kernels, local_call(): pl.pallas_call(kernel, out_shape=[jax.ShapeDtypeStruct(s, t) if last else...  6.81 us
    all_gather x1, blocking collectives, shards(): whole = lax.all_gather(of_core, 'core', axis=0)  4.7 us
    all_gather x1, blocking collectives, shards(): both = lax.all_gather(sent, 'core', axis=0)  4.6 us
  transfers between devices with their start and end apart: 2, of which 1 were waited for; matrix products, arithmetic and copies ran while one was open for 0% of the time, Pallas kernels for 3%

profile of v8, /device:TPU:1, one launch (start us, length us, event | category | flops | bytes accessed | tf_op | source)
XLA Modules:
  0.0 84.4 jit_solution(950371005747153581)
XLA Ops:
  0.0 4.0 %collective-permute-start = (bf16[128,128]{1,0:T(8,128)(2,1)}, bf16[128,128]{1,0:T(8,128)(2,1)S(1)}, u32[]{:S(2)}, u32[]{:S(2)}) collective-permute-start(bf16[128,128]{1,0:T(8,128)(2,1)} %refs_8_.1), channel_id=1, source_target_pairs={{0,16},{16,32},{32,48},{48,64},{64,80},{80,96},{96,112},{112,128},... | collective-permute-start | bytes 98312 | tf_op jit(solution)/shard_map/ppermute | solution.py:319
  4.0 1.3 %fetch.1 = (bf16[2048,256]{1,0:T(8,128)(2,1)S(1)}, f32[1,2048]{1,0:T(1,128)S(1)}, bf16[16,2048]{1,0:T(8,128)(2,1)S(1)}, bf16[16,256]{1,0:T(8,128)(2,1)S(1)}, f32...) custom-call(s32[1]{0:T(128)} %bitcast.1.index, ...), custom_call_target="tpu_custom_call" | custom-call | tf_op jit(solution)/shard_map/fetch/pallas_call | solution.py:38
  5.4 0.0 collective-permute-done.neighbour
  5.4 19.5 %all_to_all.20 = bf16[8,136,128]{2,1,0:T(8,128)(2,1)S(1)} all-to-all(bf16[8,136,128]{2,1,0:T(8,128)(2,1)S(1)} %spread_out.1), channel_id=1, replica_groups=mesh['x'=4,'y'=8,'row'=4,'zhi'=2,'core'=2] {'row','zhi'}, dimensions={0} | all-to-all | bytes 557056 | tf_op jit(solution)/shard_map/all_to_all | solution.py:344
  25.0 4.7 %all-gather = bf16[16,136,128]{2,1,0:T(8,128)(2,1)S(1)} all-gather(bf16[8,136,128]{2,1,0:T(8,128)(2,1)S(1)} %all_to_all.20), channel_id=2, replica_groups=mesh['x'=4,'y'=8,'row'=4,'zhi'=2,'core'=2] {'core'}, dimensions={0}, use_global_device_ids=true | all-gather | bytes 835584 | tf_op jit(solution)/shard_map/all_gather | solution.py:345
  29.7 0.0 copy-done.2
  29.7 2.5 %block_state.1 = (bf16[32,16,128]{2,1,0:T(8,128)(2,1)}, bf16[136,2048]{1,0:T(8,128)(2,1)S(1)}, f32[128,256]{1,0:T(8,128)S(1)}, bf16[128,128]{1,0:T(8,128)(2,1)S(...) custom-call(s32[1]{0:T(128)} %bitcast.1.index, bf16[2,8,136,128]{3,2,1,0:T(8,128)(2,1)S(1)} %bitcast.10, ...), custom_call_target="tpu_custom_call" | custom-call | tf_op jit(solution)/shard_map/block_state/pallas_call | solution.py:38
  32.2 11.2 %all-to-all-start.1 = ((bf16[32,16,128]{2,1,0:T(8,128)(2,1)}), bf16[32,16,128]{2,1,0:T(8,128)(2,1)S(1)}, u32[]{:S(2)}, u32[]{:S(2)}) async-start(bf16[32,16,128]{2,1,0:T(8,128)(2,1)} %get-tuple-element.44), calls=%async_computation.1 | async-start | bytes 262144 | tf_op jit(solution)/shard_map/all_to_all | solution.py:371
  43.4 0.0 copy-start.4
  43.4 0.0 copy-start.5
  43.4 0.0 copy-done
  43.4 0.0 copy-done.3
  43.4 0.6 copy-done.4
  44.1 0.0 copy-done.5
  44.1 1.3 %block_attention.1 = (f32[128,128]{1,0:T(8,128)S(1)}, f32[128,256]{1,0:T(8,128)S(1)}, f32[128,128]{1,0:T(8,128)S(1)}) custom-call(bf16[136,2048]{1,0:T(8,128)(2,1)S(1)} %get-tuple-element.36.normed, bf16[2048,256]{1,0:T(8,128)(2,1)S(1)} %copy-done, bf16[2048,128]{1,0:T(8,128)(2,1)S(1)} %copy-done.3, f32[4,256]{1,0:T(4,128)S(1)} %copy-done.4, ...), custom_call_target="tpu_custom_call" | custom-call | tf_op jit(solution)/shard_map/block_attention/pallas_call | solution.py:38
  45.4 7.3 %all-to-all-done.1.pieces = bf16[32,16,128]{2,1,0:T(8,128)(2,1)S(1)} async-done(((bf16[32,16,128]{2,1,0:T(8,128)(2,1)}), bf16[32,16,128]{2,1,0:T(8,128)(2,1)S(1)}, u32[]{:S(2)}, u32[]{:S(2)}) %all-to-all-start.1) | async-done | bytes 131104 | tf_op jit(solution)/shard_map/all_to_all | solution.py:371
  52.7 0.1 scan_blocks.1
  52.8 12.6 %all_to_all.21 = bf16[32,8,128]{2,1,0:T(8,128)(2,1)S(1)} all-to-all(bf16[32,8,128]{2,1,0:T(8,128)(2,1)S(1)} %scan_blocks.1), channel_id=1, replica_groups=mesh['x'=4,'y'=8,'row'=4,'zhi'=2,'core'=2] {'y','x'}, dimensions={0} | all-to-all | bytes 131072 | tf_op jit(solution)/shard_map/all_to_all | solution.py:390
  65.4 0.0 copy-done.1
  65.4 0.6 attend.1
  66.0 4.6 %all-gather.1 = bf16[2064,128]{1,0:T(8,128)(2,1)S(1)} all-gather(bf16[1032,128]{1,0:T(8,128)(2,1)S(1)} %get-tuple-element.48), channel_id=3, replica_groups=mesh['x'=4,'y'=8,'row'=4,'zhi'=2,'core'=2] {'core'}, dimensions={0}, use_global_device_ids=true | all-gather | bytes 792576 | tf_op jit(solution)/shard_map/all_gather | solution.py:402
  70.6 0.1 pair_sum.1
  70.6 12.9 %all_to_all.22.received = bf16[8,136,128]{2,1,0:T(8,128)(2,1)S(1)} all-to-all(bf16[8,136,128]{2,1,0:T(8,128)(2,1)S(1)} %pair_sum.1), channel_id=1, replica_groups=mesh['x'=4,'y'=8,'row'=4,'zhi'=2,'core'=2] {'row','zhi'}, dimensions={0} | all-to-all | bytes 557056 | tf_op jit(solution)/shard_map/all_to_all | solution.py:406
  83.5 0.9 %finish.1 = bf16[128,128]{1,0:T(8,128)(2,1)} custom-call(bf16[8,136,128]{2,1,0:T(8,128)(2,1)S(1)} %all_to_all.22.received, bf16[128,128]{1,0:T(8,128)(2,1)S(1)} %get-tuple-element.27.hidden), custom_call_target="tpu_custom_call" | custom-call | tf_op jit(solution)/shard_map/finish/pallas_call | solution.py:38
  (5 shorter events, 0.0 us)
Async XLA Ops:
  0.0 5.4 %collective-permute-start = (bf16[128,128]{1,0:T(8,128)(2,1)}, bf16[128,128]{1,0:T(8,128)(2,1)S(1)}, u32[]{:S(2)}, u32[]{:S(2)}) collective-permute-start(bf16[128,128]{1,0:T(8,128)(2,1)} %refs_8_.1), channel_id=1, source_target_pairs={{0,16},{16,32},{32,48},{48,64},{64,80},{80,96},{96,112},{112,128},... | collective-permute-start | bytes 98312 | tf_op jit(solution)/shard_map/ppermute | solution.py:319
  24.9 4.7 %copy-start.2 = (bf16[2048,128]{1,0:T(8,128)(2,1)S(1)}, bf16[2048,128]{1,0:T(8,128)(2,1)}, u32[]{:S(2)}) copy-start(bf16[2048,128]{1,0:T(8,128)(2,1)} %w_value.1) | copy-start | bytes 1572868
  29.7 13.7 %copy-start = (bf16[2048,256]{1,0:T(8,128)(2,1)S(1)}, bf16[2048,256]{1,0:T(8,128)(2,1)}, u32[]{:S(2)}) copy-start(bf16[2048,256]{1,0:T(8,128)(2,1)} %w_query.1) | copy-start | bytes 3145732
  29.7 13.7 %copy-start.3 = (bf16[2048,128]{1,0:T(8,128)(2,1)S(1)}, bf16[2048,128]{1,0:T(8,128)(2,1)}, u32[]{:S(2)}) copy-start(bf16[2048,128]{1,0:T(8,128)(2,1)} %w_gate.1) | copy-start | bytes 1572868
  32.2 20.5 %all-to-all-start.1 = ((bf16[32,16,128]{2,1,0:T(8,128)(2,1)}), bf16[32,16,128]{2,1,0:T(8,128)(2,1)S(1)}, u32[]{:S(2)}, u32[]{:S(2)}) async-start(bf16[32,16,128]{2,1,0:T(8,128)(2,1)} %get-tuple-element.44), calls=%async_computation.1 | async-start | bytes 262144 | tf_op jit(solution)/shard_map/all_to_all | solution.py:371
  43.4 0.7 copy-start.4
  43.4 0.7 copy-start.5
  44.1 21.3 %copy-start.1 = (bf16[128,2048]{1,0:T(8,128)(2,1)S(1)}, bf16[128,2048]{1,0:T(8,128)(2,1)}, u32[]{:S(2)}) copy-start(bf16[128,2048]{1,0:T(8,128)(2,1)} %w_out.1) | copy-start | bytes 1572868

commit v9 on v8

--- a/solution.py
+++ b/solution.py
@@ -74,38 +74,54 @@
     return value * jax.nn.sigmoid(value)
 
 
-def fetch(index, core, *refs):
+def fetch_and_spread(index, core, *refs):
     del index, core
-    count = (len(refs) - 1) // 2
-    arrived = refs[-1]
-    copies = [
+    *refs, copies, arrived = refs
+    count = len(refs) // 2
+    fetches = [
         pltpu.make_async_copy(refs[i], refs[count + i], arrived.at[i]) for i in range(count)
     ]
-    for copy in copies:
-        copy.start()
-    for copy in copies:
-        copy.wait()
-
-
-def spread_out(hidden, neighbour, w_key, copies):
-    del w_key
-    edge = neighbour[BLOCK - 8 :, :]
+    for fetch in fetches:
+        fetch.start()
+    fetches[0].wait()
     for j in range(8):
-        copies[j, 0:BLOCK, :] = hidden[...]
-        copies[j, BLOCK:, :] = edge
-
-
-def conv(pre, taps, extended, columns):
-    extended[0:8, :] = pre[BLOCK:, :]
-    extended[8:, :] = pre[0:BLOCK, :]
+        copies[j] = refs[count][...]
+    for fetch in fetches[1:]:
+        fetch.wait()
+
+
+def conv(pre, edge, taps, extended, columns):
+    extended[0:8, :] = jnp.zeros((8, pre.shape[1]), F32) if edge is None else edge
+    extended[8:, :] = pre
     seg = columns[:, 0:1]
-    total = taps[0:1, :] * pre[0:BLOCK, :]
+    total = taps[0:1, :] * pre
     for j in range(1, 4):
         same = columns[:, 8 * j : 8 * j + 1] == seg
         total = total + jnp.where(
             same, taps[j : j + 1, :] * extended[8 - j : 8 - j + BLOCK, :], 0.0
         )
-    return silu(total)
+    return total
+
+
+def onward(pre, taps, own, following):
+    sums = []
+    for t in range(3):
+        total = jnp.zeros((1, pre.shape[1]), F32)
+        for j in range(t + 1, 4):
+            at = BLOCK + t - j
+            same = following[0:1, t : t + 1] == own[0:1, at : at + 1]
+            total = total + jnp.where(same, taps[j : j + 1, :] * pre[at : at + 1, :], 0.0)
+        sums.append(total)
+    return sums
+
+
+def stacked_rows(rows):
+    shape = (8, LANES)
+    index = lax.broadcasted_iota(jnp.int32, shape, 0)
+    out = jnp.zeros(shape, F32)
+    for at, row in rows.items():
+        out = jnp.where(index == at, jnp.broadcast_to(row, shape), out)
+    return out.astype(BF16)
 
 
 def block_state(
@@ -122,8 +138,8 @@
     taps_v,
     pieces,
     normed,
-    keys_out,
-    values_out,
+    pre_k,
+    pre_v,
     cumulated,
     columns_out,
     own_rows,
@@ -131,7 +147,7 @@
     extended_v,
 ):
     chunks = WIDTH // CHUNK
-    squares = jnp.zeros((BLOCK + 8, CHUNK), F32)
+    squares = jnp.zeros((BLOCK, CHUNK), F32)
     for f in range(chunks):
         activ = whole[f % 2, f // 2].astype(F32)
         squares = squares + activ * activ
@@ -141,12 +157,13 @@
         activ = whole[f % 2, f // 2].astype(F32)
         normed[:, lanes] = (activ * scale * gain[:, lanes]).astype(BF16)
     rows = normed[...]
-    rank_part = dot(rows, w_down[...], LAST)[0:BLOCK, :]
+    rank_part = dot(rows, w_down[...], LAST)
 
     at = index[0]
     own = seg_ids[pl.ds(at, 1), :].astype(F32)
     before = seg_ids[pl.ds(jnp.maximum(at - 1, 0), 1), :].astype(F32)
     before = jnp.where(at > 0, before, -1.0)
+    following = seg_ids[pl.ds(jnp.minimum(at + 1, BLOCKS - 1), 1), :].astype(F32)
     own = jnp.broadcast_to(own, (8, BLOCK))
     before = jnp.broadcast_to(before, (8, BLOCK))
     lane = lax.broadcasted_iota(jnp.int32, (8, BLOCK), 1)
@@ -169,43 +186,84 @@
     cum = dot(lower, log_decay, precision=HIGHEST)
     cumulated[...] = cum
 
-    keys = conv(dot(rows, w_key[...]), taps_k, extended_k, columns)
-    values = conv(dot(rows, w_value[...]), taps_v, extended_v, columns).astype(BF16)
-    keys_out[...] = keys
-    values_out[...] = values
+    of_keys = dot(rows, w_key[...])
+    of_values = dot(rows, w_value[...])
+    pre_k[...] = of_keys
+    pre_v[...] = of_values
+    sums_k = conv(of_keys, None, taps_k, extended_k, columns)
+    sums_v = conv(of_values, None, taps_v, extended_v, columns)
+    next_k = onward(of_keys, taps_k, own, following)
+    next_v = onward(of_values, taps_v, own, following)
     final = cum[BLOCK - 1 :, :]
-    pushed = jnp.where(columns[:, 0:1] == columns[:, 40:41], keys * jnp.exp(final - cum), 0.0)
-    state = dot(values, pushed.astype(BF16), FIRST)
+    factors = jnp.where(columns[:, 0:1] == columns[:, 40:41], jnp.exp(final - cum), 0.0)
+    later = lax.broadcasted_iota(jnp.int32, (BLOCK, HEAD_K), 0) >= 3
+    pushed = jnp.where(later, silu(sums_k) * factors, 0.0)
+    state = dot(silu(sums_v).astype(BF16), pushed.astype(BF16), FIRST)
     keep = jnp.where(before[0:1, 0:1] == last[0:1, 0:1], jnp.exp(final), 0.0)
+    high, low = halves(keep)
+    lane = lax.broadcasted_iota(jnp.int32, (1, LANES), 1)
+    mixed_v = []
+    for upper in range(2):
+        mine = (lane >= LANES // 2) == (upper == 1)
+        mixed_v.append(
+            [
+                jnp.where(mine, sums_v[t : t + 1, :], pltpu.roll(next_v[t], LANES // 2, 1))
+                for t in range(3)
+            ]
+        )
     for h in range(2):
         lanes = slice(h * LANES, (h + 1) * LANES)
-        keep_rows = pair_rows(keep[:, lanes])
-        for j in range(BLOCKS // 2):
-            piece = state[j * PIECE : (j + 1) * PIECE, lanes]
-            pieces[h * BLOCKS // 2 + j, 0:PIECE, :] = piece.astype(BF16)
-            pieces[h * BLOCKS // 2 + j, PIECE:, :] = keep_rows
+        rows_b = {0: high.astype(F32)[:, lanes], 1: low.astype(F32)[:, lanes]}
+        for t in range(3):
+            rows_b[2 + t] = sums_k[t : t + 1, lanes]
+            rows_b[5 + t] = next_k[t][:, lanes]
+        tile_b = stacked_rows(rows_b)
+        for upper in range(2):
+            rows_c = {2 + t: factors[t : t + 1, lanes] for t in range(3)}
+            rows_c.update({5 + t: mixed_v[upper][t] for t in range(3)})
+            tile_c = stacked_rows(rows_c)
+            for j in range(8):
+                g = 8 * upper + j
+                p = h * BLOCKS // 2 + g
+                pieces[p, 0:PIECE, :] = state[g * PIECE : (g + 1) * PIECE, lanes].astype(BF16)
+                pieces[p, PIECE : PIECE + 8, :] = tile_b
+                pieces[p, PIECE + 8 :, :] = tile_c
+
+
+def queries_gate(normed, w_query, w_gate, head_gain, pre_k, pre_v, pre_q, gate, tail):
+    rows = normed[...]
+    gate[...] = silu(dot(rows, w_gate[...])) * head_gain[...]
+    of_queries = dot(rows, w_query[...])
+    pre_q[...] = of_queries
+    tail[:, :HEAD_K] = of_queries[BLOCK - 8 :, :]
+    tail[:, HEAD_K : 2 * HEAD_K] = pre_k[BLOCK - 8 :, :]
+    tail[:, 2 * HEAD_K :] = pre_v[BLOCK - 8 :, :]
 
 
 def block_attention(
-    normed,
-    w_query,
-    w_gate,
+    pre_q,
+    pre_k,
+    pre_v,
+    edge,
     taps_q,
-    head_gain,
-    keys_in,
-    values,
+    taps_k,
+    taps_v,
     cumulated,
     columns,
     own_rows,
     intra,
     reach,
-    gate,
     extended,
+    extended_v,
 ):
-    rows = normed[...]
-    gate[...] = silu(dot(rows, w_gate[...])[0:BLOCK, :]) * head_gain[...]
-    queries = conv(dot(rows, w_query[...]), taps_q, extended, columns) * HEAD_K ** (-0.5)
-    keys, cum, seg = keys_in[...], cumulated[...], columns[:, 0:1]
+    edges = edge[...]
+    queries = silu(conv(pre_q[...], edges[:, :HEAD_K], taps_q, extended.at[0], columns))
+    queries = queries * HEAD_K ** (-0.5)
+    keys = silu(
+        conv(pre_k[...], edges[:, HEAD_K : 2 * HEAD_K], taps_k, extended.at[1], columns)
+    )
+    values = silu(conv(pre_v[...], edges[:, 2 * HEAD_K :], taps_v, extended_v, columns))
+    cum, seg = cumulated[...], columns[:, 0:1]
     row_iota = lax.broadcasted_iota(jnp.int32, (BLOCK, BLOCK), 0)
     col_iota = lax.broadcasted_iota(jnp.int32, (BLOCK, BLOCK), 1)
     reach[...] = jnp.where(seg == columns[:, 32:33], queries * jnp.exp(cum), 0.0)
@@ -238,17 +296,32 @@
         weights = jnp.where(inside, sums, weights)
     visible = (seg == own_rows[0:1, :]) & (row_iota >= col_iota)
     weights = jnp.where(visible, weights, 0.0)
-    intra[...] = dot(weights.astype(BF16), values[...])
-
-
-def scan_blocks(pieces, reach, states):
+    intra[...] = dot(weights.astype(BF16), values.astype(BF16))
+
+
+def scan_blocks(index, pieces, reach, states):
     del reach
-    state = jnp.zeros((PIECE, LANES), F32)
+    owner = (index[0] % ROWS_Y) * ROWS_X + index[0] // ROWS_Y
+    first = (owner % (BLOCKS // 2)) * PIECE
+    shape = (PIECE, LANES)
+    lane = lax.broadcasted_iota(jnp.int32, shape, 1)
+    chosen = lane == lax.broadcasted_iota(jnp.int32, shape, 0) + first
+    state = jnp.zeros(shape, F32)
+    back_b = back_c = jnp.zeros((8, LANES), F32)
     for block in range(BLOCKS):
         at = (block % ROWS_Y) * ROWS_X + block // ROWS_Y
         states[at] = state.astype(BF16)
-        pair = pieces[at, PIECE:, :].astype(F32)
-        state = state * (pair[0:1, :] + pair[1:2, :]) + pieces[at, 0:PIECE, :].astype(F32)
+        tile_b = pieces[at, PIECE : PIECE + 8, :].astype(F32)
+        tile_c = pieces[at, PIECE + 8 :, :].astype(F32)
+        pushed = silu(tile_b + pltpu.roll(back_b, 5, 0)) * tile_c
+        values = silu(tile_c + pltpu.roll(back_c, LANES // 2, 1))
+        added = pieces[at, 0:PIECE, :].astype(F32)
+        for t in range(3):
+            row = jnp.broadcast_to(values[5 + t : 6 + t, :], shape)
+            column = jnp.sum(jnp.where(chosen, row, 0.0), axis=1, keepdims=True)
+            added = added + column * pushed[2 + t : 3 + t, :]
+        state = state * (tile_b[0:1, :] + tile_b[1:2, :]) + added
+        back_b, back_c = tile_b, tile_c
 
 
 def attend(index, intra, reach, incoming, gate, w_out, kept, kept_squares, sent):
@@ -315,22 +388,21 @@
     block_at = jnp.reshape(block, (1,)).astype(jnp.int32)
     core_at = jnp.reshape(lax.axis_index("core"), (1,)).astype(jnp.int32)
 
-    onward = [(i, i + 1) for i in range(BLOCKS - 1)]
-    neighbour = lax.ppermute(hidden_in, SEQ, onward)
     needed = (
-        w_key,
+        hidden_in,
         norm_gain.reshape(1, WIDTH),
         w_decay_down.T,
         w_decay_up,
         decay_bias.reshape(1, HEAD_K),
         seg_ids.reshape(BLOCKS, BLOCK),
+        conv_query,
         conv_key,
         conv_value,
-        hidden_in,
-    )
-    key_here, gain, down, up, bias, segs, taps_k, taps_v, hidden = local_call(
-        fetch,
-        [(a.shape, a.dtype) for a in needed],
+        head_gain.reshape(1, CHUNK),
+    )
+    hidden, gain, down, up, bias, segs, taps_q, taps_k, taps_v, out_gain, copies = local_call(
+        fetch_and_spread,
+        [*((a.shape, a.dtype) for a in needed), ((8, BLOCK, CHUNK), BF16)],
         block_at,
         core_at,
         *needed,
@@ -338,18 +410,15 @@
         scalars=2,
         anywhere=range(2, 2 + len(needed)),
     )
-    (copies,) = local_call(
-        spread_out, [((8, BLOCK + 8, CHUNK), BF16)], hidden, neighbour, key_here
-    )
     of_core = lax.all_to_all(copies, CHIPS, 0, 0)
     whole = lax.all_gather(of_core, "core", axis=0)
-    pieces, normed, keys, values, cumulated, columns, own_rows = local_call(
+    pieces, normed, pre_k, pre_v, cumulated, columns, own_rows = local_call(
         block_state,
         [
-            ((BLOCKS, PIECE + 8, LANES), BF16),
-            ((BLOCK + 8, WIDTH), BF16),
+            ((BLOCKS, PIECE + 16, LANES), BF16),
+            ((BLOCK, WIDTH), BF16),
             ((BLOCK, HEAD_K), F32),
-            ((BLOCK, CHUNK), BF16),
+            ((BLOCK, CHUNK), F32),
             ((BLOCK, HEAD_K), F32),
             ((BLOCK, BLOCK), F32),
             ((8, BLOCK), F32),
@@ -357,7 +426,7 @@
         block_at,
         whole,
         gain,
-        key_here,
+        w_key,
         w_value,
         down,
         up,
@@ -369,23 +438,42 @@
         scalars=1,
     )
     owned = lax.all_to_all(pieces, GRID, 0, 0)
-    intra, reach, gate = local_call(
-        block_attention,
-        [((BLOCK, CHUNK), F32), ((BLOCK, HEAD_K), F32), ((BLOCK, CHUNK), F32)],
+    pre_q, gate, tail = local_call(
+        queries_gate,
+        [((BLOCK, HEAD_K), F32), ((BLOCK, CHUNK), F32), ((8, 2 * HEAD_K + CHUNK), F32)],
         normed,
         w_query,
         w_gate,
-        conv_query,
-        head_gain.reshape(1, CHUNK),
-        keys,
-        values,
+        out_gain,
+        pre_k,
+        pre_v,
+    )
+    edge = lax.ppermute(tail, SEQ, [(i, i + 1) for i in range(BLOCKS - 1)])
+    intra, reach = local_call(
+        block_attention,
+        [((BLOCK, CHUNK), F32), ((BLOCK, HEAD_K), F32)],
+        pre_q,
+        pre_k,
+        pre_v,
+        edge,
+        taps_q,
+        taps_k,
+        taps_v,
         cumulated,
         columns,
         own_rows,
-        scratch=[pltpu.VMEM((BLOCK + 8, HEAD_K), F32)],
+        scratch=[
+            pltpu.VMEM((2, BLOCK + 8, HEAD_K), F32),
+            pltpu.VMEM((BLOCK + 8, CHUNK), F32),
+        ],
     )
     (states,) = local_call(
-        scan_blocks, [((BLOCKS, PIECE, LANES), BF16)], owned, reach
+        scan_blocks,
+        [((BLOCKS, PIECE, LANES), BF16)],
+        block_at,
+        owned,
+        reach,
+        scalars=1,
     )
     incoming = lax.all_to_all(states, GRID, 0, 0).reshape(2, CHUNK, LANES)
     mine, my_squares, sent = local_call(

time: 84.8 us -> 85.9 us (1.013)
  blocking collectives: 54.3 us -> 57.5 us
  starting transfers between devices: 15.2 us -> 12.8 us
  waiting for transfers between devices: 7.34 us -> 4.96 us
  local copies, waits for them, and re-layouts: 0.67 us -> 2.21 us
  Pallas kernels: 6.81 us -> 7.86 us
    all_to_all x1, waiting for transfers between devices: 7.34 us -> 4.07 us  [shards(): owned = lax.all_to_all(pieces, GRID, 0, 0)]
    all_to_all x1, blocking collectives: 12.6 us -> 15.5 us  [shards(): incoming = lax.all_to_all(states, GRID, 0, 0).reshape(2, CHUNK, LANES)]
    all_to_all x1, blocking collectives: 19.5 us -> 17.8 us  [shards(): of_core = lax.all_to_all(copies, CHIPS, 0, 0)]
    all_to_all x1, blocking collectives: 12.9 us -> 14.5 us  [shards(): arrived = lax.all_to_all(pairs, CHIPS, 0, 0)]
    unnamed x12 -> x18, local copies, waits for them, and re-layouts: 0.67 us -> 2.21 us
    all_to_all x1, starting transfers between devices: 11.2 us -> 9.67 us  [shards(): owned = lax.all_to_all(pieces, GRID, 0, 0)]
    pallas_call x8, Pallas kernels: 6.81 us -> 7.86 us  [local_call(): pl.pallas_call(kernel, out_shape=[jax.ShapeDtypeStruct(s, t) if last else...]
    ppermute x1, waiting for transfers between devices: 0.01 us -> 0.89 us  [shards(): edge = lax.ppermute(tail, SEQ, [(i, i + 1) for i in range(BLOCKS - 1)])]
  transfers between devices with their start and end apart: 2 -> 2, of which waited for: 1 -> 2; matrix products, arithmetic and copies ran while one was open for 0% -> 0% of each run, Pallas kernels for 3% -> 2%
where the time goes in v9:
time: 85.9 us; the launch traced here: 85.5 us
  blocking collectives  57.5 us (67%)
  starting transfers between devices  12.8 us (15%)
  Pallas kernels  7.86 us (9%)
  waiting for transfers between devices  4.96 us (6%)
  local copies, waits for them, and re-layouts  2.21 us (3%)
    all_to_all x1, blocking collectives, shards(): of_core = lax.all_to_all(copies, CHIPS, 0, 0)  17.8 us
    all_to_all x1, blocking collectives, shards(): incoming = lax.all_to_all(states, GRID, 0, 0).reshape(2, CHUNK, LANES)  15.5 us
    all_to_all x1, blocking collectives, shards(): arrived = lax.all_to_all(pairs, CHIPS, 0, 0)  14.5 us
    all_to_all x1, starting transfers between devices, shards(): owned = lax.all_to_all(pieces, GRID, 0, 0)  9.67 us
    pallas_call x8, Pallas kernels, local_call(): pl.pallas_call(kernel, out_shape=[jax.ShapeDtypeStruct(s, t) if last else...  7.86 us
    all_gather x1, blocking collectives, shards(): both = lax.all_gather(sent, 'core', axis=0)  5.3 us
    all_gather x1, blocking collectives, shards(): whole = lax.all_gather(of_core, 'core', axis=0)  4.46 us
    all_to_all x1, waiting for transfers between devices, shards(): owned = lax.all_to_all(pieces, GRID, 0, 0)  4.07 us
  transfers between devices with their start and end apart: 2, of which 2 were waited for; matrix products, arithmetic and copies ran while one was open for 0% of the time, Pallas kernels for 2%

profile of v9, /device:TPU:1, one launch (start us, length us, event | category | flops | bytes accessed | tf_op | source)
XLA Modules:
  0.0 85.5 jit_solution(17108730947914759742)
XLA Ops:
  0.0 1.1 %fetch_and_spread.1 = (bf16[128,128]{1,0:T(8,128)(2,1)S(1)}, f32[1,2048]{1,0:T(1,128)S(1)}, bf16[16,2048]{1,0:T(8,128)(2,1)S(1)}, bf16[16,256]{1,0:T(8,128)(2,1)...) custom-call(s32[1]{0:T(128)} %bitcast.1.index, ...), custom_call_target="tpu_custom_call" | custom-call | tf_op jit(solution)/shard_map/fetch_and_spread/pallas_call | solution.py:38
  1.1 0.0 copy-start.7
  1.1 0.5 copy-done.7
  1.6 17.8 %all_to_all.20 = bf16[8,128,128]{2,1,0:T(8,128)(2,1)S(1)} all-to-all(bf16[8,128,128]{2,1,0:T(8,128)(2,1)S(1)} %get-tuple-element.31), channel_id=1, replica_groups=mesh['x'=4,'y'=8,'row'=4,'zhi'=2,'core'=2] {'row','zhi'}, dimensions={0} | all-to-all | bytes 524288 | tf_op jit(solution)/shard_map/all_to_all | solution.py:413
  19.4 0.0 copy-done.5
  19.4 4.5 %all-gather = bf16[16,128,128]{2,1,0:T(8,128)(2,1)S(1)} all-gather(bf16[8,128,128]{2,1,0:T(8,128)(2,1)S(1)} %all_to_all.20), channel_id=2, replica_groups=mesh['x'=4,'y'=8,'row'=4,'zhi'=2,'core'=2] {'core'}, dimensions={0}, use_global_device_ids=true | all-gather | bytes 786432 | tf_op jit(solution)/shard_map/all_gather | solution.py:414
  23.9 0.0 copy-done.1
  23.9 1.0 %copy-done.4 = bf16[2048,128]{1,0:T(8,128)(2,1)S(1)} copy-done((bf16[2048,128]{1,0:T(8,128)(2,1)S(1)}, bf16[2048,128]{1,0:T(8,128)(2,1)}, u32[]{:S(2)}) %copy-start.4) | copy-done | bytes 524312
  24.9 2.4 %block_state.1 = (bf16[32,24,128]{2,1,0:T(8,128)(2,1)}, bf16[128,2048]{1,0:T(8,128)(2,1)S(1)}, f32[128,256]{1,0:T(8,128)S(1)}, f32[128,128]{1,0:T(8,128)S(1)}, f...) custom-call(s32[1]{0:T(128)} %bitcast.1.index, bf16[2,8,128,128]{3,2,1,0:T(8,128)(2,1)S(1)} %bitcast.11, ...), custom_call_target="tpu_custom_call" | custom-call | tf_op jit(solution)/shard_map/block_state/pallas_call | solution.py:38
  27.3 9.7 %all-to-all-start.1 = ((bf16[32,24,128]{2,1,0:T(8,128)(2,1)}), bf16[32,24,128]{2,1,0:T(8,128)(2,1)S(1)}, u32[]{:S(2)}, u32[]{:S(2)}) async-start(bf16[32,24,128]{2,1,0:T(8,128)(2,1)} %get-tuple-element.51), calls=%async_computation.1 | async-start | bytes 393216 | tf_op jit(solution)/shard_map/all_to_all | solution.py:440
  37.0 0.6 copy-done.8
  37.6 0.4 queries_gate.1
  38.0 3.1 %collective-permute-start = (f32[8,640]{1,0:T(8,128)S(1)}, f32[8,640]{1,0:T(8,128)S(1)}, u32[]{:S(2)}, u32[]{:S(2)}) collective-permute-start(f32[8,640]{1,0:T(8,128)S(1)} %get-tuple-element.44), channel_id=1, source_target_pairs={{0,16},{16,32},{32,48},{48,64},{64,80},{80,96},{96,112},{112,128},... | collective-permute-start | bytes 61448 | tf_op jit(solution)/shard_map/ppermute | solution.py:451
  41.2 0.9 %collective-permute-done.edge = f32[8,640]{1,0:T(8,128)S(1)} collective-permute-done((f32[8,640]{1,0:T(8,128)S(1)}, f32[8,640]{1,0:T(8,128)S(1)}, u32[]{:S(2)}, u32[]{:S(2)}) %collective-permute-start) | collective-permute-done | bytes 20512 | tf_op jit(solution)/shard_map/ppermute | solution.py:451
  42.1 1.4 %block_attention.1 = (f32[128,128]{1,0:T(8,128)S(1)}, f32[128,256]{1,0:T(8,128)S(1)}) custom-call(f32[128,256]{1,0:T(8,128)S(1)} %get-tuple-element.43.pre_q, f32[128,256]{1,0:T(8,128)S(1)} %get-tuple-element.41.pre_k, f32[128,128]{1,0:T(8,128)S(1)} %get-tuple-element.42.pre_v, f32[8,640]{1,0:T(8,128)S(1)} %collective-permute-done.edge, ...), custom_call_target="tpu_custom_call" | custom-call | tf_op jit(solution)/shard_map/block_attention/pallas_call | solution.py:38
  43.5 4.1 %all-to-all-done.1.pieces = bf16[32,24,128]{2,1,0:T(8,128)(2,1)S(1)} async-done(((bf16[32,24,128]{2,1,0:T(8,128)(2,1)}), bf16[32,24,128]{2,1,0:T(8,128)(2,1)S(1)}, u32[]{:S(2)}, u32[]{:S(2)}) %all-to-all-start.1) | async-done | bytes 196640 | tf_op jit(solution)/shard_map/all_to_all | solution.py:440
  47.5 1.1 %scan_blocks.1 = bf16[32,8,128]{2,1,0:T(8,128)(2,1)S(1)} custom-call(s32[1]{0:T(128)} %bitcast.1.index, bf16[32,24,128]{2,1,0:T(8,128)(2,1)S(1)} %all-to-all-done.1.pieces, f32[128,256]{1,0:T(8,128)S(1)} %get-tuple-element.50.reach), custom_call_target="tpu_custom_call" | custom-call | tf_op jit(solution)/shard_map/scan_blocks/pallas_call | solution.py:38
  48.6 15.5 %all_to_all.21 = bf16[32,8,128]{2,1,0:T(8,128)(2,1)S(1)} all-to-all(bf16[32,8,128]{2,1,0:T(8,128)(2,1)S(1)} %scan_blocks.1), channel_id=1, replica_groups=mesh['x'=4,'y'=8,'row'=4,'zhi'=2,'core'=2] {'y','x'}, dimensions={0} | all-to-all | bytes 131072 | tf_op jit(solution)/shard_map/all_to_all | solution.py:478
  64.1 0.6 attend.1
  64.7 5.3 %all-gather.1 = bf16[2064,128]{1,0:T(8,128)(2,1)S(1)} all-gather(bf16[1032,128]{1,0:T(8,128)(2,1)S(1)} %get-tuple-element.55), channel_id=3, replica_groups=mesh['x'=4,'y'=8,'row'=4,'zhi'=2,'core'=2] {'core'}, dimensions={0}, use_global_device_ids=true | all-gather | bytes 792576 | tf_op jit(solution)/shard_map/all_gather | solution.py:490
  70.0 0.1 pair_sum.1
  70.1 0.0 copy-start.6
  70.1 14.5 %all_to_all.22.received = bf16[8,136,128]{2,1,0:T(8,128)(2,1)S(1)} all-to-all(bf16[8,136,128]{2,1,0:T(8,128)(2,1)S(1)} %pair_sum.1), channel_id=1, replica_groups=mesh['x'=4,'y'=8,'row'=4,'zhi'=2,'core'=2] {'row','zhi'}, dimensions={0} | all-to-all | bytes 557056 | tf_op jit(solution)/shard_map/all_to_all | solution.py:494
  84.6 0.9 %finish.1 = bf16[128,128]{1,0:T(8,128)(2,1)} custom-call(bf16[8,136,128]{2,1,0:T(8,128)(2,1)S(1)} %all_to_all.22.received, bf16[128,128]{1,0:T(8,128)(2,1)S(1)} %copy-done.6), custom_call_target="tpu_custom_call" | custom-call | tf_op jit(solution)/shard_map/finish/pallas_call | solution.py:38
  (11 shorter events, 0.0 us)
Async XLA Ops:
  0.0 23.9 %copy-start.1 = (bf16[2048,256]{1,0:T(8,128)(2,1)S(1)}, bf16[2048,256]{1,0:T(8,128)(2,1)}, u32[]{:S(2)}) copy-start(bf16[2048,256]{1,0:T(8,128)(2,1)} %w_key.1) | copy-start | bytes 3145732
  1.1 0.5 copy-start.7
  1.6 17.8 %copy-start.5 = (bf16[128,128]{1,0:T(8,128)(2,1)}, bf16[128,128]{1,0:T(8,128)(2,1)S(1)}, u32[]{:S(2)}) copy-start(bf16[128,128]{1,0:T(8,128)(2,1)S(1)} %get-tuple-element.56.hidden) | copy-start | bytes 98308
  23.9 1.0 %copy-start.4 = (bf16[2048,128]{1,0:T(8,128)(2,1)S(1)}, bf16[2048,128]{1,0:T(8,128)(2,1)}, u32[]{:S(2)}) copy-start(bf16[2048,128]{1,0:T(8,128)(2,1)} %w_value.1) | copy-start | bytes 1572868
  24.9 12.1 %copy-start = (bf16[2048,256]{1,0:T(8,128)(2,1)S(1)}, bf16[2048,256]{1,0:T(8,128)(2,1)}, u32[]{:S(2)}) copy-start(bf16[2048,256]{1,0:T(8,128)(2,1)} %w_query.1) | copy-start | bytes 3145732
  24.9 12.1 %copy-start.2 = (bf16[2048,128]{1,0:T(8,128)(2,1)S(1)}, bf16[2048,128]{1,0:T(8,128)(2,1)}, u32[]{:S(2)}) copy-start(bf16[2048,128]{1,0:T(8,128)(2,1)} %w_gate.1) | copy-start | bytes 1572868
  27.3 20.3 %all-to-all-start.1 = ((bf16[32,24,128]{2,1,0:T(8,128)(2,1)}), bf16[32,24,128]{2,1,0:T(8,128)(2,1)S(1)}, u32[]{:S(2)}, u32[]{:S(2)}) async-start(bf16[32,24,128]{2,1,0:T(8,128)(2,1)} %get-tuple-element.51), calls=%async_computation.1 | async-start | bytes 393216 | tf_op jit(solution)/shard_map/all_to_all | solution.py:440
  37.0 0.6 copy-start.8
  38.0 4.0 %collective-permute-start = (f32[8,640]{1,0:T(8,128)S(1)}, f32[8,640]{1,0:T(8,128)S(1)}, u32[]{:S(2)}, u32[]{:S(2)}) collective-permute-start(f32[8,640]{1,0:T(8,128)S(1)} %get-tuple-element.44), channel_id=1, source_target_pairs={{0,16},{16,32},{32,48},{48,64},{64,80},{80,96},{96,112},{112,128},... | collective-permute-start | bytes 61448 | tf_op jit(solution)/shard_map/ppermute | solution.py:451
  42.1 22.0 %copy-start.3 = (bf16[128,2048]{1,0:T(8,128)(2,1)S(1)}, bf16[128,2048]{1,0:T(8,128)(2,1)}, u32[]{:S(2)}) copy-start(bf16[128,2048]{1,0:T(8,128)(2,1)} %w_out.1) | copy-start | bytes 1572868
  70.1 14.5 %copy-start.6 = (bf16[128,128]{1,0:T(8,128)(2,1)S(1)}, bf16[128,128]{1,0:T(8,128)(2,1)}, u32[]{:S(2)}) copy-start(bf16[128,128]{1,0:T(8,128)(2,1)} %copy-done.5) | copy-start | bytes 98308

commit v10 on v9

--- a/solution.py
+++ b/solution.py
@@ -128,6 +128,7 @@
     index,
     whole,
     gain,
+    query_hbm,
     w_key,
     w_value,
     w_down,
@@ -137,7 +138,9 @@
     taps_k,
     taps_v,
     pieces,
+    tail,
     normed,
+    pre_q,
     pre_k,
     pre_v,
     cumulated,
@@ -145,7 +148,11 @@
     own_rows,
     extended_k,
     extended_v,
+    w_query,
+    arrived,
 ):
+    fetch = pltpu.make_async_copy(query_hbm, w_query, arrived.at[0])
+    fetch.start()
     chunks = WIDTH // CHUNK
     squares = jnp.zeros((BLOCK, CHUNK), F32)
     for f in range(chunks):
@@ -228,19 +235,18 @@
                 pieces[p, 0:PIECE, :] = state[g * PIECE : (g + 1) * PIECE, lanes].astype(BF16)
                 pieces[p, PIECE : PIECE + 8, :] = tile_b
                 pieces[p, PIECE + 8 :, :] = tile_c
-
-
-def queries_gate(normed, w_query, w_gate, head_gain, pre_k, pre_v, pre_q, gate, tail):
-    rows = normed[...]
-    gate[...] = silu(dot(rows, w_gate[...])) * head_gain[...]
+    fetch.wait()
     of_queries = dot(rows, w_query[...])
     pre_q[...] = of_queries
     tail[:, :HEAD_K] = of_queries[BLOCK - 8 :, :]
-    tail[:, HEAD_K : 2 * HEAD_K] = pre_k[BLOCK - 8 :, :]
-    tail[:, 2 * HEAD_K :] = pre_v[BLOCK - 8 :, :]
+    tail[:, HEAD_K : 2 * HEAD_K] = of_keys[BLOCK - 8 :, :]
+    tail[:, 2 * HEAD_K :] = of_values[BLOCK - 8 :, :]
 
 
 def block_attention(
+    normed,
+    w_gate,
+    head_gain,
     pre_q,
     pre_k,
     pre_v,
@@ -251,11 +257,15 @@
     cumulated,
     columns,
     own_rows,
+    left,
     intra,
     reach,
+    gate,
     extended,
     extended_v,
 ):
+    del left
+    gate[...] = silu(dot(normed[...], w_gate[...])) * head_gain[...]
     edges = edge[...]
     queries = silu(conv(pre_q[...], edges[:, :HEAD_K], taps_q, extended.at[0], columns))
     queries = queries * HEAD_K ** (-0.5)
@@ -299,8 +309,7 @@
     intra[...] = dot(weights.astype(BF16), values.astype(BF16))
 
 
-def scan_blocks(index, pieces, reach, states):
-    del reach
+def scan_blocks(index, pieces, states, left):
     owner = (index[0] % ROWS_Y) * ROWS_X + index[0] // ROWS_Y
     first = (owner % (BLOCKS // 2)) * PIECE
     shape = (PIECE, LANES)
@@ -322,6 +331,7 @@
             added = added + column * pushed[2 + t : 3 + t, :]
         state = state * (tile_b[0:1, :] + tile_b[1:2, :]) + added
         back_b, back_c = tile_b, tile_c
+    left[...] = state
 
 
 def attend(index, intra, reach, incoming, gate, w_out, kept, kept_squares, sent):
@@ -398,9 +408,9 @@
         conv_query,
         conv_key,
         conv_value,
-        head_gain.reshape(1, CHUNK),
-    )
-    hidden, gain, down, up, bias, segs, taps_q, taps_k, taps_v, out_gain, copies = local_call(
+        w_value,
+    )
+    hidden, gain, down, up, bias, segs, taps_q, taps_k, taps_v, value_here, copies = local_call(
         fetch_and_spread,
         [*((a.shape, a.dtype) for a in needed), ((8, BLOCK, CHUNK), BF16)],
         block_at,
@@ -412,11 +422,13 @@
     )
     of_core = lax.all_to_all(copies, CHIPS, 0, 0)
     whole = lax.all_gather(of_core, "core", axis=0)
-    pieces, normed, pre_k, pre_v, cumulated, columns, own_rows = local_call(
+    pieces, tail, normed, pre_q, pre_k, pre_v, cumulated, columns, own_rows = local_call(
         block_state,
         [
             ((BLOCKS, PIECE + 16, LANES), BF16),
+            ((8, 2 * HEAD_K + CHUNK), F32),
             ((BLOCK, WIDTH), BF16),
+            ((BLOCK, HEAD_K), F32),
             ((BLOCK, HEAD_K), F32),
             ((BLOCK, CHUNK), F32),
             ((BLOCK, HEAD_K), F32),
@@ -426,32 +438,40 @@
         block_at,
         whole,
         gain,
+        w_query,
         w_key,
-        w_value,
+        value_here,
         down,
         up,
         bias,
         segs,
         taps_k,
         taps_v,
-        scratch=[pltpu.VMEM((BLOCK + 8, HEAD_K), F32), pltpu.VMEM((BLOCK + 8, CHUNK), F32)],
+        scratch=[
+            pltpu.VMEM((BLOCK + 8, HEAD_K), F32),
+            pltpu.VMEM((BLOCK + 8, CHUNK), F32),
+            pltpu.VMEM((WIDTH, HEAD_K), BF16),
+            pltpu.SemaphoreType.DMA((1,)),
+        ],
         scalars=1,
-    )
+        anywhere=(3,),
+    )
+    edge = lax.ppermute(tail, SEQ, [(i, i + 1) for i in range(BLOCKS - 1)])
     owned = lax.all_to_all(pieces, GRID, 0, 0)
-    pre_q, gate, tail = local_call(
-        queries_gate,
-        [((BLOCK, HEAD_K), F32), ((BLOCK, CHUNK), F32), ((8, 2 * HEAD_K + CHUNK), F32)],
+    states, left = local_call(
+        scan_blocks,
+        [((BLOCKS, PIECE, LANES), BF16), ((PIECE, LANES), F32)],
+        block_at,
+        owned,
+        scalars=1,
+    )
+    incoming = lax.all_to_all(states, GRID, 0, 0).reshape(2, CHUNK, LANES)
+    intra, reach, gate = local_call(
+        block_attention,
+        [((BLOCK, CHUNK), F32), ((BLOCK, HEAD_K), F32), ((BLOCK, CHUNK), F32)],
         normed,
-        w_query,
         w_gate,
-        out_gain,
-        pre_k,
-        pre_v,
-    )
-    edge = lax.ppermute(tail, SEQ, [(i, i + 1) for i in range(BLOCKS - 1)])
-    intra, reach = local_call(
-        block_attention,
-        [((BLOCK, CHUNK), F32), ((BLOCK, HEAD_K), F32)],
+        head_gain.reshape(1, CHUNK),
         pre_q,
         pre_k,
         pre_v,
@@ -462,20 +482,12 @@
         cumulated,
         columns,
         own_rows,
+        left,
         scratch=[
             pltpu.VMEM((2, BLOCK + 8, HEAD_K), F32),
             pltpu.VMEM((BLOCK + 8, CHUNK), F32),
         ],
     )
-    (states,) = local_call(
-        scan_blocks,
-        [((BLOCKS, PIECE, LANES), BF16)],
-        block_at,
-        owned,
-        reach,
-        scalars=1,
-    )
-    incoming = lax.all_to_all(states, GRID, 0, 0).reshape(2, CHUNK, LANES)
     mine, my_squares, sent = local_call(
         attend,
         [((8, BLOCK, CHUNK), F32), ((8, BLOCK), F32), ((8 * BLOCK + 8, CHUNK), BF16)],

time: 85.9 us -> 82.7 us (0.963)
  starting transfers between devices: 12.8 us -> 7.26 us
  blocking collectives: 57.5 us -> 62 us
  local copies, waits for them, and re-layouts: 2.21 us -> 0.67 us
  waiting for transfers between devices: 4.96 us -> 3.47 us
    all_to_all x1, starting transfers between devices: 9.67 us -> 4.13 us  [shards(): incoming = lax.all_to_all(states, GRID, 0, 0).reshape(2, CHUNK, LANES)]
    all_to_all x1, blocking collectives: 15.5 us -> 20.2 us  [shards(): owned = lax.all_to_all(pieces, GRID, 0, 0)]
    unnamed x18 -> x8, local copies, waits for them, and re-layouts: 2.21 us -> 0.67 us
    all_to_all x1, waiting for transfers between devices: 4.07 us -> 2.58 us  [shards(): incoming = lax.all_to_all(states, GRID, 0, 0).reshape(2, CHUNK, LANES)]
    pallas_call x8 -> x7, Pallas kernels: 7.86 us -> 8.41 us  [local_call(): pl.pallas_call(kernel, out_shape=[jax.ShapeDtypeStruct(s, t) if last else...]
where the time goes in v10:
time: 82.7 us; the launch traced here: 81.8 us
  blocking collectives  62 us (75%)
  Pallas kernels  8.41 us (10%)
  starting transfers between devices  7.26 us (9%)
  waiting for transfers between devices  3.47 us (4%)
    all_to_all x1, blocking collectives, shards(): owned = lax.all_to_all(pieces, GRID, 0, 0)  20.2 us
    all_to_all x1, blocking collectives, shards(): of_core = lax.all_to_all(copies, CHIPS, 0, 0)  17.8 us
    all_to_all x1, blocking collectives, shards(): arrived = lax.all_to_all(pairs, CHIPS, 0, 0)  14.5 us
    pallas_call x7, Pallas kernels, local_call(): pl.pallas_call(kernel, out_shape=[jax.ShapeDtypeStruct(s, t) if last else...  8.41 us
    all_gather x1, blocking collectives, shards(): both = lax.all_gather(sent, 'core', axis=0)  5 us
    all_gather x1, blocking collectives, shards(): whole = lax.all_gather(of_core, 'core', axis=0)  4.46 us
    all_to_all x1, starting transfers between devices, shards(): incoming = lax.all_to_all(states, GRID, 0, 0).reshape(2, CHUNK, LANES)  4.13 us
    ppermute x1, starting transfers between devices, shards(): edge = lax.ppermute(tail, SEQ, [(i, i + 1) for i in range(BLOCKS - 1)])  3.14 us
  transfers between devices with their start and end apart: 2, of which 2 were waited for; matrix products, arithmetic and copies ran while one was open for 0% of the time, Pallas kernels for 2%

profile of v10, /device:TPU:1, one launch (start us, length us, event | category | flops | bytes accessed | tf_op | source)
XLA Modules:
  0.0 81.8 jit_solution(3442390856845609174)
XLA Ops:
  0.0 0.0 copy-start
  0.0 1.4 %fetch_and_spread.1 = (bf16[128,128]{1,0:T(8,128)(2,1)S(1)}, f32[1,2048]{1,0:T(1,128)S(1)}, bf16[16,2048]{1,0:T(8,128)(2,1)S(1)}, bf16[16,256]{1,0:T(8,128)(2,1)...) custom-call(s32[1]{0:T(128)} %bitcast.1.index, ...), custom_call_target="tpu_custom_call" | custom-call | tf_op jit(solution)/shard_map/fetch_and_spread/pallas_call | solution.py:38
  1.4 17.8 %all_to_all.20 = bf16[8,128,128]{2,1,0:T(8,128)(2,1)S(1)} all-to-all(bf16[8,128,128]{2,1,0:T(8,128)(2,1)S(1)} %get-tuple-element.33), channel_id=1, replica_groups=mesh['x'=4,'y'=8,'row'=4,'zhi'=2,'core'=2] {'row','zhi'}, dimensions={0} | all-to-all | bytes 524288 | tf_op jit(solution)/shard_map/all_to_all | solution.py:423
  19.2 4.5 %all-gather = bf16[16,128,128]{2,1,0:T(8,128)(2,1)S(1)} all-gather(bf16[8,128,128]{2,1,0:T(8,128)(2,1)S(1)} %all_to_all.20), channel_id=2, replica_groups=mesh['x'=4,'y'=8,'row'=4,'zhi'=2,'core'=2] {'core'}, dimensions={0}, use_global_device_ids=true | all-gather | bytes 786432 | tf_op jit(solution)/shard_map/all_gather | solution.py:424
  23.6 0.0 copy-done
  23.6 2.3 %block_state.1 = (bf16[32,24,128]{2,1,0:T(8,128)(2,1)S(1)}, f32[8,640]{1,0:T(8,128)S(1)}, bf16[128,2048]{1,0:T(8,128)(2,1)S(1)}, f32[128,256]{1,0:T(8,128)S(1)},...) custom-call(s32[1]{0:T(128)} %bitcast.1.index, ...), custom_call_target="tpu_custom_call" | custom-call | tf_op jit(solution)/shard_map/block_state/pallas_call | solution.py:38
  25.9 0.0 copy-start.1
  25.9 20.2 %all_to_all.21.pieces = bf16[32,24,128]{2,1,0:T(8,128)(2,1)S(1)} all-to-all(bf16[32,24,128]{2,1,0:T(8,128)(2,1)S(1)} %get-tuple-element.51), channel_id=1, replica_groups=mesh['x'=4,'y'=8,'row'=4,'zhi'=2,'core'=2] {'y','x'}, dimensions={0} | all-to-all | bytes 393216 | tf_op jit(solution)/shard_map/all_to_all | solution.py:460
  46.1 1.7 %scan_blocks.1 = (bf16[32,8,128]{2,1,0:T(8,128)(2,1)}, f32[8,128]{1,0:T(8,128)S(1)}) custom-call(s32[1]{0:T(128)} %bitcast.1.index, bf16[32,24,128]{2,1,0:T(8,128)(2,1)S(1)} %all_to_all.21.pieces), custom_call_target="tpu_custom_call" | custom-call | tf_op jit(solution)/shard_map/scan_blocks/pallas_call | solution.py:38
  47.8 4.1 %all-to-all-start.2 = ((bf16[32,8,128]{2,1,0:T(8,128)(2,1)}), bf16[32,8,128]{2,1,0:T(8,128)(2,1)S(1)}, u32[]{:S(2)}, u32[]{:S(2)}) async-start(bf16[32,8,128]{2,1,0:T(8,128)(2,1)} %get-tuple-element.55), calls=%async_computation.2 | async-start | bytes 131072 | tf_op jit(solution)/shard_map/all_to_all | solution.py:468
  51.9 3.1 %collective-permute-start = (f32[8,640]{1,0:T(8,128)S(1)}, f32[8,640]{1,0:T(8,128)S(1)}, u32[]{:S(2)}, u32[]{:S(2)}) collective-permute-start(f32[8,640]{1,0:T(8,128)S(1)} %get-tuple-element.46), channel_id=1, source_target_pairs={{0,16},{16,32},{32,48},{48,64},{64,80},{80,96},{96,112},{112,128},... | collective-permute-start | bytes 61448 | tf_op jit(solution)/shard_map/ppermute | solution.py:459
  55.1 0.9 %collective-permute-done.edge = f32[8,640]{1,0:T(8,128)S(1)} collective-permute-done((f32[8,640]{1,0:T(8,128)S(1)}, f32[8,640]{1,0:T(8,128)S(1)}, u32[]{:S(2)}, u32[]{:S(2)}) %collective-permute-start) | collective-permute-done | bytes 20512 | tf_op jit(solution)/shard_map/ppermute | solution.py:459
  56.0 0.0 copy-start.3
  56.0 0.0 copy-done.1
  56.0 0.7 copy-done.3
  56.6 0.0 copy-start.2
  56.6 1.6 %block_attention.1 = (f32[128,128]{1,0:T(8,128)S(1)}, f32[128,256]{1,0:T(8,128)S(1)}, f32[128,128]{1,0:T(8,128)S(1)}) custom-call(bf16[128,2048]{1,0:T(8,128)(2,1)S(1)} %get-tuple-element.42.normed, bf16[2048,128]{1,0:T(8,128)(2,1)S(1)} %copy-done.1, f32[1,128]{1,0:T(1,128)S(1)} %bitcast.13, f32[128,256]{1,0:T(8,128)S(1)} %get-tuple-element.43.pre_q, ...), custom_call_target="tpu_custom_call" | custom-call | tf_op jit(solution)/shard_map/block_attention/pallas_call | solution.py:38
  58.2 2.6 %all-to-all-done.2 = bf16[32,8,128]{2,1,0:T(8,128)(2,1)S(1)} async-done(((bf16[32,8,128]{2,1,0:T(8,128)(2,1)}), bf16[32,8,128]{2,1,0:T(8,128)(2,1)S(1)}, u32[]{:S(2)}, u32[]{:S(2)}) %all-to-all-start.2) | async-done | bytes 65568 | tf_op jit(solution)/shard_map/all_to_all | solution.py:468
  60.8 0.0 copy-done.2
  60.8 0.6 attend.1
  61.4 5.0 %all-gather.1 = bf16[2064,128]{1,0:T(8,128)(2,1)S(1)} all-gather(bf16[1032,128]{1,0:T(8,128)(2,1)S(1)} %get-tuple-element.59), channel_id=3, replica_groups=mesh['x'=4,'y'=8,'row'=4,'zhi'=2,'core'=2] {'core'}, dimensions={0}, use_global_device_ids=true | all-gather | bytes 792576 | tf_op jit(solution)/shard_map/all_gather | solution.py:502
  66.4 0.1 pair_sum.1
  66.4 14.5 %all_to_all.22.received = bf16[8,136,128]{2,1,0:T(8,128)(2,1)S(1)} all-to-all(bf16[8,136,128]{2,1,0:T(8,128)(2,1)S(1)} %pair_sum.1), channel_id=1, replica_groups=mesh['x'=4,'y'=8,'row'=4,'zhi'=2,'core'=2] {'row','zhi'}, dimensions={0} | all-to-all | bytes 557056 | tf_op jit(solution)/shard_map/all_to_all | solution.py:506
  80.9 0.9 %finish.1 = bf16[128,128]{1,0:T(8,128)(2,1)} custom-call(bf16[8,136,128]{2,1,0:T(8,128)(2,1)S(1)} %all_to_all.22.received, bf16[128,128]{1,0:T(8,128)(2,1)S(1)} %get-tuple-element.60.hidden), custom_call_target="tpu_custom_call" | custom-call | tf_op jit(solution)/shard_map/finish/pallas_call | solution.py:38
Async XLA Ops:
  0.0 23.6 %copy-start = (bf16[2048,256]{1,0:T(8,128)(2,1)S(1)}, bf16[2048,256]{1,0:T(8,128)(2,1)}, u32[]{:S(2)}) copy-start(bf16[2048,256]{1,0:T(8,128)(2,1)} %w_key.1) | copy-start | bytes 3145732
  25.9 30.1 %copy-start.1 = (bf16[2048,128]{1,0:T(8,128)(2,1)S(1)}, bf16[2048,128]{1,0:T(8,128)(2,1)}, u32[]{:S(2)}) copy-start(bf16[2048,128]{1,0:T(8,128)(2,1)} %w_gate.1) | copy-start | bytes 1572868
  47.8 13.0 %all-to-all-start.2 = ((bf16[32,8,128]{2,1,0:T(8,128)(2,1)}), bf16[32,8,128]{2,1,0:T(8,128)(2,1)S(1)}, u32[]{:S(2)}, u32[]{:S(2)}) async-start(bf16[32,8,128]{2,1,0:T(8,128)(2,1)} %get-tuple-element.55), calls=%async_computation.2 | async-start | bytes 131072 | tf_op jit(solution)/shard_map/all_to_all | solution.py:468
  51.9 4.0 %collective-permute-start = (f32[8,640]{1,0:T(8,128)S(1)}, f32[8,640]{1,0:T(8,128)S(1)}, u32[]{:S(2)}, u32[]{:S(2)}) collective-permute-start(f32[8,640]{1,0:T(8,128)S(1)} %get-tuple-element.46), channel_id=1, source_target_pairs={{0,16},{16,32},{32,48},{48,64},{64,80},{80,96},{96,112},{112,128},... | collective-permute-start | bytes 61448 | tf_op jit(solution)/shard_map/ppermute | solution.py:459
  56.0 0.7 copy-start.3
  56.6 4.1 %copy-start.2 = (bf16[128,2048]{1,0:T(8,128)(2,1)S(1)}, bf16[128,2048]{1,0:T(8,128)(2,1)}, u32[]{:S(2)}) copy-start(bf16[128,2048]{1,0:T(8,128)(2,1)} %w_out.1) | copy-start | bytes 1572868

commit v11 on v10

--- a/solution.py
+++ b/solution.py
@@ -309,28 +309,36 @@
     intra[...] = dot(weights.astype(BF16), values.astype(BF16))
 
 
-def scan_blocks(index, pieces, states, left):
+def scan_blocks(index, pieces, edge, states, left):
+    del edge
     owner = (index[0] % ROWS_Y) * ROWS_X + index[0] // ROWS_Y
     first = (owner % (BLOCKS // 2)) * PIECE
-    shape = (PIECE, LANES)
-    lane = lax.broadcasted_iota(jnp.int32, shape, 1)
-    chosen = lane == lax.broadcasted_iota(jnp.int32, shape, 0) + first
-    state = jnp.zeros(shape, F32)
-    back_b = back_c = jnp.zeros((8, LANES), F32)
-    for block in range(BLOCKS):
-        at = (block % ROWS_Y) * ROWS_X + block // ROWS_Y
+    order = [(block % ROWS_Y) * ROWS_X + block // ROWS_Y for block in range(BLOCKS)]
+    shape = (BLOCKS, 8, LANES)
+    tiles_b = jnp.stack([pieces[at, PIECE : PIECE + 8, :].astype(F32) for at in order])
+    tiles_c = jnp.stack([pieces[at, PIECE + 8 :, :].astype(F32) for at in order])
+    nothing = jnp.zeros((1, 8, LANES), F32)
+    back_b = jnp.concatenate([nothing, tiles_b[:-1]], axis=0)
+    back_c = jnp.concatenate([nothing, tiles_c[:-1]], axis=0)
+    pushed = silu(tiles_b + pltpu.roll(back_b, 5, 1)) * tiles_c
+    values = pltpu.roll(silu(tiles_c + pltpu.roll(back_c, LANES // 2, 2)), 5, 1)
+    row = lax.broadcasted_iota(jnp.int32, shape, 1)
+    values = jnp.where((row >= 2) & (row < 5), values, 0.0)
+    rows = BLOCKS * 8
+    lane = lax.broadcasted_iota(jnp.int32, (PIECE, LANES), 1)
+    chosen = lane == lax.broadcasted_iota(jnp.int32, (PIECE, LANES), 0) + first
+    chosen = jnp.where(chosen, 1.0, 0.0).astype(BF16)
+    mine = dot(chosen, values.reshape(rows, LANES).astype(BF16), LAST)
+    same = lax.broadcasted_iota(jnp.int32, (rows, rows), 0) // 8
+    same = same == lax.broadcasted_iota(jnp.int32, (rows, rows), 1) // 8
+    spread = jnp.where(same, jnp.concatenate([mine] * BLOCKS, axis=0), 0.0)
+    added = dot(spread.astype(BF16), pushed.reshape(rows, LANES).astype(BF16))
+    state = jnp.zeros((PIECE, LANES), F32)
+    for block, at in enumerate(order):
         states[at] = state.astype(BF16)
-        tile_b = pieces[at, PIECE : PIECE + 8, :].astype(F32)
-        tile_c = pieces[at, PIECE + 8 :, :].astype(F32)
-        pushed = silu(tile_b + pltpu.roll(back_b, 5, 0)) * tile_c
-        values = silu(tile_c + pltpu.roll(back_c, LANES // 2, 1))
-        added = pieces[at, 0:PIECE, :].astype(F32)
-        for t in range(3):
-            row = jnp.broadcast_to(values[5 + t : 6 + t, :], shape)
-            column = jnp.sum(jnp.where(chosen, row, 0.0), axis=1, keepdims=True)
-            added = added + column * pushed[2 + t : 3 + t, :]
-        state = state * (tile_b[0:1, :] + tile_b[1:2, :]) + added
-        back_b, back_c = tile_b, tile_c
+        decay = tiles_b[block, 0:1, :] + tiles_b[block, 1:2, :]
+        own = pieces[at, 0:PIECE, :].astype(F32) + added[block * 8 : block * 8 + 8, :]
+        state = state * decay + own
     left[...] = state
 
 
@@ -463,6 +471,7 @@
         [((BLOCKS, PIECE, LANES), BF16), ((PIECE, LANES), F32)],
         block_at,
         owned,
+        edge,
         scalars=1,
     )
     incoming = lax.all_to_all(states, GRID, 0, 0).reshape(2, CHUNK, LANES)

time: 82.7 us -> 83.5 us (level)
  blocking collectives: 62 us -> 41.8 us
  waiting for transfers between devices: 3.47 us -> 14 us
  starting transfers between devices: 7.26 us -> 17.7 us
    all_to_all x1 -> x0, blocking collectives: 20.2 us -> none  [shards(): owned = lax.all_to_all(pieces, GRID, 0, 0)]
    all_to_all x0 -> x1, starting transfers between devices: none -> 9.81 us  [shards(): owned = lax.all_to_all(pieces, GRID, 0, 0)]
    all_to_all x0 -> x1, waiting for transfers between devices: none -> 6.55 us  [shards(): owned = lax.all_to_all(pieces, GRID, 0, 0)]
    all_to_all x1, waiting for transfers between devices: 2.58 us -> 6.6 us  [shards(): incoming = lax.all_to_all(states, GRID, 0, 0).reshape(2, CHUNK, LANES)]
  transfers between devices with their start and end apart: 2 -> 3, of which waited for: 2 -> 3; matrix products, arithmetic and copies ran while one was open for 0% -> 0% of each run, Pallas kernels for 2% -> 2%
where the time goes in v11:
time: 83.5 us; the launch traced here: 83.1 us
  blocking collectives  41.8 us (50%)
  starting transfers between devices  17.7 us (21%)
  waiting for transfers between devices  14 us (17%)
  Pallas kernels  8.84 us (11%)
    all_to_all x1, blocking collectives, shards(): of_core = lax.all_to_all(copies, CHIPS, 0, 0)  17.8 us
    all_to_all x1, blocking collectives, shards(): arrived = lax.all_to_all(pairs, CHIPS, 0, 0)  14.5 us
    all_to_all x1, starting transfers between devices, shards(): owned = lax.all_to_all(pieces, GRID, 0, 0)  9.81 us
    pallas_call x7, Pallas kernels, local_call(): pl.pallas_call(kernel, out_shape=[jax.ShapeDtypeStruct(s, t) if last else...  8.84 us
    all_to_all x1, waiting for transfers between devices, shards(): incoming = lax.all_to_all(states, GRID, 0, 0).reshape(2, CHUNK, LANES)  6.6 us
    all_to_all x1, waiting for transfers between devices, shards(): owned = lax.all_to_all(pieces, GRID, 0, 0)  6.55 us
    all_gather x1, blocking collectives, shards(): both = lax.all_gather(sent, 'core', axis=0)  5 us
    all_to_all x1, starting transfers between devices, shards(): incoming = lax.all_to_all(states, GRID, 0, 0).reshape(2, CHUNK, LANES)  4.77 us
  transfers between devices with their start and end apart: 3, of which 3 were waited for; matrix products, arithmetic and copies ran while one was open for 0% of the time, Pallas kernels for 2%

profile of v11, /device:TPU:1, one launch (start us, length us, event | category | flops | bytes accessed | tf_op | source)
XLA Modules:
  0.0 83.1 jit_solution(15960574707583921652)
XLA Ops:
  0.0 0.0 copy-start
  0.0 1.4 %fetch_and_spread.1 = (bf16[128,128]{1,0:T(8,128)(2,1)S(1)}, f32[1,2048]{1,0:T(1,128)S(1)}, bf16[16,2048]{1,0:T(8,128)(2,1)S(1)}, bf16[16,256]{1,0:T(8,128)(2,1)...) custom-call(s32[1]{0:T(128)} %bitcast.1.index, ...), custom_call_target="tpu_custom_call" | custom-call | tf_op jit(solution)/shard_map/fetch_and_spread/pallas_call | solution.py:38
  1.4 17.8 %all_to_all.20 = bf16[8,128,128]{2,1,0:T(8,128)(2,1)S(1)} all-to-all(bf16[8,128,128]{2,1,0:T(8,128)(2,1)S(1)} %get-tuple-element.33), channel_id=1, replica_groups=mesh['x'=4,'y'=8,'row'=4,'zhi'=2,'core'=2] {'row','zhi'}, dimensions={0} | all-to-all | bytes 524288 | tf_op jit(solution)/shard_map/all_to_all | solution.py:431
  19.2 4.5 %all-gather = bf16[16,128,128]{2,1,0:T(8,128)(2,1)S(1)} all-gather(bf16[8,128,128]{2,1,0:T(8,128)(2,1)S(1)} %all_to_all.20), channel_id=2, replica_groups=mesh['x'=4,'y'=8,'row'=4,'zhi'=2,'core'=2] {'core'}, dimensions={0}, use_global_device_ids=true | all-gather | bytes 786432 | tf_op jit(solution)/shard_map/all_gather | solution.py:432
  23.6 0.0 copy-done
  23.6 3.3 %block_state.1 = (bf16[32,24,128]{2,1,0:T(8,128)(2,1)}, f32[8,640]{1,0:T(8,128)S(1)}, bf16[128,2048]{1,0:T(8,128)(2,1)S(1)}, f32[128,256]{1,0:T(8,128)S(1)}, f32...) custom-call(s32[1]{0:T(128)} %bitcast.1.index, ...), custom_call_target="tpu_custom_call" | custom-call | tf_op jit(solution)/shard_map/block_state/pallas_call | solution.py:38
  27.0 0.0 copy-start.1
  27.0 9.8 %all-to-all-start.1 = ((bf16[32,24,128]{2,1,0:T(8,128)(2,1)}), bf16[32,24,128]{2,1,0:T(8,128)(2,1)S(1)}, u32[]{:S(2)}, u32[]{:S(2)}) async-start(bf16[32,24,128]{2,1,0:T(8,128)(2,1)} %get-tuple-element.51), calls=%async_computation.1 | async-start | bytes 393216 | tf_op jit(solution)/shard_map/all_to_all | solution.py:468
  36.8 3.1 %collective-permute-start = (f32[8,640]{1,0:T(8,128)S(1)}, f32[8,640]{1,0:T(8,128)S(1)}, u32[]{:S(2)}, u32[]{:S(2)}) collective-permute-start(f32[8,640]{1,0:T(8,128)S(1)} %get-tuple-element.46), channel_id=1, source_target_pairs={{0,16},{16,32},{32,48},{48,64},{64,80},{80,96},{96,112},{112,128},... | collective-permute-start | bytes 61448 | tf_op jit(solution)/shard_map/ppermute | solution.py:467
  39.9 0.9 %collective-permute-done.edge = f32[8,640]{1,0:T(8,128)S(1)} collective-permute-done((f32[8,640]{1,0:T(8,128)S(1)}, f32[8,640]{1,0:T(8,128)S(1)}, u32[]{:S(2)}, u32[]{:S(2)}) %collective-permute-start) | collective-permute-done | bytes 20512 | tf_op jit(solution)/shard_map/ppermute | solution.py:467
  40.8 6.5 %all-to-all-done.1.pieces = bf16[32,24,128]{2,1,0:T(8,128)(2,1)S(1)} async-done(((bf16[32,24,128]{2,1,0:T(8,128)(2,1)}), bf16[32,24,128]{2,1,0:T(8,128)(2,1)S(1)}, u32[]{:S(2)}, u32[]{:S(2)}) %all-to-all-start.1) | async-done | bytes 196640 | tf_op jit(solution)/shard_map/all_to_all | solution.py:468
  47.4 1.0 %scan_blocks.1 = (bf16[32,8,128]{2,1,0:T(8,128)(2,1)}, f32[8,128]{1,0:T(8,128)S(1)}) custom-call(s32[1]{0:T(128)} %bitcast.1.index, bf16[32,24,128]{2,1,0:T(8,128)(2,1)S(1)} %all-to-all-done.1.pieces, f32[8,640]{1,0:T(8,128)S(1)} %collective-permute-done.edge), custom_call_target="tpu_custom_call" | custom-call | tf_op jit(solution)/shard_map/scan_blocks/pallas_call | solution.py:38
  48.4 4.8 %all-to-all-start.2 = ((bf16[32,8,128]{2,1,0:T(8,128)(2,1)}), bf16[32,8,128]{2,1,0:T(8,128)(2,1)S(1)}, u32[]{:S(2)}, u32[]{:S(2)}) async-start(bf16[32,8,128]{2,1,0:T(8,128)(2,1)} %get-tuple-element.55), calls=%async_computation.2 | async-start | bytes 131072 | tf_op jit(solution)/shard_map/all_to_all | solution.py:477
  53.2 0.0 copy-start.3
  53.2 0.0 copy-done.1
  53.2 0.6 copy-done.3
  53.9 1.6 %block_attention.1 = (f32[128,128]{1,0:T(8,128)S(1)}, f32[128,256]{1,0:T(8,128)S(1)}, f32[128,128]{1,0:T(8,128)S(1)}) custom-call(bf16[128,2048]{1,0:T(8,128)(2,1)S(1)} %get-tuple-element.42.normed, bf16[2048,128]{1,0:T(8,128)(2,1)S(1)} %copy-done.1, f32[1,128]{1,0:T(1,128)S(1)} %bitcast.13, f32[128,256]{1,0:T(8,128)S(1)} %get-tuple-element.43.pre_q, ...), custom_call_target="tpu_custom_call" | custom-call | tf_op jit(solution)/shard_map/block_attention/pallas_call | solution.py:38
  55.4 6.6 %all-to-all-done.2 = bf16[32,8,128]{2,1,0:T(8,128)(2,1)S(1)} async-done(((bf16[32,8,128]{2,1,0:T(8,128)(2,1)}), bf16[32,8,128]{2,1,0:T(8,128)(2,1)S(1)}, u32[]{:S(2)}, u32[]{:S(2)}) %all-to-all-start.2) | async-done | bytes 65568 | tf_op jit(solution)/shard_map/all_to_all | solution.py:477
  62.0 0.0 copy-done.2
  62.0 0.6 attend.1
  62.6 5.0 %all-gather.1 = bf16[2064,128]{1,0:T(8,128)(2,1)S(1)} all-gather(bf16[1032,128]{1,0:T(8,128)(2,1)S(1)} %get-tuple-element.59), channel_id=3, replica_groups=mesh['x'=4,'y'=8,'row'=4,'zhi'=2,'core'=2] {'core'}, dimensions={0}, use_global_device_ids=true | all-gather | bytes 792576 | tf_op jit(solution)/shard_map/all_gather | solution.py:511
  67.7 0.1 pair_sum.1
  67.7 14.5 %all_to_all.21.received = bf16[8,136,128]{2,1,0:T(8,128)(2,1)S(1)} all-to-all(bf16[8,136,128]{2,1,0:T(8,128)(2,1)S(1)} %pair_sum.1), channel_id=1, replica_groups=mesh['x'=4,'y'=8,'row'=4,'zhi'=2,'core'=2] {'row','zhi'}, dimensions={0} | all-to-all | bytes 557056 | tf_op jit(solution)/shard_map/all_to_all | solution.py:515
  82.2 0.9 %finish.1 = bf16[128,128]{1,0:T(8,128)(2,1)} custom-call(bf16[8,136,128]{2,1,0:T(8,128)(2,1)S(1)} %all_to_all.21.received, bf16[128,128]{1,0:T(8,128)(2,1)S(1)} %get-tuple-element.60.hidden), custom_call_target="tpu_custom_call" | custom-call | tf_op jit(solution)/shard_map/finish/pallas_call | solution.py:38
  (1 shorter events, 0.0 us)
Async XLA Ops:
  0.0 23.6 %copy-start = (bf16[2048,256]{1,0:T(8,128)(2,1)S(1)}, bf16[2048,256]{1,0:T(8,128)(2,1)}, u32[]{:S(2)}) copy-start(bf16[2048,256]{1,0:T(8,128)(2,1)} %w_key.1) | copy-start | bytes 3145732
  27.0 26.3 %copy-start.1 = (bf16[2048,128]{1,0:T(8,128)(2,1)S(1)}, bf16[2048,128]{1,0:T(8,128)(2,1)}, u32[]{:S(2)}) copy-start(bf16[2048,128]{1,0:T(8,128)(2,1)} %w_gate.1) | copy-start | bytes 1572868
  27.0 20.4 %all-to-all-start.1 = ((bf16[32,24,128]{2,1,0:T(8,128)(2,1)}), bf16[32,24,128]{2,1,0:T(8,128)(2,1)S(1)}, u32[]{:S(2)}, u32[]{:S(2)}) async-start(bf16[32,24,128]{2,1,0:T(8,128)(2,1)} %get-tuple-element.51), calls=%async_computation.1 | async-start | bytes 393216 | tf_op jit(solution)/shard_map/all_to_all | solution.py:468
  36.8 4.0 %collective-permute-start = (f32[8,640]{1,0:T(8,128)S(1)}, f32[8,640]{1,0:T(8,128)S(1)}, u32[]{:S(2)}, u32[]{:S(2)}) collective-permute-start(f32[8,640]{1,0:T(8,128)S(1)} %get-tuple-element.46), channel_id=1, source_target_pairs={{0,16},{16,32},{32,48},{48,64},{64,80},{80,96},{96,112},{112,128},... | collective-permute-start | bytes 61448 | tf_op jit(solution)/shard_map/ppermute | solution.py:467
  48.4 13.6 %all-to-all-start.2 = ((bf16[32,8,128]{2,1,0:T(8,128)(2,1)}), bf16[32,8,128]{2,1,0:T(8,128)(2,1)S(1)}, u32[]{:S(2)}, u32[]{:S(2)}) async-start(bf16[32,8,128]{2,1,0:T(8,128)(2,1)} %get-tuple-element.55), calls=%async_computation.2 | async-start | bytes 131072 | tf_op jit(solution)/shard_map/all_to_all | solution.py:477
  53.2 0.7 copy-start.3
  53.9 8.2 %copy-start.2 = (bf16[128,2048]{1,0:T(8,128)(2,1)S(1)}, bf16[128,2048]{1,0:T(8,128)(2,1)}, u32[]{:S(2)}) copy-start(bf16[128,2048]{1,0:T(8,128)(2,1)} %w_out.1) | copy-start | bytes 1572868

commit v12 on v11

--- a/solution.py
+++ b/solution.py
@@ -76,11 +76,10 @@
 
 def fetch_and_spread(index, core, *refs):
     del index, core
-    *refs, copies, arrived = refs
-    count = len(refs) // 2
-    fetches = [
-        pltpu.make_async_copy(refs[i], refs[count + i], arrived.at[i]) for i in range(count)
-    ]
+    *refs, copies, taps, arrived, gain = refs
+    count = (len(refs) + 1) // 2
+    targets = [*refs[count:], gain]
+    fetches = [pltpu.make_async_copy(refs[i], targets[i], arrived.at[i]) for i in range(count)]
     for fetch in fetches:
         fetch.start()
     fetches[0].wait()
@@ -88,6 +87,9 @@
         copies[j] = refs[count][...]
     for fetch in fetches[1:]:
         fetch.wait()
+    taps[0:4, :] = refs[2 * count - 2][...]
+    taps[4:8, :CHUNK] = jnp.broadcast_to(gain[...], (4, CHUNK))
+    taps[4:8, CHUNK:] = jnp.zeros((4, HEAD_K - CHUNK), F32)
 
 
 def conv(pre, edge, taps, extended, columns):
@@ -243,10 +245,12 @@
     tail[:, 2 * HEAD_K :] = of_values[BLOCK - 8 :, :]
 
 
+def output_gate(normed, w_gate, taps, left, gate):
+    del left
+    gate[...] = silu(dot(normed[...], w_gate[...])) * taps[4:5, :CHUNK]
+
+
 def block_attention(
-    normed,
-    w_gate,
-    head_gain,
     pre_q,
     pre_k,
     pre_v,
@@ -260,12 +264,10 @@
     left,
     intra,
     reach,
-    gate,
     extended,
     extended_v,
 ):
     del left
-    gate[...] = silu(dot(normed[...], w_gate[...])) * head_gain[...]
     edges = edge[...]
     queries = silu(conv(pre_q[...], edges[:, :HEAD_K], taps_q, extended.at[0], columns))
     queries = queries * HEAD_K ** (-0.5)
@@ -309,8 +311,7 @@
     intra[...] = dot(weights.astype(BF16), values.astype(BF16))
 
 
-def scan_blocks(index, pieces, edge, states, left):
-    del edge
+def scan_blocks(index, pieces, states, left):
     owner = (index[0] % ROWS_Y) * ROWS_X + index[0] // ROWS_Y
     first = (owner % (BLOCKS // 2)) * PIECE
     order = [(block % ROWS_Y) * ROWS_X + block // ROWS_Y for block in range(BLOCKS)]
@@ -413,18 +414,23 @@
         w_decay_up,
         decay_bias.reshape(1, HEAD_K),
         seg_ids.reshape(BLOCKS, BLOCK),
-        conv_query,
         conv_key,
         conv_value,
         w_value,
-    )
-    hidden, gain, down, up, bias, segs, taps_q, taps_k, taps_v, value_here, copies = local_call(
+        conv_query,
+        head_gain.reshape(1, CHUNK),
+    )
+    hidden, gain, down, up, bias, segs, taps_k, taps_v, value_here, _, copies, taps_q = local_call(
         fetch_and_spread,
-        [*((a.shape, a.dtype) for a in needed), ((8, BLOCK, CHUNK), BF16)],
+        [
+            *((a.shape, a.dtype) for a in needed[:-1]),
+            ((8, BLOCK, CHUNK), BF16),
+            ((8, HEAD_K), F32),
+        ],
         block_at,
         core_at,
         *needed,
-        scratch=[pltpu.SemaphoreType.DMA((len(needed),))],
+        scratch=[pltpu.SemaphoreType.DMA((len(needed),)), pltpu.VMEM((1, CHUNK), F32)],
         scalars=2,
         anywhere=range(2, 2 + len(needed)),
     )
@@ -471,16 +477,13 @@
         [((BLOCKS, PIECE, LANES), BF16), ((PIECE, LANES), F32)],
         block_at,
         owned,
-        edge,
         scalars=1,
     )
     incoming = lax.all_to_all(states, GRID, 0, 0).reshape(2, CHUNK, LANES)
-    intra, reach, gate = local_call(
+    (gate,) = local_call(output_gate, [((BLOCK, CHUNK), F32)], normed, w_gate, taps_q, left)
+    intra, reach = local_call(
         block_attention,
-        [((BLOCK, CHUNK), F32), ((BLOCK, HEAD_K), F32), ((BLOCK, CHUNK), F32)],
-        normed,
-        w_gate,
-        head_gain.reshape(1, CHUNK),
+        [((BLOCK, CHUNK), F32), ((BLOCK, HEAD_K), F32)],
         pre_q,
         pre_k,
         pre_v,

time: 83.5 us -> 82.1 us (0.983)
  blocking collectives: 41.8 us -> 62 us
  starting transfers between devices: 17.7 us -> 7.26 us
  waiting for transfers between devices: 14 us -> 3.96 us
    all_to_all x0 -> x1, blocking collectives: none -> 20.2 us  [shards(): owned = lax.all_to_all(pieces, GRID, 0, 0)]
    all_to_all x1 -> x0, starting transfers between devices: 9.81 us -> none  [shards(): owned = lax.all_to_all(pieces, GRID, 0, 0)]
    all_to_all x1 -> x0, waiting for transfers between devices: 6.55 us -> none  [shards(): owned = lax.all_to_all(pieces, GRID, 0, 0)]
    all_to_all x1, waiting for transfers between devices: 6.6 us -> 3.4 us  [shards(): incoming = lax.all_to_all(states, GRID, 0, 0).reshape(2, CHUNK, LANES)]
    pallas_call x7 -> x8, Pallas kernels: 8.84 us -> 8.51 us  [local_call(): pl.pallas_call(kernel, out_shape=[jax.ShapeDtypeStruct(s, t) if last else...]
  transfers between devices with their start and end apart: 3 -> 2, of which waited for: 3 -> 2; matrix products, arithmetic and copies ran while one was open for 0% -> 0% of each run, Pallas kernels for 2% -> 2%
where the time goes in v12:
time: 82.1 us; the launch traced here: 81.8 us
  blocking collectives  62 us (76%)
  Pallas kernels  8.51 us (10%)
  starting transfers between devices  7.26 us (9%)
  waiting for transfers between devices  3.96 us (5%)
    all_to_all x1, blocking collectives, shards(): owned = lax.all_to_all(pieces, GRID, 0, 0)  20.2 us
    all_to_all x1, blocking collectives, shards(): of_core = lax.all_to_all(copies, CHIPS, 0, 0)  17.8 us
    all_to_all x1, blocking collectives, shards(): arrived = lax.all_to_all(pairs, CHIPS, 0, 0)  14.5 us
    pallas_call x8, Pallas kernels, local_call(): pl.pallas_call(kernel, out_shape=[jax.ShapeDtypeStruct(s, t) if last else...  8.51 us
    all_gather x1, blocking collectives, shards(): both = lax.all_gather(sent, 'core', axis=0)  5 us
    all_gather x1, blocking collectives, shards(): whole = lax.all_gather(of_core, 'core', axis=0)  4.46 us
    all_to_all x1, starting transfers between devices, shards(): incoming = lax.all_to_all(states, GRID, 0, 0).reshape(2, CHUNK, LANES)  4.13 us
    all_to_all x1, waiting for transfers between devices, shards(): incoming = lax.all_to_all(states, GRID, 0, 0).reshape(2, CHUNK, LANES)  3.4 us
  transfers between devices with their start and end apart: 2, of which 2 were waited for; matrix products, arithmetic and copies ran while one was open for 0% of the time, Pallas kernels for 2%

profile of v12, /device:TPU:1, one launch (start us, length us, event | category | flops | bytes accessed | tf_op | source)
XLA Modules:
  0.0 81.8 jit_solution(7500627410816811087)
XLA Ops:
  0.0 0.0 copy-start
  0.0 2.0 %fetch_and_spread.1 = (bf16[128,128]{1,0:T(8,128)(2,1)S(1)}, f32[1,2048]{1,0:T(1,128)S(1)}, bf16[16,2048]{1,0:T(8,128)(2,1)S(1)}, bf16[16,256]{1,0:T(8,128)(2,1)...) custom-call(s32[1]{0:T(128)} %bitcast.1.index, ...), custom_call_target="tpu_custom_call" | custom-call | tf_op jit(solution)/shard_map/fetch_and_spread/pallas_call | solution.py:38
  2.0 17.8 %all_to_all.20 = bf16[8,128,128]{2,1,0:T(8,128)(2,1)S(1)} all-to-all(bf16[8,128,128]{2,1,0:T(8,128)(2,1)S(1)} %get-tuple-element.32), channel_id=1, replica_groups=mesh['x'=4,'y'=8,'row'=4,'zhi'=2,'core'=2] {'row','zhi'}, dimensions={0} | all-to-all | bytes 524288 | tf_op jit(solution)/shard_map/all_to_all | solution.py:437
  19.8 4.5 %all-gather = bf16[16,128,128]{2,1,0:T(8,128)(2,1)S(1)} all-gather(bf16[8,128,128]{2,1,0:T(8,128)(2,1)S(1)} %all_to_all.20), channel_id=2, replica_groups=mesh['x'=4,'y'=8,'row'=4,'zhi'=2,'core'=2] {'core'}, dimensions={0}, use_global_device_ids=true | all-gather | bytes 786432 | tf_op jit(solution)/shard_map/all_gather | solution.py:438
  24.2 0.0 copy-done
  24.2 2.3 %block_state.1 = (bf16[32,24,128]{2,1,0:T(8,128)(2,1)S(1)}, f32[8,640]{1,0:T(8,128)S(1)}, bf16[128,2048]{1,0:T(8,128)(2,1)S(1)}, f32[128,256]{1,0:T(8,128)S(1)},...) custom-call(s32[1]{0:T(128)} %bitcast.1.index, ...), custom_call_target="tpu_custom_call" | custom-call | tf_op jit(solution)/shard_map/block_state/pallas_call | solution.py:38
  26.5 0.0 copy-start.1
  26.5 20.2 %all_to_all.21.pieces = bf16[32,24,128]{2,1,0:T(8,128)(2,1)S(1)} all-to-all(bf16[32,24,128]{2,1,0:T(8,128)(2,1)S(1)} %get-tuple-element.49), channel_id=1, replica_groups=mesh['x'=4,'y'=8,'row'=4,'zhi'=2,'core'=2] {'y','x'}, dimensions={0} | all-to-all | bytes 393216 | tf_op jit(solution)/shard_map/all_to_all | solution.py:474
  46.7 1.1 %scan_blocks.1 = (bf16[32,8,128]{2,1,0:T(8,128)(2,1)}, f32[8,128]{1,0:T(8,128)S(1)}) custom-call(s32[1]{0:T(128)} %bitcast.1.index, bf16[32,24,128]{2,1,0:T(8,128)(2,1)S(1)} %all_to_all.21.pieces), custom_call_target="tpu_custom_call" | custom-call | tf_op jit(solution)/shard_map/scan_blocks/pallas_call | solution.py:38
  47.7 4.1 %all-to-all-start.2 = ((bf16[32,8,128]{2,1,0:T(8,128)(2,1)}), bf16[32,8,128]{2,1,0:T(8,128)(2,1)S(1)}, u32[]{:S(2)}, u32[]{:S(2)}) async-start(bf16[32,8,128]{2,1,0:T(8,128)(2,1)} %get-tuple-element.53), calls=%async_computation.2 | async-start | bytes 131072 | tf_op jit(solution)/shard_map/all_to_all | solution.py:482
  51.9 3.1 %collective-permute-start = (f32[8,640]{1,0:T(8,128)S(1)}, f32[8,640]{1,0:T(8,128)S(1)}, u32[]{:S(2)}, u32[]{:S(2)}) collective-permute-start(f32[8,640]{1,0:T(8,128)S(1)} %get-tuple-element.44), channel_id=1, source_target_pairs={{0,16},{16,32},{32,48},{48,64},{64,80},{80,96},{96,112},{112,128},... | collective-permute-start | bytes 61448 | tf_op jit(solution)/shard_map/ppermute | solution.py:473
  55.0 0.0 copy-done.1
  55.0 0.3 output_gate.1.gate
  55.3 0.0 copy-start.2
  55.4 0.6 collective-permute-done.edge
  55.9 1.4 %block_attention.1 = (f32[128,128]{1,0:T(8,128)S(1)}, f32[128,256]{1,0:T(8,128)S(1)}) custom-call(f32[128,256]{1,0:T(8,128)S(1)} %get-tuple-element.41.pre_q, f32[128,256]{1,0:T(8,128)S(1)} %get-tuple-element.42.pre_k, f32[128,128]{1,0:T(8,128)S(1)} %get-tuple-element.43.pre_v, f32[8,640]{1,0:T(8,128)S(1)} %collective-permute-done.edge, ...), custom_call_target="tpu_custom_call" | custom-call | tf_op jit(solution)/shard_map/block_attention/pallas_call | solution.py:38
  57.3 3.4 %all-to-all-done.2 = bf16[32,8,128]{2,1,0:T(8,128)(2,1)S(1)} async-done(((bf16[32,8,128]{2,1,0:T(8,128)(2,1)}), bf16[32,8,128]{2,1,0:T(8,128)(2,1)S(1)}, u32[]{:S(2)}, u32[]{:S(2)}) %all-to-all-start.2) | async-done | bytes 65568 | tf_op jit(solution)/shard_map/all_to_all | solution.py:482
  60.7 0.0 copy-done.2
  60.7 0.6 attend.1
  61.3 5.0 %all-gather.1 = bf16[2064,128]{1,0:T(8,128)(2,1)S(1)} all-gather(bf16[1032,128]{1,0:T(8,128)(2,1)S(1)} %get-tuple-element.57), channel_id=3, replica_groups=mesh['x'=4,'y'=8,'row'=4,'zhi'=2,'core'=2] {'core'}, dimensions={0}, use_global_device_ids=true | all-gather | bytes 792576 | tf_op jit(solution)/shard_map/all_gather | solution.py:514
  66.3 0.1 pair_sum.1
  66.4 14.5 %all_to_all.22.received = bf16[8,136,128]{2,1,0:T(8,128)(2,1)S(1)} all-to-all(bf16[8,136,128]{2,1,0:T(8,128)(2,1)S(1)} %pair_sum.1), channel_id=1, replica_groups=mesh['x'=4,'y'=8,'row'=4,'zhi'=2,'core'=2] {'row','zhi'}, dimensions={0} | all-to-all | bytes 557056 | tf_op jit(solution)/shard_map/all_to_all | solution.py:518
  80.9 0.9 %finish.1 = bf16[128,128]{1,0:T(8,128)(2,1)} custom-call(bf16[8,136,128]{2,1,0:T(8,128)(2,1)S(1)} %all_to_all.22.received, bf16[128,128]{1,0:T(8,128)(2,1)S(1)} %get-tuple-element.58.hidden), custom_call_target="tpu_custom_call" | custom-call | tf_op jit(solution)/shard_map/finish/pallas_call | solution.py:38
Async XLA Ops:
  0.0 24.2 %copy-start = (bf16[2048,256]{1,0:T(8,128)(2,1)S(1)}, bf16[2048,256]{1,0:T(8,128)(2,1)}, u32[]{:S(2)}) copy-start(bf16[2048,256]{1,0:T(8,128)(2,1)} %w_key.1) | copy-start | bytes 3145732
  26.5 28.5 %copy-start.1 = (bf16[2048,128]{1,0:T(8,128)(2,1)S(1)}, bf16[2048,128]{1,0:T(8,128)(2,1)}, u32[]{:S(2)}) copy-start(bf16[2048,128]{1,0:T(8,128)(2,1)} %w_gate.1) | copy-start | bytes 1572868
  47.7 13.0 %all-to-all-start.2 = ((bf16[32,8,128]{2,1,0:T(8,128)(2,1)}), bf16[32,8,128]{2,1,0:T(8,128)(2,1)S(1)}, u32[]{:S(2)}, u32[]{:S(2)}) async-start(bf16[32,8,128]{2,1,0:T(8,128)(2,1)} %get-tuple-element.53), calls=%async_computation.2 | async-start | bytes 131072 | tf_op jit(solution)/shard_map/all_to_all | solution.py:482
  51.9 4.0 %collective-permute-start = (f32[8,640]{1,0:T(8,128)S(1)}, f32[8,640]{1,0:T(8,128)S(1)}, u32[]{:S(2)}, u32[]{:S(2)}) collective-permute-start(f32[8,640]{1,0:T(8,128)S(1)} %get-tuple-element.44), channel_id=1, source_target_pairs={{0,16},{16,32},{32,48},{48,64},{64,80},{80,96},{96,112},{112,128},... | collective-permute-start | bytes 61448 | tf_op jit(solution)/shard_map/ppermute | solution.py:473
  55.3 5.4 %copy-start.2 = (bf16[128,2048]{1,0:T(8,128)(2,1)S(1)}, bf16[128,2048]{1,0:T(8,128)(2,1)}, u32[]{:S(2)}) copy-start(bf16[128,2048]{1,0:T(8,128)(2,1)} %w_out.1) | copy-start | bytes 1572868

commit v13 on v11

--- a/solution.py
+++ b/solution.py
@@ -139,7 +139,8 @@
     taps_v,
     pieces,
     tail,
-    normed,
+    gained,
+    row_scale,
     pre_q,
     pre_k,
     pre_v,
@@ -153,18 +154,16 @@
 ):
     fetch = pltpu.make_async_copy(query_hbm, w_query, arrived.at[0])
     fetch.start()
-    chunks = WIDTH // CHUNK
     squares = jnp.zeros((BLOCK, CHUNK), F32)
-    for f in range(chunks):
+    for f in range(WIDTH // CHUNK):
+        lanes = slice(f * CHUNK, (f + 1) * CHUNK)
         activ = whole[f % 2, f // 2].astype(F32)
         squares = squares + activ * activ
+        gained[:, lanes] = (activ * gain[:, lanes]).astype(BF16)
     scale = lax.rsqrt(jnp.sum(squares, axis=1, keepdims=True) / WIDTH + 1e-06)
-    for f in range(chunks):
-        lanes = slice(f * CHUNK, (f + 1) * CHUNK)
-        activ = whole[f % 2, f // 2].astype(F32)
-        normed[:, lanes] = (activ * scale * gain[:, lanes]).astype(BF16)
-    rows = normed[...]
-    rank_part = dot(rows, w_down[...], LAST)
+    row_scale[...] = jnp.broadcast_to(scale, (BLOCK, CHUNK))
+    rows = gained[...]
+    rank_part = dot(rows, w_down[...], LAST) * scale
 
     at = index[0]
     own = seg_ids[pl.ds(at, 1), :].astype(F32)
@@ -193,8 +192,8 @@
     cum = dot(lower, log_decay, precision=HIGHEST)
     cumulated[...] = cum
 
-    of_keys = dot(rows, w_key[...])
-    of_values = dot(rows, w_value[...])
+    of_keys = dot(rows, w_key[...]) * scale
+    of_values = dot(rows, w_value[...]) * scale
     pre_k[...] = of_keys
     pre_v[...] = of_values
     sums_k = conv(of_keys, None, taps_k, extended_k, columns)
@@ -236,17 +235,19 @@
                 pieces[p, PIECE : PIECE + 8, :] = tile_b
                 pieces[p, PIECE + 8 :, :] = tile_c
     fetch.wait()
-    of_queries = dot(rows, w_query[...])
+    of_queries = dot(rows, w_query[...]) * scale
     pre_q[...] = of_queries
     tail[:, :HEAD_K] = of_queries[BLOCK - 8 :, :]
     tail[:, HEAD_K : 2 * HEAD_K] = of_keys[BLOCK - 8 :, :]
     tail[:, 2 * HEAD_K :] = of_values[BLOCK - 8 :, :]
 
 
+def output_gate(gained, row_scale, w_gate, head_gain, left, gate):
+    del left
+    gate[...] = silu(dot(gained[...], w_gate[...]) * row_scale[...]) * head_gain[...]
+
+
 def block_attention(
-    normed,
-    w_gate,
-    head_gain,
     pre_q,
     pre_k,
     pre_v,
@@ -260,12 +261,10 @@
     left,
     intra,
     reach,
-    gate,
     extended,
     extended_v,
 ):
     del left
-    gate[...] = silu(dot(normed[...], w_gate[...])) * head_gain[...]
     edges = edge[...]
     queries = silu(conv(pre_q[...], edges[:, :HEAD_K], taps_q, extended.at[0], columns))
     queries = queries * HEAD_K ** (-0.5)
@@ -309,8 +308,7 @@
     intra[...] = dot(weights.astype(BF16), values.astype(BF16))
 
 
-def scan_blocks(index, pieces, edge, states, left):
-    del edge
+def scan_blocks(index, pieces, states, left):
     owner = (index[0] % ROWS_Y) * ROWS_X + index[0] // ROWS_Y
     first = (owner % (BLOCKS // 2)) * PIECE
     order = [(block % ROWS_Y) * ROWS_X + block // ROWS_Y for block in range(BLOCKS)]
@@ -430,12 +428,13 @@
     )
     of_core = lax.all_to_all(copies, CHIPS, 0, 0)
     whole = lax.all_gather(of_core, "core", axis=0)
-    pieces, tail, normed, pre_q, pre_k, pre_v, cumulated, columns, own_rows = local_call(
+    pieces, tail, gained, row_scale, pre_q, pre_k, pre_v, cumulated, columns, own_rows = local_call(
         block_state,
         [
             ((BLOCKS, PIECE + 16, LANES), BF16),
             ((8, 2 * HEAD_K + CHUNK), F32),
             ((BLOCK, WIDTH), BF16),
+            ((BLOCK, CHUNK), F32),
             ((BLOCK, HEAD_K), F32),
             ((BLOCK, HEAD_K), F32),
             ((BLOCK, CHUNK), F32),
@@ -471,16 +470,21 @@
         [((BLOCKS, PIECE, LANES), BF16), ((PIECE, LANES), F32)],
         block_at,
         owned,
-        edge,
         scalars=1,
     )
     incoming = lax.all_to_all(states, GRID, 0, 0).reshape(2, CHUNK, LANES)
-    intra, reach, gate = local_call(
-        block_attention,
-        [((BLOCK, CHUNK), F32), ((BLOCK, HEAD_K), F32), ((BLOCK, CHUNK), F32)],
-        normed,
+    (gate,) = local_call(
+        output_gate,
+        [((BLOCK, CHUNK), F32)],
+        gained,
+        row_scale,
         w_gate,
         head_gain.reshape(1, CHUNK),
+        left,
+    )
+    intra, reach = local_call(
+        block_attention,
+        [((BLOCK, CHUNK), F32), ((BLOCK, HEAD_K), F32)],
         pre_q,
         pre_k,
         pre_v,

time: 83.5 us -> 81.5 us (0.976)
  blocking collectives: 41.8 us -> 62 us
  waiting for transfers between devices: 14 us -> 3.3 us
  starting transfers between devices: 17.7 us -> 7.26 us
  Pallas kernels: 8.84 us -> 7.89 us
    all_to_all x0 -> x1, blocking collectives: none -> 20.2 us  [shards(): owned = lax.all_to_all(pieces, GRID, 0, 0)]
    all_to_all x1 -> x0, starting transfers between devices: 9.81 us -> none  [shards(): owned = lax.all_to_all(pieces, GRID, 0, 0)]
    all_to_all x1 -> x0, waiting for transfers between devices: 6.55 us -> none  [shards(): owned = lax.all_to_all(pieces, GRID, 0, 0)]
    all_to_all x1, waiting for transfers between devices: 6.6 us -> 3.3 us  [shards(): incoming = lax.all_to_all(states, GRID, 0, 0).reshape(2, CHUNK, LANES)]
    pallas_call x7 -> x8, Pallas kernels: 8.84 us -> 7.89 us  [local_call(): pl.pallas_call(kernel, out_shape=[jax.ShapeDtypeStruct(s, t) if last else...]
    ppermute x1, waiting for transfers between devices: 0.89 us -> 0.01 us  [shards(): edge = lax.ppermute(tail, SEQ, [(i, i + 1) for i in range(BLOCKS - 1)])]
  transfers between devices with their start and end apart: 3 -> 2, of which waited for: 3 -> 1; matrix products, arithmetic and copies ran while one was open for 0% -> 0% of each run, Pallas kernels for 2% -> 2%
where the time goes in v13:
time: 81.5 us; the launch traced here: 81.2 us
  blocking collectives  62 us (76%)
  Pallas kernels  7.89 us (10%)
  starting transfers between devices  7.26 us (9%)
  waiting for transfers between devices  3.3 us (4%)
    all_to_all x1, blocking collectives, shards(): owned = lax.all_to_all(pieces, GRID, 0, 0)  20.2 us
    all_to_all x1, blocking collectives, shards(): of_core = lax.all_to_all(copies, CHIPS, 0, 0)  17.8 us
    all_to_all x1, blocking collectives, shards(): arrived = lax.all_to_all(pairs, CHIPS, 0, 0)  14.5 us
    pallas_call x8, Pallas kernels, local_call(): pl.pallas_call(kernel, out_shape=[jax.ShapeDtypeStruct(s, t) if last else...  7.89 us
    all_gather x1, blocking collectives, shards(): both = lax.all_gather(sent, 'core', axis=0)  5 us
    all_gather x1, blocking collectives, shards(): whole = lax.all_gather(of_core, 'core', axis=0)  4.46 us
    all_to_all x1, starting transfers between devices, shards(): incoming = lax.all_to_all(states, GRID, 0, 0).reshape(2, CHUNK, LANES)  4.13 us
    all_to_all x1, waiting for transfers between devices, shards(): incoming = lax.all_to_all(states, GRID, 0, 0).reshape(2, CHUNK, LANES)  3.3 us
  transfers between devices with their start and end apart: 2, of which 1 were waited for; matrix products, arithmetic and copies ran while one was open for 0% of the time, Pallas kernels for 2%

profile of v13, /device:TPU:1, one launch (start us, length us, event | category | flops | bytes accessed | tf_op | source)
XLA Modules:
  0.0 81.2 jit_solution(16235999631926803687)
XLA Ops:
  0.0 1.4 %fetch_and_spread.1 = (bf16[128,128]{1,0:T(8,128)(2,1)S(1)}, f32[1,2048]{1,0:T(1,128)S(1)}, bf16[16,2048]{1,0:T(8,128)(2,1)S(1)}, bf16[16,256]{1,0:T(8,128)(2,1)...) custom-call(s32[1]{0:T(128)} %bitcast.1.index, ...), custom_call_target="tpu_custom_call" | custom-call | tf_op jit(solution)/shard_map/fetch_and_spread/pallas_call | solution.py:38
  1.4 17.8 %all_to_all.20 = bf16[8,128,128]{2,1,0:T(8,128)(2,1)S(1)} all-to-all(bf16[8,128,128]{2,1,0:T(8,128)(2,1)S(1)} %get-tuple-element.33), channel_id=1, replica_groups=mesh['x'=4,'y'=8,'row'=4,'zhi'=2,'core'=2] {'row','zhi'}, dimensions={0} | all-to-all | bytes 524288 | tf_op jit(solution)/shard_map/all_to_all | solution.py:429
  19.2 4.5 %all-gather = bf16[16,128,128]{2,1,0:T(8,128)(2,1)S(1)} all-gather(bf16[8,128,128]{2,1,0:T(8,128)(2,1)S(1)} %all_to_all.20), channel_id=2, replica_groups=mesh['x'=4,'y'=8,'row'=4,'zhi'=2,'core'=2] {'core'}, dimensions={0}, use_global_device_ids=true | all-gather | bytes 786432 | tf_op jit(solution)/shard_map/all_gather | solution.py:430
  23.6 0.0 copy-done
  23.6 2.2 %block_state.1 = (bf16[32,24,128]{2,1,0:T(8,128)(2,1)S(1)}, f32[8,640]{1,0:T(8,128)S(1)}, bf16[128,2048]{1,0:T(8,128)(2,1)S(1)}, f32[128,128]{1,0:T(8,128)S(1)},...) custom-call(s32[1]{0:T(128)} %bitcast.1.index, ...), custom_call_target="tpu_custom_call" | custom-call | tf_op jit(solution)/shard_map/block_state/pallas_call | solution.py:38
  25.9 0.0 copy-start.1
  25.9 20.2 %all_to_all.21.pieces = bf16[32,24,128]{2,1,0:T(8,128)(2,1)S(1)} all-to-all(bf16[32,24,128]{2,1,0:T(8,128)(2,1)S(1)} %get-tuple-element.50), channel_id=1, replica_groups=mesh['x'=4,'y'=8,'row'=4,'zhi'=2,'core'=2] {'y','x'}, dimensions={0} | all-to-all | bytes 393216 | tf_op jit(solution)/shard_map/all_to_all | solution.py:467
  46.1 1.0 %scan_blocks.1 = (bf16[32,8,128]{2,1,0:T(8,128)(2,1)}, f32[8,128]{1,0:T(8,128)S(1)}) custom-call(s32[1]{0:T(128)} %bitcast.1.index, bf16[32,24,128]{2,1,0:T(8,128)(2,1)S(1)} %all_to_all.21.pieces), custom_call_target="tpu_custom_call" | custom-call | tf_op jit(solution)/shard_map/scan_blocks/pallas_call | solution.py:38
  47.1 4.1 %all-to-all-start.2 = ((bf16[32,8,128]{2,1,0:T(8,128)(2,1)}), bf16[32,8,128]{2,1,0:T(8,128)(2,1)S(1)}, u32[]{:S(2)}, u32[]{:S(2)}) async-start(bf16[32,8,128]{2,1,0:T(8,128)(2,1)} %get-tuple-element.54), calls=%async_computation.2 | async-start | bytes 131072 | tf_op jit(solution)/shard_map/all_to_all | solution.py:475
  51.3 3.1 %collective-permute-start = (f32[8,640]{1,0:T(8,128)S(1)}, f32[8,640]{1,0:T(8,128)S(1)}, u32[]{:S(2)}, u32[]{:S(2)}) collective-permute-start(f32[8,640]{1,0:T(8,128)S(1)} %get-tuple-element.45), channel_id=1, source_target_pairs={{0,16},{16,32},{32,48},{48,64},{64,80},{80,96},{96,112},{112,128},... | collective-permute-start | bytes 61448 | tf_op jit(solution)/shard_map/ppermute | solution.py:466
  54.4 0.0 copy-start.3
  54.4 0.0 copy-done.1
  54.4 0.6 copy-done.3
  55.1 0.3 output_gate.1.gate
  55.4 0.0 copy-start.2
  55.4 0.0 collective-permute-done.edge
  55.4 1.4 %block_attention.1 = (f32[128,128]{1,0:T(8,128)S(1)}, f32[128,256]{1,0:T(8,128)S(1)}) custom-call(f32[128,256]{1,0:T(8,128)S(1)} %get-tuple-element.42.pre_q, f32[128,256]{1,0:T(8,128)S(1)} %get-tuple-element.43.pre_k, f32[128,128]{1,0:T(8,128)S(1)} %get-tuple-element.44.pre_v, f32[8,640]{1,0:T(8,128)S(1)} %collective-permute-done.edge, ...), custom_call_target="tpu_custom_call" | custom-call | tf_op jit(solution)/shard_map/block_attention/pallas_call | solution.py:38
  56.8 3.3 %all-to-all-done.2 = bf16[32,8,128]{2,1,0:T(8,128)(2,1)S(1)} async-done(((bf16[32,8,128]{2,1,0:T(8,128)(2,1)}), bf16[32,8,128]{2,1,0:T(8,128)(2,1)S(1)}, u32[]{:S(2)}, u32[]{:S(2)}) %all-to-all-start.2) | async-done | bytes 65568 | tf_op jit(solution)/shard_map/all_to_all | solution.py:475
  60.1 0.0 copy-done.2
  60.1 0.6 attend.1
  60.7 5.0 %all-gather.1 = bf16[2064,128]{1,0:T(8,128)(2,1)S(1)} all-gather(bf16[1032,128]{1,0:T(8,128)(2,1)S(1)} %get-tuple-element.59), channel_id=3, replica_groups=mesh['x'=4,'y'=8,'row'=4,'zhi'=2,'core'=2] {'core'}, dimensions={0}, use_global_device_ids=true | all-gather | bytes 792576 | tf_op jit(solution)/shard_map/all_gather | solution.py:515
  65.7 0.1 pair_sum.1
  65.8 14.5 %all_to_all.22.received = bf16[8,136,128]{2,1,0:T(8,128)(2,1)S(1)} all-to-all(bf16[8,136,128]{2,1,0:T(8,128)(2,1)S(1)} %pair_sum.1), channel_id=1, replica_groups=mesh['x'=4,'y'=8,'row'=4,'zhi'=2,'core'=2] {'row','zhi'}, dimensions={0} | all-to-all | bytes 557056 | tf_op jit(solution)/shard_map/all_to_all | solution.py:519
  80.3 0.9 %finish.1 = bf16[128,128]{1,0:T(8,128)(2,1)} custom-call(bf16[8,136,128]{2,1,0:T(8,128)(2,1)S(1)} %all_to_all.22.received, bf16[128,128]{1,0:T(8,128)(2,1)S(1)} %get-tuple-element.60.hidden), custom_call_target="tpu_custom_call" | custom-call | tf_op jit(solution)/shard_map/finish/pallas_call | solution.py:38
  (1 shorter events, 0.0 us)
Async XLA Ops:
  0.0 23.6 %copy-start = (bf16[2048,256]{1,0:T(8,128)(2,1)S(1)}, bf16[2048,256]{1,0:T(8,128)(2,1)}, u32[]{:S(2)}) copy-start(bf16[2048,256]{1,0:T(8,128)(2,1)} %w_key.1) | copy-start | bytes 3145732
  25.9 28.5 %copy-start.1 = (bf16[2048,128]{1,0:T(8,128)(2,1)S(1)}, bf16[2048,128]{1,0:T(8,128)(2,1)}, u32[]{:S(2)}) copy-start(bf16[2048,128]{1,0:T(8,128)(2,1)} %w_gate.1) | copy-start | bytes 1572868
  47.1 13.0 %all-to-all-start.2 = ((bf16[32,8,128]{2,1,0:T(8,128)(2,1)}), bf16[32,8,128]{2,1,0:T(8,128)(2,1)S(1)}, u32[]{:S(2)}, u32[]{:S(2)}) async-start(bf16[32,8,128]{2,1,0:T(8,128)(2,1)} %get-tuple-element.54), calls=%async_computation.2 | async-start | bytes 131072 | tf_op jit(solution)/shard_map/all_to_all | solution.py:475
  51.3 4.1 %collective-permute-start = (f32[8,640]{1,0:T(8,128)S(1)}, f32[8,640]{1,0:T(8,128)S(1)}, u32[]{:S(2)}, u32[]{:S(2)}) collective-permute-start(f32[8,640]{1,0:T(8,128)S(1)} %get-tuple-element.45), channel_id=1, source_target_pairs={{0,16},{16,32},{32,48},{48,64},{64,80},{80,96},{96,112},{112,128},... | collective-permute-start | bytes 61448 | tf_op jit(solution)/shard_map/ppermute | solution.py:466
  54.4 0.7 copy-start.3
  55.4 4.7 %copy-start.2 = (bf16[128,2048]{1,0:T(8,128)(2,1)S(1)}, bf16[128,2048]{1,0:T(8,128)(2,1)}, u32[]{:S(2)}) copy-start(bf16[128,2048]{1,0:T(8,128)(2,1)} %w_out.1) | copy-start | bytes 1572868

commit v14 on v13

--- a/solution.py
+++ b/solution.py
@@ -85,7 +85,8 @@
         fetch.start()
     fetches[0].wait()
     for j in range(8):
-        copies[j] = refs[count][...]
+        copies[j, 0:BLOCK, :] = refs[count][...]
+        copies[j, BLOCK:, :] = jnp.zeros((8, CHUNK), BF16)
     for fetch in fetches[1:]:
         fetch.wait()
 
@@ -157,7 +158,7 @@
     squares = jnp.zeros((BLOCK, CHUNK), F32)
     for f in range(WIDTH // CHUNK):
         lanes = slice(f * CHUNK, (f + 1) * CHUNK)
-        activ = whole[f % 2, f // 2].astype(F32)
+        activ = whole[f % 2, f // 2, 0:BLOCK, :].astype(F32)
         squares = squares + activ * activ
         gained[:, lanes] = (activ * gain[:, lanes]).astype(BF16)
     scale = lax.rsqrt(jnp.sum(squares, axis=1, keepdims=True) / WIDTH + 1e-06)
@@ -418,7 +419,7 @@
     )
     hidden, gain, down, up, bias, segs, taps_q, taps_k, taps_v, value_here, copies = local_call(
         fetch_and_spread,
-        [*((a.shape, a.dtype) for a in needed), ((8, BLOCK, CHUNK), BF16)],
+        [*((a.shape, a.dtype) for a in needed), ((8, BLOCK + 8, CHUNK), BF16)],
         block_at,
         core_at,
         *needed,

time: 81.5 us -> 82.6 us (1.013)
  blocking collectives: 62 us -> 63 us
    all_to_all x1, blocking collectives: 17.8 us -> 20.7 us  [shards(): of_core = lax.all_to_all(copies, CHIPS, 0, 0)]
    all_to_all x1, blocking collectives: 14.5 us -> 12.9 us  [shards(): arrived = lax.all_to_all(pairs, CHIPS, 0, 0)]
where the time goes in v14:
time: 82.6 us; the launch traced here: 82.2 us
  blocking collectives  63 us (76%)
  Pallas kernels  7.9 us (10%)
  starting transfers between devices  7.26 us (9%)
  waiting for transfers between devices  3.3 us (4%)
    all_to_all x1, blocking collectives, shards(): of_core = lax.all_to_all(copies, CHIPS, 0, 0)  20.7 us
    all_to_all x1, blocking collectives, shards(): owned = lax.all_to_all(pieces, GRID, 0, 0)  20.2 us
    all_to_all x1, blocking collectives, shards(): arrived = lax.all_to_all(pairs, CHIPS, 0, 0)  12.9 us
    pallas_call x8, Pallas kernels, local_call(): pl.pallas_call(kernel, out_shape=[jax.ShapeDtypeStruct(s, t) if last else...  7.9 us
    all_gather x1, blocking collectives, shards(): both = lax.all_gather(sent, 'core', axis=0)  5 us
    all_gather x1, blocking collectives, shards(): whole = lax.all_gather(of_core, 'core', axis=0)  4.24 us
    all_to_all x1, starting transfers between devices, shards(): incoming = lax.all_to_all(states, GRID, 0, 0).reshape(2, CHUNK, LANES)  4.12 us
    all_to_all x1, waiting for transfers between devices, shards(): incoming = lax.all_to_all(states, GRID, 0, 0).reshape(2, CHUNK, LANES)  3.3 us
  transfers between devices with their start and end apart: 2, of which 1 were waited for; matrix products, arithmetic and copies ran while one was open for 0% of the time, Pallas kernels for 2%

profile of v14, /device:TPU:1, one launch (start us, length us, event | category | flops | bytes accessed | tf_op | source)
XLA Modules:
  0.0 82.2 jit_solution(11847329290141347793)
XLA Ops:
  0.0 1.4 %fetch_and_spread.1 = (bf16[128,128]{1,0:T(8,128)(2,1)S(1)}, f32[1,2048]{1,0:T(1,128)S(1)}, bf16[16,2048]{1,0:T(8,128)(2,1)S(1)}, bf16[16,256]{1,0:T(8,128)(2,1)...) custom-call(s32[1]{0:T(128)} %bitcast.1.index, ...), custom_call_target="tpu_custom_call" | custom-call | tf_op jit(solution)/shard_map/fetch_and_spread/pallas_call | solution.py:38
  1.4 20.7 %all_to_all.20 = bf16[8,136,128]{2,1,0:T(8,128)(2,1)S(1)} all-to-all(bf16[8,136,128]{2,1,0:T(8,128)(2,1)S(1)} %get-tuple-element.33), channel_id=1, replica_groups=mesh['x'=4,'y'=8,'row'=4,'zhi'=2,'core'=2] {'row','zhi'}, dimensions={0} | all-to-all | bytes 557056 | tf_op jit(solution)/shard_map/all_to_all | solution.py:430
  22.0 4.2 %all-gather = bf16[16,136,128]{2,1,0:T(8,128)(2,1)S(1)} all-gather(bf16[8,136,128]{2,1,0:T(8,128)(2,1)S(1)} %all_to_all.20), channel_id=2, replica_groups=mesh['x'=4,'y'=8,'row'=4,'zhi'=2,'core'=2] {'core'}, dimensions={0}, use_global_device_ids=true | all-gather | bytes 835584 | tf_op jit(solution)/shard_map/all_gather | solution.py:431
  26.3 0.0 copy-done
  26.3 2.3 %block_state.1 = (bf16[32,24,128]{2,1,0:T(8,128)(2,1)S(1)}, f32[8,640]{1,0:T(8,128)S(1)}, bf16[128,2048]{1,0:T(8,128)(2,1)S(1)}, f32[128,128]{1,0:T(8,128)S(1)},...) custom-call(s32[1]{0:T(128)} %bitcast.1.index, ...), custom_call_target="tpu_custom_call" | custom-call | tf_op jit(solution)/shard_map/block_state/pallas_call | solution.py:38
  28.5 0.0 copy-start.1
  28.5 20.2 %all_to_all.21.pieces = bf16[32,24,128]{2,1,0:T(8,128)(2,1)S(1)} all-to-all(bf16[32,24,128]{2,1,0:T(8,128)(2,1)S(1)} %get-tuple-element.50), channel_id=1, replica_groups=mesh['x'=4,'y'=8,'row'=4,'zhi'=2,'core'=2] {'y','x'}, dimensions={0} | all-to-all | bytes 393216 | tf_op jit(solution)/shard_map/all_to_all | solution.py:468
  48.7 1.0 %scan_blocks.1 = (bf16[32,8,128]{2,1,0:T(8,128)(2,1)}, f32[8,128]{1,0:T(8,128)S(1)}) custom-call(s32[1]{0:T(128)} %bitcast.1.index, bf16[32,24,128]{2,1,0:T(8,128)(2,1)S(1)} %all_to_all.21.pieces), custom_call_target="tpu_custom_call" | custom-call | tf_op jit(solution)/shard_map/scan_blocks/pallas_call | solution.py:38
  49.8 4.1 %all-to-all-start.2 = ((bf16[32,8,128]{2,1,0:T(8,128)(2,1)}), bf16[32,8,128]{2,1,0:T(8,128)(2,1)S(1)}, u32[]{:S(2)}, u32[]{:S(2)}) async-start(bf16[32,8,128]{2,1,0:T(8,128)(2,1)} %get-tuple-element.54), calls=%async_computation.2 | async-start | bytes 131072 | tf_op jit(solution)/shard_map/all_to_all | solution.py:476
  53.9 3.1 %collective-permute-start = (f32[8,640]{1,0:T(8,128)S(1)}, f32[8,640]{1,0:T(8,128)S(1)}, u32[]{:S(2)}, u32[]{:S(2)}) collective-permute-start(f32[8,640]{1,0:T(8,128)S(1)} %get-tuple-element.45), channel_id=1, source_target_pairs={{0,16},{16,32},{32,48},{48,64},{64,80},{80,96},{96,112},{112,128},... | collective-permute-start | bytes 61448 | tf_op jit(solution)/shard_map/ppermute | solution.py:467
  57.1 0.0 copy-start.3
  57.1 0.0 copy-done.1
  57.1 0.6 copy-done.3
  57.7 0.3 output_gate.1.gate
  58.0 0.0 copy-start.2
  58.0 0.0 collective-permute-done.edge
  58.0 1.4 %block_attention.1 = (f32[128,128]{1,0:T(8,128)S(1)}, f32[128,256]{1,0:T(8,128)S(1)}) custom-call(f32[128,256]{1,0:T(8,128)S(1)} %get-tuple-element.42.pre_q, f32[128,256]{1,0:T(8,128)S(1)} %get-tuple-element.43.pre_k, f32[128,128]{1,0:T(8,128)S(1)} %get-tuple-element.44.pre_v, f32[8,640]{1,0:T(8,128)S(1)} %collective-permute-done.edge, ...), custom_call_target="tpu_custom_call" | custom-call | tf_op jit(solution)/shard_map/block_attention/pallas_call | solution.py:38
  59.4 3.3 %all-to-all-done.2 = bf16[32,8,128]{2,1,0:T(8,128)(2,1)S(1)} async-done(((bf16[32,8,128]{2,1,0:T(8,128)(2,1)}), bf16[32,8,128]{2,1,0:T(8,128)(2,1)S(1)}, u32[]{:S(2)}, u32[]{:S(2)}) %all-to-all-start.2) | async-done | bytes 65568 | tf_op jit(solution)/shard_map/all_to_all | solution.py:476
  62.7 0.0 copy-done.2
  62.7 0.6 attend.1
  63.4 5.0 %all-gather.1 = bf16[2064,128]{1,0:T(8,128)(2,1)S(1)} all-gather(bf16[1032,128]{1,0:T(8,128)(2,1)S(1)} %get-tuple-element.59), channel_id=3, replica_groups=mesh['x'=4,'y'=8,'row'=4,'zhi'=2,'core'=2] {'core'}, dimensions={0}, use_global_device_ids=true | all-gather | bytes 792576 | tf_op jit(solution)/shard_map/all_gather | solution.py:516
  68.4 0.1 pair_sum.1
  68.4 12.9 %all_to_all.22.received = bf16[8,136,128]{2,1,0:T(8,128)(2,1)S(1)} all-to-all(bf16[8,136,128]{2,1,0:T(8,128)(2,1)S(1)} %pair_sum.1), channel_id=1, replica_groups=mesh['x'=4,'y'=8,'row'=4,'zhi'=2,'core'=2] {'row','zhi'}, dimensions={0} | all-to-all | bytes 557056 | tf_op jit(solution)/shard_map/all_to_all | solution.py:520
  81.3 0.9 %finish.1 = bf16[128,128]{1,0:T(8,128)(2,1)} custom-call(bf16[8,136,128]{2,1,0:T(8,128)(2,1)S(1)} %all_to_all.22.received, bf16[128,128]{1,0:T(8,128)(2,1)S(1)} %get-tuple-element.60.hidden), custom_call_target="tpu_custom_call" | custom-call | tf_op jit(solution)/shard_map/finish/pallas_call | solution.py:38
  (1 shorter events, 0.0 us)
Async XLA Ops:
  0.0 26.3 %copy-start = (bf16[2048,256]{1,0:T(8,128)(2,1)S(1)}, bf16[2048,256]{1,0:T(8,128)(2,1)}, u32[]{:S(2)}) copy-start(bf16[2048,256]{1,0:T(8,128)(2,1)} %w_key.1) | copy-start | bytes 3145732
  28.5 28.5 %copy-start.1 = (bf16[2048,128]{1,0:T(8,128)(2,1)S(1)}, bf16[2048,128]{1,0:T(8,128)(2,1)}, u32[]{:S(2)}) copy-start(bf16[2048,128]{1,0:T(8,128)(2,1)} %w_gate.1) | copy-start | bytes 1572868
  49.8 13.0 %all-to-all-start.2 = ((bf16[32,8,128]{2,1,0:T(8,128)(2,1)}), bf16[32,8,128]{2,1,0:T(8,128)(2,1)S(1)}, u32[]{:S(2)}, u32[]{:S(2)}) async-start(bf16[32,8,128]{2,1,0:T(8,128)(2,1)} %get-tuple-element.54), calls=%async_computation.2 | async-start | bytes 131072 | tf_op jit(solution)/shard_map/all_to_all | solution.py:476
  53.9 4.1 %collective-permute-start = (f32[8,640]{1,0:T(8,128)S(1)}, f32[8,640]{1,0:T(8,128)S(1)}, u32[]{:S(2)}, u32[]{:S(2)}) collective-permute-start(f32[8,640]{1,0:T(8,128)S(1)} %get-tuple-element.45), channel_id=1, source_target_pairs={{0,16},{16,32},{32,48},{48,64},{64,80},{80,96},{96,112},{112,128},... | collective-permute-start | bytes 61448 | tf_op jit(solution)/shard_map/ppermute | solution.py:467
  57.1 0.7 copy-start.3
  58.0 4.7 %copy-start.2 = (bf16[128,2048]{1,0:T(8,128)(2,1)S(1)}, bf16[128,2048]{1,0:T(8,128)(2,1)}, u32[]{:S(2)}) copy-start(bf16[128,2048]{1,0:T(8,128)(2,1)} %w_out.1) | copy-start | bytes 1572868

commit v15 on v13

--- a/solution.py
+++ b/solution.py
@@ -128,9 +128,9 @@
     index,
     whole,
     gain,
+    value_hbm,
     query_hbm,
     w_key,
-    w_value,
     w_down,
     w_up,
     bias,
@@ -149,11 +149,14 @@
     own_rows,
     extended_k,
     extended_v,
+    w_value,
     w_query,
     arrived,
 ):
-    fetch = pltpu.make_async_copy(query_hbm, w_query, arrived.at[0])
-    fetch.start()
+    fetch_value = pltpu.make_async_copy(value_hbm, w_value, arrived.at[0])
+    fetch_query = pltpu.make_async_copy(query_hbm, w_query, arrived.at[1])
+    fetch_value.start()
+    fetch_query.start()
     squares = jnp.zeros((BLOCK, CHUNK), F32)
     for f in range(WIDTH // CHUNK):
         lanes = slice(f * CHUNK, (f + 1) * CHUNK)
@@ -193,6 +196,7 @@
     cumulated[...] = cum
 
     of_keys = dot(rows, w_key[...]) * scale
+    fetch_value.wait()
     of_values = dot(rows, w_value[...]) * scale
     pre_k[...] = of_keys
     pre_v[...] = of_values
@@ -234,7 +238,7 @@
                 pieces[p, 0:PIECE, :] = state[g * PIECE : (g + 1) * PIECE, lanes].astype(BF16)
                 pieces[p, PIECE : PIECE + 8, :] = tile_b
                 pieces[p, PIECE + 8 :, :] = tile_c
-    fetch.wait()
+    fetch_query.wait()
     of_queries = dot(rows, w_query[...]) * scale
     pre_q[...] = of_queries
     tail[:, :HEAD_K] = of_queries[BLOCK - 8 :, :]
@@ -414,9 +418,8 @@
         conv_query,
         conv_key,
         conv_value,
-        w_value,
-    )
-    hidden, gain, down, up, bias, segs, taps_q, taps_k, taps_v, value_here, copies = local_call(
+    )
+    hidden, gain, down, up, bias, segs, taps_q, taps_k, taps_v, copies = local_call(
         fetch_and_spread,
         [*((a.shape, a.dtype) for a in needed), ((8, BLOCK, CHUNK), BF16)],
         block_at,
@@ -445,9 +448,9 @@
         block_at,
         whole,
         gain,
+        w_value,
         w_query,
         w_key,
-        value_here,
         down,
         up,
         bias,
@@ -457,11 +460,12 @@
         scratch=[
             pltpu.VMEM((BLOCK + 8, HEAD_K), F32),
             pltpu.VMEM((BLOCK + 8, CHUNK), F32),
+            pltpu.VMEM((WIDTH, CHUNK), BF16),
             pltpu.VMEM((WIDTH, HEAD_K), BF16),
-            pltpu.SemaphoreType.DMA((1,)),
+            pltpu.SemaphoreType.DMA((2,)),
         ],
         scalars=1,
-        anywhere=(3,),
+        anywhere=(3, 4),
     )
     edge = lax.ppermute(tail, SEQ, [(i, i + 1) for i in range(BLOCKS - 1)])
     owned = lax.all_to_all(pieces, GRID, 0, 0)

time: 81.5 us -> 81.4 us (level)
  no operation moved by 1% of the time
where the time goes in v15:
time: 81.4 us; the launch traced here: 81 us
  blocking collectives  62 us (76%)
  Pallas kernels  7.74 us (10%)
  starting transfers between devices  7.26 us (9%)
  waiting for transfers between devices  3.3 us (4%)
    all_to_all x1, blocking collectives, shards(): owned = lax.all_to_all(pieces, GRID, 0, 0)  20.2 us
    all_to_all x1, blocking collectives, shards(): of_core = lax.all_to_all(copies, CHIPS, 0, 0)  17.8 us
    all_to_all x1, blocking collectives, shards(): arrived = lax.all_to_all(pairs, CHIPS, 0, 0)  14.5 us
    pallas_call x8, Pallas kernels, local_call(): pl.pallas_call(kernel, out_shape=[jax.ShapeDtypeStruct(s, t) if last else...  7.74 us
    all_gather x1, blocking collectives, shards(): both = lax.all_gather(sent, 'core', axis=0)  5 us
    all_gather x1, blocking collectives, shards(): whole = lax.all_gather(of_core, 'core', axis=0)  4.46 us
    all_to_all x1, starting transfers between devices, shards(): incoming = lax.all_to_all(states, GRID, 0, 0).reshape(2, CHUNK, LANES)  4.12 us
    all_to_all x1, waiting for transfers between devices, shards(): incoming = lax.all_to_all(states, GRID, 0, 0).reshape(2, CHUNK, LANES)  3.3 us
  transfers between devices with their start and end apart: 2, of which 1 were waited for; matrix products, arithmetic and copies ran while one was open for 0% of the time, Pallas kernels for 2%

profile of v15, /device:TPU:1, one launch (start us, length us, event | category | flops | bytes accessed | tf_op | source)
XLA Modules:
  0.0 81.0 jit_solution(1350714372397915448)
XLA Ops:
  0.0 1.0 %fetch_and_spread.1 = (bf16[128,128]{1,0:T(8,128)(2,1)S(1)}, f32[1,2048]{1,0:T(1,128)S(1)}, bf16[16,2048]{1,0:T(8,128)(2,1)S(1)}, bf16[16,256]{1,0:T(8,128)(2,1)...) custom-call(s32[1]{0:T(128)} %bitcast.1.index, ...), custom_call_target="tpu_custom_call" | custom-call | tf_op jit(solution)/shard_map/fetch_and_spread/pallas_call | solution.py:38
  1.1 17.8 %all_to_all.20 = bf16[8,128,128]{2,1,0:T(8,128)(2,1)S(1)} all-to-all(bf16[8,128,128]{2,1,0:T(8,128)(2,1)S(1)} %get-tuple-element.32), channel_id=1, replica_groups=mesh['x'=4,'y'=8,'row'=4,'zhi'=2,'core'=2] {'row','zhi'}, dimensions={0} | all-to-all | bytes 524288 | tf_op jit(solution)/shard_map/all_to_all | solution.py:432
  18.9 4.5 %all-gather = bf16[16,128,128]{2,1,0:T(8,128)(2,1)S(1)} all-gather(bf16[8,128,128]{2,1,0:T(8,128)(2,1)S(1)} %all_to_all.20), channel_id=2, replica_groups=mesh['x'=4,'y'=8,'row'=4,'zhi'=2,'core'=2] {'core'}, dimensions={0}, use_global_device_ids=true | all-gather | bytes 786432 | tf_op jit(solution)/shard_map/all_gather | solution.py:433
  23.3 0.0 copy-done
  23.3 2.4 %block_state.1 = (bf16[32,24,128]{2,1,0:T(8,128)(2,1)S(1)}, f32[8,640]{1,0:T(8,128)S(1)}, bf16[128,2048]{1,0:T(8,128)(2,1)S(1)}, f32[128,128]{1,0:T(8,128)S(1)},...) custom-call(s32[1]{0:T(128)} %bitcast.1.index, ...), custom_call_target="tpu_custom_call" | custom-call | tf_op jit(solution)/shard_map/block_state/pallas_call | solution.py:38
  25.7 0.0 copy-start.1
  25.7 20.2 %all_to_all.21.pieces = bf16[32,24,128]{2,1,0:T(8,128)(2,1)S(1)} all-to-all(bf16[32,24,128]{2,1,0:T(8,128)(2,1)S(1)} %get-tuple-element.48), channel_id=1, replica_groups=mesh['x'=4,'y'=8,'row'=4,'zhi'=2,'core'=2] {'y','x'}, dimensions={0} | all-to-all | bytes 393216 | tf_op jit(solution)/shard_map/all_to_all | solution.py:471
  45.9 1.0 %scan_blocks.1 = (bf16[32,8,128]{2,1,0:T(8,128)(2,1)}, f32[8,128]{1,0:T(8,128)S(1)}) custom-call(s32[1]{0:T(128)} %bitcast.1.index, bf16[32,24,128]{2,1,0:T(8,128)(2,1)S(1)} %all_to_all.21.pieces), custom_call_target="tpu_custom_call" | custom-call | tf_op jit(solution)/shard_map/scan_blocks/pallas_call | solution.py:38
  47.0 4.1 %all-to-all-start.2 = ((bf16[32,8,128]{2,1,0:T(8,128)(2,1)}), bf16[32,8,128]{2,1,0:T(8,128)(2,1)S(1)}, u32[]{:S(2)}, u32[]{:S(2)}) async-start(bf16[32,8,128]{2,1,0:T(8,128)(2,1)} %get-tuple-element.52), calls=%async_computation.2 | async-start | bytes 131072 | tf_op jit(solution)/shard_map/all_to_all | solution.py:479
  51.1 3.1 %collective-permute-start = (f32[8,640]{1,0:T(8,128)S(1)}, f32[8,640]{1,0:T(8,128)S(1)}, u32[]{:S(2)}, u32[]{:S(2)}) collective-permute-start(f32[8,640]{1,0:T(8,128)S(1)} %get-tuple-element.43), channel_id=1, source_target_pairs={{0,16},{16,32},{32,48},{48,64},{64,80},{80,96},{96,112},{112,128},... | collective-permute-start | bytes 61448 | tf_op jit(solution)/shard_map/ppermute | solution.py:470
  54.3 0.0 copy-start.3
  54.3 0.0 copy-done.1
  54.3 0.6 copy-done.3
  54.9 0.3 output_gate.1.gate
  55.2 0.0 copy-start.2
  55.2 0.0 collective-permute-done.edge
  55.2 1.4 %block_attention.1 = (f32[128,128]{1,0:T(8,128)S(1)}, f32[128,256]{1,0:T(8,128)S(1)}) custom-call(f32[128,256]{1,0:T(8,128)S(1)} %get-tuple-element.40.pre_q, f32[128,256]{1,0:T(8,128)S(1)} %get-tuple-element.41.pre_k, f32[128,128]{1,0:T(8,128)S(1)} %get-tuple-element.42.pre_v, f32[8,640]{1,0:T(8,128)S(1)} %collective-permute-done.edge, ...), custom_call_target="tpu_custom_call" | custom-call | tf_op jit(solution)/shard_map/block_attention/pallas_call | solution.py:38
  56.6 3.3 %all-to-all-done.2 = bf16[32,8,128]{2,1,0:T(8,128)(2,1)S(1)} async-done(((bf16[32,8,128]{2,1,0:T(8,128)(2,1)}), bf16[32,8,128]{2,1,0:T(8,128)(2,1)S(1)}, u32[]{:S(2)}, u32[]{:S(2)}) %all-to-all-start.2) | async-done | bytes 65568 | tf_op jit(solution)/shard_map/all_to_all | solution.py:479
  59.9 0.0 copy-done.2
  59.9 0.6 attend.1
  60.6 5.0 %all-gather.1 = bf16[2064,128]{1,0:T(8,128)(2,1)S(1)} all-gather(bf16[1032,128]{1,0:T(8,128)(2,1)S(1)} %get-tuple-element.57), channel_id=3, replica_groups=mesh['x'=4,'y'=8,'row'=4,'zhi'=2,'core'=2] {'core'}, dimensions={0}, use_global_device_ids=true | all-gather | bytes 792576 | tf_op jit(solution)/shard_map/all_gather | solution.py:519
  65.6 0.1 pair_sum.1
  65.6 14.5 %all_to_all.22.received = bf16[8,136,128]{2,1,0:T(8,128)(2,1)S(1)} all-to-all(bf16[8,136,128]{2,1,0:T(8,128)(2,1)S(1)} %pair_sum.1), channel_id=1, replica_groups=mesh['x'=4,'y'=8,'row'=4,'zhi'=2,'core'=2] {'row','zhi'}, dimensions={0} | all-to-all | bytes 557056 | tf_op jit(solution)/shard_map/all_to_all | solution.py:523
  80.1 0.9 %finish.1 = bf16[128,128]{1,0:T(8,128)(2,1)} custom-call(bf16[8,136,128]{2,1,0:T(8,128)(2,1)S(1)} %all_to_all.22.received, bf16[128,128]{1,0:T(8,128)(2,1)S(1)} %get-tuple-element.58.hidden), custom_call_target="tpu_custom_call" | custom-call | tf_op jit(solution)/shard_map/finish/pallas_call | solution.py:38
  (1 shorter events, 0.0 us)
Async XLA Ops:
  0.0 23.3 %copy-start = (bf16[2048,256]{1,0:T(8,128)(2,1)S(1)}, bf16[2048,256]{1,0:T(8,128)(2,1)}, u32[]{:S(2)}) copy-start(bf16[2048,256]{1,0:T(8,128)(2,1)} %w_key.1) | copy-start | bytes 3145732
  25.7 28.5 %copy-start.1 = (bf16[2048,128]{1,0:T(8,128)(2,1)S(1)}, bf16[2048,128]{1,0:T(8,128)(2,1)}, u32[]{:S(2)}) copy-start(bf16[2048,128]{1,0:T(8,128)(2,1)} %w_gate.1) | copy-start | bytes 1572868
  47.0 13.0 %all-to-all-start.2 = ((bf16[32,8,128]{2,1,0:T(8,128)(2,1)}), bf16[32,8,128]{2,1,0:T(8,128)(2,1)S(1)}, u32[]{:S(2)}, u32[]{:S(2)}) async-start(bf16[32,8,128]{2,1,0:T(8,128)(2,1)} %get-tuple-element.52), calls=%async_computation.2 | async-start | bytes 131072 | tf_op jit(solution)/shard_map/all_to_all | solution.py:479
  51.1 4.1 %collective-permute-start = (f32[8,640]{1,0:T(8,128)S(1)}, f32[8,640]{1,0:T(8,128)S(1)}, u32[]{:S(2)}, u32[]{:S(2)}) collective-permute-start(f32[8,640]{1,0:T(8,128)S(1)} %get-tuple-element.43), channel_id=1, source_target_pairs={{0,16},{16,32},{32,48},{48,64},{64,80},{80,96},{96,112},{112,128},... | collective-permute-start | bytes 61448 | tf_op jit(solution)/shard_map/ppermute | solution.py:470
  54.3 0.7 copy-start.3
  55.2 4.7 %copy-start.2 = (bf16[128,2048]{1,0:T(8,128)(2,1)S(1)}, bf16[128,2048]{1,0:T(8,128)(2,1)}, u32[]{:S(2)}) copy-start(bf16[128,2048]{1,0:T(8,128)(2,1)} %w_out.1) | copy-start | bytes 1572868

commit v16 on v15

--- a/solution.py
+++ b/solution.py
@@ -7,7 +7,6 @@
 
 F32 = jnp.float32
 BF16 = jnp.bfloat16
-HIGHEST = lax.Precision.HIGHEST
 HEAD_V = 512
 WIDTH = 2048
 BLOCK = 128
@@ -49,13 +48,19 @@
     )(*args)
 
 
-def dot(a, b, dims=(((1,), (0,)), ((), ())), precision=None):
-    return lax.dot_general(a, b, dims, precision=precision, preferred_element_type=F32)
+def dot(a, b, dims=(((1,), (0,)), ((), ()))):
+    return lax.dot_general(a, b, dims, preferred_element_type=F32)
 
 
 def halves(value):
     high = value.astype(BF16)
     return high, (value - high.astype(F32)).astype(BF16)
+
+
+def thirds(value):
+    high, _ = halves(value)
+    middle, low = halves(value - high.astype(F32))
+    return high, middle, low
 
 
 def pair_rows(value):
@@ -187,12 +192,16 @@
     columns_out[...] = columns
     own_rows[...] = own
 
-    logits = dot(rank_part, w_up[...].astype(F32), precision=HIGHEST) + bias[...]
+    logits = bias[...]
+    for part in thirds(rank_part):
+        logits = logits + dot(part, w_up[...])
     log_decay = (jnp.minimum(logits, 0.0) - jnp.log(1.0 + jnp.exp(-jnp.abs(logits)))) / 16.0
     row_iota = lax.broadcasted_iota(jnp.int32, (BLOCK, BLOCK), 0)
     col_iota = lax.broadcasted_iota(jnp.int32, (BLOCK, BLOCK), 1)
-    lower = jnp.where(row_iota >= col_iota, 1.0, 0.0).astype(F32)
-    cum = dot(lower, log_decay, precision=HIGHEST)
+    lower = jnp.where(row_iota >= col_iota, 1.0, 0.0).astype(BF16)
+    cum = dot(
+        jnp.concatenate([lower] * 3, axis=1), jnp.concatenate(thirds(log_decay), axis=0)
+    )
     cumulated[...] = cum
 
     of_keys = dot(rows, w_key[...]) * scale
@@ -348,7 +357,8 @@
     high, low = halves(reach[...])
     state = jnp.concatenate([incoming[0], incoming[1]], axis=1)
     attended = intra[...] + dot(high, state, LAST) + dot(low, state, LAST)
-    squares = dot(jnp.ones((8, CHUNK), F32), attended * attended, LAST, precision=HIGHEST)
+    ones = jnp.ones((8, CHUNK), BF16)
+    squares = sum(dot(ones, part, LAST) for part in thirds(attended * attended))
     terms = dot((attended * gate[...]).astype(BF16), w_out[...])
     first = index[0] == 0
     for j in range(8):

time: 81.4 us -> 81.6 us (level)
  no operation moved by 1% of the time
where the time goes in v16:
time: 81.6 us; the launch traced here: 81.3 us
  blocking collectives  62 us (76%)
  Pallas kernels  7.99 us (10%)
  starting transfers between devices  7.26 us (9%)
  waiting for transfers between devices  3.3 us (4%)
    all_to_all x1, blocking collectives, shards(): owned = lax.all_to_all(pieces, GRID, 0, 0)  20.2 us
    all_to_all x1, blocking collectives, shards(): of_core = lax.all_to_all(copies, CHIPS, 0, 0)  17.8 us
    all_to_all x1, blocking collectives, shards(): arrived = lax.all_to_all(pairs, CHIPS, 0, 0)  14.5 us
    pallas_call x8, Pallas kernels, local_call(): pl.pallas_call(kernel, out_shape=[jax.ShapeDtypeStruct(s, t) if last else...  7.99 us
    all_gather x1, blocking collectives, shards(): both = lax.all_gather(sent, 'core', axis=0)  5 us
    all_gather x1, blocking collectives, shards(): whole = lax.all_gather(of_core, 'core', axis=0)  4.46 us
    all_to_all x1, starting transfers between devices, shards(): incoming = lax.all_to_all(states, GRID, 0, 0).reshape(2, CHUNK, LANES)  4.13 us
    all_to_all x1, waiting for transfers between devices, shards(): incoming = lax.all_to_all(states, GRID, 0, 0).reshape(2, CHUNK, LANES)  3.3 us
  transfers between devices with their start and end apart: 2, of which 1 were waited for; matrix products, arithmetic and copies ran while one was open for 0% of the time, Pallas kernels for 2%

profile of v16, /device:TPU:1, one launch (start us, length us, event | category | flops | bytes accessed | tf_op | source)
XLA Modules:
  0.0 81.3 jit_solution(3258855449652849616)
XLA Ops:
  0.0 1.0 %fetch_and_spread.1 = (bf16[128,128]{1,0:T(8,128)(2,1)S(1)}, f32[1,2048]{1,0:T(1,128)S(1)}, bf16[16,2048]{1,0:T(8,128)(2,1)S(1)}, bf16[16,256]{1,0:T(8,128)(2,1)...) custom-call(s32[1]{0:T(128)} %bitcast.1.index, ...), custom_call_target="tpu_custom_call" | custom-call | tf_op jit(solution)/shard_map/fetch_and_spread/pallas_call | solution.py:37
  1.1 17.8 %all_to_all.20 = bf16[8,128,128]{2,1,0:T(8,128)(2,1)S(1)} all-to-all(bf16[8,128,128]{2,1,0:T(8,128)(2,1)S(1)} %get-tuple-element.32), channel_id=1, replica_groups=mesh['x'=4,'y'=8,'row'=4,'zhi'=2,'core'=2] {'row','zhi'}, dimensions={0} | all-to-all | bytes 524288 | tf_op jit(solution)/shard_map/all_to_all | solution.py:442
  18.9 4.5 %all-gather = bf16[16,128,128]{2,1,0:T(8,128)(2,1)S(1)} all-gather(bf16[8,128,128]{2,1,0:T(8,128)(2,1)S(1)} %all_to_all.20), channel_id=2, replica_groups=mesh['x'=4,'y'=8,'row'=4,'zhi'=2,'core'=2] {'core'}, dimensions={0}, use_global_device_ids=true | all-gather | bytes 786432 | tf_op jit(solution)/shard_map/all_gather | solution.py:443
  23.3 0.0 copy-done
  23.3 2.7 %block_state.1 = (bf16[32,24,128]{2,1,0:T(8,128)(2,1)S(1)}, f32[8,640]{1,0:T(8,128)S(1)}, bf16[128,2048]{1,0:T(8,128)(2,1)S(1)}, f32[128,128]{1,0:T(8,128)S(1)},...) custom-call(s32[1]{0:T(128)} %bitcast.1.index, ...), custom_call_target="tpu_custom_call" | custom-call | tf_op jit(solution)/shard_map/block_state/pallas_call | solution.py:37
  26.0 0.0 copy-start.1
  26.0 20.2 %all_to_all.21.pieces = bf16[32,24,128]{2,1,0:T(8,128)(2,1)S(1)} all-to-all(bf16[32,24,128]{2,1,0:T(8,128)(2,1)S(1)} %get-tuple-element.48), channel_id=1, replica_groups=mesh['x'=4,'y'=8,'row'=4,'zhi'=2,'core'=2] {'y','x'}, dimensions={0} | all-to-all | bytes 393216 | tf_op jit(solution)/shard_map/all_to_all | solution.py:481
  46.2 1.0 %scan_blocks.1 = (bf16[32,8,128]{2,1,0:T(8,128)(2,1)}, f32[8,128]{1,0:T(8,128)S(1)}) custom-call(s32[1]{0:T(128)} %bitcast.1.index, bf16[32,24,128]{2,1,0:T(8,128)(2,1)S(1)} %all_to_all.21.pieces), custom_call_target="tpu_custom_call" | custom-call | tf_op jit(solution)/shard_map/scan_blocks/pallas_call | solution.py:37
  47.3 4.1 %all-to-all-start.2 = ((bf16[32,8,128]{2,1,0:T(8,128)(2,1)}), bf16[32,8,128]{2,1,0:T(8,128)(2,1)S(1)}, u32[]{:S(2)}, u32[]{:S(2)}) async-start(bf16[32,8,128]{2,1,0:T(8,128)(2,1)} %get-tuple-element.52), calls=%async_computation.2 | async-start | bytes 131072 | tf_op jit(solution)/shard_map/all_to_all | solution.py:489
  51.4 3.1 %collective-permute-start = (f32[8,640]{1,0:T(8,128)S(1)}, f32[8,640]{1,0:T(8,128)S(1)}, u32[]{:S(2)}, u32[]{:S(2)}) collective-permute-start(f32[8,640]{1,0:T(8,128)S(1)} %get-tuple-element.43), channel_id=1, source_target_pairs={{0,16},{16,32},{32,48},{48,64},{64,80},{80,96},{96,112},{112,128},... | collective-permute-start | bytes 61448 | tf_op jit(solution)/shard_map/ppermute | solution.py:480
  54.6 0.0 copy-start.3
  54.6 0.0 copy-done.1
  54.6 0.6 copy-done.3
  55.2 0.3 output_gate.1.gate
  55.5 0.0 copy-start.2
  55.5 0.0 collective-permute-done.edge
  55.5 1.4 %block_attention.1 = (f32[128,128]{1,0:T(8,128)S(1)}, f32[128,256]{1,0:T(8,128)S(1)}) custom-call(f32[128,256]{1,0:T(8,128)S(1)} %get-tuple-element.40.pre_q, f32[128,256]{1,0:T(8,128)S(1)} %get-tuple-element.41.pre_k, f32[128,128]{1,0:T(8,128)S(1)} %get-tuple-element.42.pre_v, f32[8,640]{1,0:T(8,128)S(1)} %collective-permute-done.edge, ...), custom_call_target="tpu_custom_call" | custom-call | tf_op jit(solution)/shard_map/block_attention/pallas_call | solution.py:37
  56.9 3.3 %all-to-all-done.2 = bf16[32,8,128]{2,1,0:T(8,128)(2,1)S(1)} async-done(((bf16[32,8,128]{2,1,0:T(8,128)(2,1)}), bf16[32,8,128]{2,1,0:T(8,128)(2,1)S(1)}, u32[]{:S(2)}, u32[]{:S(2)}) %all-to-all-start.2) | async-done | bytes 65568 | tf_op jit(solution)/shard_map/all_to_all | solution.py:489
  60.2 0.0 copy-done.2
  60.2 0.5 attend.1
  60.8 5.0 %all-gather.1 = bf16[2064,128]{1,0:T(8,128)(2,1)S(1)} all-gather(bf16[1032,128]{1,0:T(8,128)(2,1)S(1)} %get-tuple-element.57), channel_id=3, replica_groups=mesh['x'=4,'y'=8,'row'=4,'zhi'=2,'core'=2] {'core'}, dimensions={0}, use_global_device_ids=true | all-gather | bytes 792576 | tf_op jit(solution)/shard_map/all_gather | solution.py:529
  65.8 0.1 pair_sum.1
  65.9 14.5 %all_to_all.22.received = bf16[8,136,128]{2,1,0:T(8,128)(2,1)S(1)} all-to-all(bf16[8,136,128]{2,1,0:T(8,128)(2,1)S(1)} %pair_sum.1), channel_id=1, replica_groups=mesh['x'=4,'y'=8,'row'=4,'zhi'=2,'core'=2] {'row','zhi'}, dimensions={0} | all-to-all | bytes 557056 | tf_op jit(solution)/shard_map/all_to_all | solution.py:533
  80.4 0.9 %finish.1 = bf16[128,128]{1,0:T(8,128)(2,1)} custom-call(bf16[8,136,128]{2,1,0:T(8,128)(2,1)S(1)} %all_to_all.22.received, bf16[128,128]{1,0:T(8,128)(2,1)S(1)} %get-tuple-element.58.hidden), custom_call_target="tpu_custom_call" | custom-call | tf_op jit(solution)/shard_map/finish/pallas_call | solution.py:37
  (1 shorter events, 0.0 us)
Async XLA Ops:
  0.0 23.3 %copy-start = (bf16[2048,256]{1,0:T(8,128)(2,1)S(1)}, bf16[2048,256]{1,0:T(8,128)(2,1)}, u32[]{:S(2)}) copy-start(bf16[2048,256]{1,0:T(8,128)(2,1)} %w_key.1) | copy-start | bytes 3145732
  26.0 28.5 %copy-start.1 = (bf16[2048,128]{1,0:T(8,128)(2,1)S(1)}, bf16[2048,128]{1,0:T(8,128)(2,1)}, u32[]{:S(2)}) copy-start(bf16[2048,128]{1,0:T(8,128)(2,1)} %w_gate.1) | copy-start | bytes 1572868
  47.3 13.0 %all-to-all-start.2 = ((bf16[32,8,128]{2,1,0:T(8,128)(2,1)}), bf16[32,8,128]{2,1,0:T(8,128)(2,1)S(1)}, u32[]{:S(2)}, u32[]{:S(2)}) async-start(bf16[32,8,128]{2,1,0:T(8,128)(2,1)} %get-tuple-element.52), calls=%async_computation.2 | async-start | bytes 131072 | tf_op jit(solution)/shard_map/all_to_all | solution.py:489
  51.4 4.1 %collective-permute-start = (f32[8,640]{1,0:T(8,128)S(1)}, f32[8,640]{1,0:T(8,128)S(1)}, u32[]{:S(2)}, u32[]{:S(2)}) collective-permute-start(f32[8,640]{1,0:T(8,128)S(1)} %get-tuple-element.43), channel_id=1, source_target_pairs={{0,16},{16,32},{32,48},{48,64},{64,80},{80,96},{96,112},{112,128},... | collective-permute-start | bytes 61448 | tf_op jit(solution)/shard_map/ppermute | solution.py:480
  54.6 0.7 copy-start.3
  55.5 4.7 %copy-start.2 = (bf16[128,2048]{1,0:T(8,128)(2,1)S(1)}, bf16[128,2048]{1,0:T(8,128)(2,1)}, u32[]{:S(2)}) copy-start(bf16[128,2048]{1,0:T(8,128)(2,1)} %w_out.1) | copy-start | bytes 1572868

commit v17 on v15

--- a/solution.py
+++ b/solution.py
@@ -241,13 +241,30 @@
     fetch_query.wait()
     of_queries = dot(rows, w_query[...]) * scale
     pre_q[...] = of_queries
-    tail[:, :HEAD_K] = of_queries[BLOCK - 8 :, :]
-    tail[:, HEAD_K : 2 * HEAD_K] = of_keys[BLOCK - 8 :, :]
-    tail[:, 2 * HEAD_K :] = of_values[BLOCK - 8 :, :]
-
-
-def output_gate(gained, row_scale, w_gate, head_gain, left, gate):
+    tail[:, :HEAD_K] = of_queries[BLOCK - 8 :, :].astype(BF16)
+    tail[:, HEAD_K : 2 * HEAD_K] = of_keys[BLOCK - 8 :, :].astype(BF16)
+    tail[:, 2 * HEAD_K :] = of_values[BLOCK - 8 :, :].astype(BF16)
+
+
+HALVES = (8, 16, 32, 64)
+GROUPS = (BLOCK // 8, 8, HEAD_K)
+
+
+def ahead(gained, row_scale, w_gate, head_gain, cumulated, left, gate, factors):
     del left
+    cum = cumulated[...]
+    for i, half in enumerate(HALVES):
+        anchors = [
+            jnp.broadcast_to(cum[b + half - 1 : b + half, :], (2 * half, HEAD_K))
+            for b in range(0, BLOCK, 2 * half)
+        ]
+        anchor = jnp.concatenate(anchors, axis=0) if len(anchors) > 1 else anchors[0]
+        factors[i] = jnp.exp(-jnp.abs(cum - anchor))
+    cum_g = cum.reshape(GROUPS)
+    for by in range(1, 8):
+        spread = jnp.minimum(cum_g - pltpu.roll(cum_g, by, 1), 0.0)
+        factors[3 + by] = jnp.exp(spread).reshape(BLOCK, HEAD_K)
+    factors[11] = jnp.exp(cum)
     gate[...] = silu(dot(gained[...], w_gate[...]) * row_scale[...]) * head_gain[...]
 
 
@@ -259,7 +276,7 @@
     taps_q,
     taps_k,
     taps_v,
-    cumulated,
+    factors,
     columns,
     own_rows,
     left,
@@ -269,25 +286,20 @@
     extended_v,
 ):
     del left
-    edges = edge[...]
+    edges = edge[...].astype(F32)
     queries = silu(conv(pre_q[...], edges[:, :HEAD_K], taps_q, extended.at[0], columns))
     queries = queries * HEAD_K ** (-0.5)
     keys = silu(
         conv(pre_k[...], edges[:, HEAD_K : 2 * HEAD_K], taps_k, extended.at[1], columns)
     )
     values = silu(conv(pre_v[...], edges[:, 2 * HEAD_K :], taps_v, extended_v, columns))
-    cum, seg = cumulated[...], columns[:, 0:1]
+    seg = columns[:, 0:1]
     row_iota = lax.broadcasted_iota(jnp.int32, (BLOCK, BLOCK), 0)
     col_iota = lax.broadcasted_iota(jnp.int32, (BLOCK, BLOCK), 1)
-    reach[...] = jnp.where(seg == columns[:, 32:33], queries * jnp.exp(cum), 0.0)
+    reach[...] = jnp.where(seg == columns[:, 32:33], queries * factors[11], 0.0)
     weights = jnp.zeros((BLOCK, BLOCK), F32)
-    for half in (8, 16, 32, 64):
-        anchors = [
-            jnp.broadcast_to(cum[b + half - 1 : b + half, :], (2 * half, HEAD_K))
-            for b in range(0, BLOCK, 2 * half)
-        ]
-        anchor = jnp.concatenate(anchors, axis=0) if len(anchors) > 1 else anchors[0]
-        factor = jnp.exp(-jnp.abs(cum - anchor))
+    for i, half in enumerate(HALVES):
+        factor = factors[i]
         part = dot((queries * factor).astype(BF16), (keys * factor).astype(BF16), LAST)
         inside = (
             (row_iota // (2 * half) == col_iota // (2 * half))
@@ -295,13 +307,10 @@
             & (col_iota % (2 * half) < half)
         )
         weights = jnp.where(inside, part, weights)
-    groups = (BLOCK // 8, 8, HEAD_K)
-    cum_g, keys_g = cum.reshape(groups), keys.reshape(groups)
-    queries_g = queries.reshape(groups)
+    keys_g, queries_g = keys.reshape(GROUPS), queries.reshape(GROUPS)
     for by in range(8):
         if by:
-            spread = jnp.minimum(cum_g - pltpu.roll(cum_g, by, 1), 0.0)
-            product = queries_g * pltpu.roll(keys_g, by, 1) * jnp.exp(spread)
+            product = queries_g * pltpu.roll(keys_g, by, 1) * factors[3 + by].reshape(GROUPS)
         else:
             product = queries_g * keys_g
         sums = jnp.sum(product.reshape(BLOCK, HEAD_K), axis=1, keepdims=True)
@@ -435,7 +444,7 @@
         block_state,
         [
             ((BLOCKS, PIECE + 16, LANES), BF16),
-            ((8, 2 * HEAD_K + CHUNK), F32),
+            ((8, 2 * HEAD_K + CHUNK), BF16),
             ((BLOCK, WIDTH), BF16),
             ((BLOCK, CHUNK), F32),
             ((BLOCK, HEAD_K), F32),
@@ -477,13 +486,14 @@
         scalars=1,
     )
     incoming = lax.all_to_all(states, GRID, 0, 0).reshape(2, CHUNK, LANES)
-    (gate,) = local_call(
-        output_gate,
-        [((BLOCK, CHUNK), F32)],
+    gate, factors = local_call(
+        ahead,
+        [((BLOCK, CHUNK), F32), ((12, BLOCK, HEAD_K), F32)],
         gained,
         row_scale,
         w_gate,
         head_gain.reshape(1, CHUNK),
+        cumulated,
         left,
     )
     intra, reach = local_call(
@@ -496,7 +506,7 @@
         taps_q,
         taps_k,
         taps_v,
-        cumulated,
+        factors,
         columns,
         own_rows,
         left,

time: 81.4 us -> 81.1 us (level)
  transfers between devices with their start and end apart: 2 -> 2, of which waited for: 1 -> 2; matrix products, arithmetic and copies ran while one was open for 0% -> 0% of each run, Pallas kernels for 2% -> 2%
where the time goes in v17:
time: 81.1 us; the launch traced here: 80.8 us
  blocking collectives  61.7 us (76%)
  Pallas kernels  7.89 us (10%)
  starting transfers between devices  7.27 us (9%)
  waiting for transfers between devices  3.8 us (5%)
    all_to_all x1, blocking collectives, shards(): owned = lax.all_to_all(pieces, GRID, 0, 0)  20.1 us
    all_to_all x1, blocking collectives, shards(): of_core = lax.all_to_all(copies, CHIPS, 0, 0)  17.8 us
    all_to_all x1, blocking collectives, shards(): arrived = lax.all_to_all(pairs, CHIPS, 0, 0)  14.5 us
    pallas_call x8, Pallas kernels, local_call(): pl.pallas_call(kernel, out_shape=[jax.ShapeDtypeStruct(s, t) if last else...  7.89 us
    all_gather x1, blocking collectives, shards(): both = lax.all_gather(sent, 'core', axis=0)  4.88 us
    all_gather x1, blocking collectives, shards(): whole = lax.all_gather(of_core, 'core', axis=0)  4.46 us
    all_to_all x1, starting transfers between devices, shards(): incoming = lax.all_to_all(states, GRID, 0, 0).reshape(2, CHUNK, LANES)  4.13 us
    all_to_all x1, waiting for transfers between devices, shards(): incoming = lax.all_to_all(states, GRID, 0, 0).reshape(2, CHUNK, LANES)  3.59 us
  transfers between devices with their start and end apart: 2, of which 2 were waited for; matrix products, arithmetic and copies ran while one was open for 0% of the time, Pallas kernels for 2%

profile of v17, /device:TPU:1, one launch (start us, length us, event | category | flops | bytes accessed | tf_op | source)
XLA Modules:
  0.0 80.8 jit_solution(17350189822308216030)
XLA Ops:
  0.0 0.0 copy-start
  0.0 1.0 %fetch_and_spread.1 = (bf16[128,128]{1,0:T(8,128)(2,1)S(1)}, f32[1,2048]{1,0:T(1,128)S(1)}, bf16[16,2048]{1,0:T(8,128)(2,1)S(1)}, bf16[16,256]{1,0:T(8,128)(2,1)...) custom-call(s32[1]{0:T(128)} %bitcast.1.index, ...), custom_call_target="tpu_custom_call" | custom-call | tf_op jit(solution)/shard_map/fetch_and_spread/pallas_call | solution.py:38
  1.1 17.8 %all_to_all.20 = bf16[8,128,128]{2,1,0:T(8,128)(2,1)S(1)} all-to-all(bf16[8,128,128]{2,1,0:T(8,128)(2,1)S(1)} %get-tuple-element.34), channel_id=1, replica_groups=mesh['x'=4,'y'=8,'row'=4,'zhi'=2,'core'=2] {'row','zhi'}, dimensions={0} | all-to-all | bytes 524288 | tf_op jit(solution)/shard_map/all_to_all | solution.py:441
  18.9 4.5 %all-gather = bf16[16,128,128]{2,1,0:T(8,128)(2,1)S(1)} all-gather(bf16[8,128,128]{2,1,0:T(8,128)(2,1)S(1)} %all_to_all.20), channel_id=2, replica_groups=mesh['x'=4,'y'=8,'row'=4,'zhi'=2,'core'=2] {'core'}, dimensions={0}, use_global_device_ids=true | all-gather | bytes 786432 | tf_op jit(solution)/shard_map/all_gather | solution.py:442
  23.3 0.0 copy-done
  23.3 0.0 copy-start.1
  23.3 2.4 %block_state.1 = (bf16[32,24,128]{2,1,0:T(8,128)(2,1)S(1)}, bf16[8,640]{1,0:T(8,128)(2,1)S(1)}, bf16[128,2048]{1,0:T(8,128)(2,1)S(1)}, f32[128,128]{1,0:T(8,128)...) custom-call(s32[1]{0:T(128)} %bitcast.1.index, ...), custom_call_target="tpu_custom_call" | custom-call | tf_op jit(solution)/shard_map/block_state/pallas_call | solution.py:38
  25.7 20.1 %all_to_all.21.pieces = bf16[32,24,128]{2,1,0:T(8,128)(2,1)S(1)} all-to-all(bf16[32,24,128]{2,1,0:T(8,128)(2,1)S(1)} %get-tuple-element.50), channel_id=1, replica_groups=mesh['x'=4,'y'=8,'row'=4,'zhi'=2,'core'=2] {'y','x'}, dimensions={0} | all-to-all | bytes 393216 | tf_op jit(solution)/shard_map/all_to_all | solution.py:480
  45.8 1.1 %scan_blocks.1 = (bf16[32,8,128]{2,1,0:T(8,128)(2,1)}, f32[8,128]{1,0:T(8,128)S(1)}) custom-call(s32[1]{0:T(128)} %bitcast.1.index, bf16[32,24,128]{2,1,0:T(8,128)(2,1)S(1)} %all_to_all.21.pieces), custom_call_target="tpu_custom_call" | custom-call | tf_op jit(solution)/shard_map/scan_blocks/pallas_call | solution.py:38
  46.9 4.1 %all-to-all-start.2 = ((bf16[32,8,128]{2,1,0:T(8,128)(2,1)}), bf16[32,8,128]{2,1,0:T(8,128)(2,1)S(1)}, u32[]{:S(2)}, u32[]{:S(2)}) async-start(bf16[32,8,128]{2,1,0:T(8,128)(2,1)} %get-tuple-element.57), calls=%async_computation.2 | async-start | bytes 131072 | tf_op jit(solution)/shard_map/all_to_all | solution.py:488
  51.0 3.1 %collective-permute-start = (bf16[8,640]{1,0:T(8,128)(2,1)S(1)}, bf16[8,640]{1,0:T(8,128)(2,1)S(1)}, u32[]{:S(2)}, u32[]{:S(2)}) collective-permute-start(bf16[8,640]{1,0:T(8,128)(2,1)S(1)} %get-tuple-element.45), channel_id=1, source_target_pairs={{0,16},{16,32},{32,48},{48,64},{64,80},{80,96},{96,112},{112,128},... | collective-permute-start | bytes 30728 | tf_op jit(solution)/shard_map/ppermute | solution.py:479
  54.1 0.0 copy-done.1
  54.1 0.0 copy-done.3
  54.2 0.0 copy-start.2
  54.2 0.5 ahead.1
  54.7 0.2 collective-permute-done.edge
  54.9 1.3 %block_attention.1 = (f32[128,128]{1,0:T(8,128)S(1)}, f32[128,256]{1,0:T(8,128)S(1)}) custom-call(f32[128,256]{1,0:T(8,128)S(1)} %get-tuple-element.42.pre_q, f32[128,256]{1,0:T(8,128)S(1)} %get-tuple-element.43.pre_k, f32[128,128]{1,0:T(8,128)S(1)} %get-tuple-element.44.pre_v, bf16[8,640]{1,0:T(8,128)(2,1)S(1)} %collective-permute-done.edge, ...), custom_call_target="tpu_custom_call" | custom-call | tf_op jit(solution)/shard_map/block_attention/pallas_call | solution.py:38
  56.2 3.6 %all-to-all-done.2 = bf16[32,8,128]{2,1,0:T(8,128)(2,1)S(1)} async-done(((bf16[32,8,128]{2,1,0:T(8,128)(2,1)}), bf16[32,8,128]{2,1,0:T(8,128)(2,1)S(1)}, u32[]{:S(2)}, u32[]{:S(2)}) %all-to-all-start.2) | async-done | bytes 65568 | tf_op jit(solution)/shard_map/all_to_all | solution.py:488
  59.8 0.0 copy-done.2
  59.8 0.6 attend.1
  60.4 4.9 %all-gather.1 = bf16[2064,128]{1,0:T(8,128)(2,1)S(1)} all-gather(bf16[1032,128]{1,0:T(8,128)(2,1)S(1)} %get-tuple-element.61), channel_id=3, replica_groups=mesh['x'=4,'y'=8,'row'=4,'zhi'=2,'core'=2] {'core'}, dimensions={0}, use_global_device_ids=true | all-gather | bytes 792576 | tf_op jit(solution)/shard_map/all_gather | solution.py:529
  65.3 0.1 pair_sum.1
  65.4 14.5 %all_to_all.22.received = bf16[8,136,128]{2,1,0:T(8,128)(2,1)S(1)} all-to-all(bf16[8,136,128]{2,1,0:T(8,128)(2,1)S(1)} %pair_sum.1), channel_id=1, replica_groups=mesh['x'=4,'y'=8,'row'=4,'zhi'=2,'core'=2] {'row','zhi'}, dimensions={0} | all-to-all | bytes 557056 | tf_op jit(solution)/shard_map/all_to_all | solution.py:533
  79.9 0.9 %finish.1 = bf16[128,128]{1,0:T(8,128)(2,1)} custom-call(bf16[8,136,128]{2,1,0:T(8,128)(2,1)S(1)} %all_to_all.22.received, bf16[128,128]{1,0:T(8,128)(2,1)S(1)} %get-tuple-element.62.hidden), custom_call_target="tpu_custom_call" | custom-call | tf_op jit(solution)/shard_map/finish/pallas_call | solution.py:38
  (1 shorter events, 0.0 us)
Async XLA Ops:
  0.0 23.3 %copy-start = (bf16[2048,256]{1,0:T(8,128)(2,1)S(1)}, bf16[2048,256]{1,0:T(8,128)(2,1)}, u32[]{:S(2)}) copy-start(bf16[2048,256]{1,0:T(8,128)(2,1)} %w_key.1) | copy-start | bytes 3145732
  23.3 30.8 %copy-start.1 = (bf16[2048,128]{1,0:T(8,128)(2,1)S(1)}, bf16[2048,128]{1,0:T(8,128)(2,1)}, u32[]{:S(2)}) copy-start(bf16[2048,128]{1,0:T(8,128)(2,1)} %w_gate.1) | copy-start | bytes 1572868
  23.3 30.8 %copy-start.3 = (f32[128]{0:T(128)S(1)}, f32[128]{0:T(128)}, u32[]{:S(2)}) copy-start(f32[128]{0:T(128)} %param.28) | copy-start | bytes 1540
  46.9 13.0 %all-to-all-start.2 = ((bf16[32,8,128]{2,1,0:T(8,128)(2,1)}), bf16[32,8,128]{2,1,0:T(8,128)(2,1)S(1)}, u32[]{:S(2)}, u32[]{:S(2)}) async-start(bf16[32,8,128]{2,1,0:T(8,128)(2,1)} %get-tuple-element.57), calls=%async_computation.2 | async-start | bytes 131072 | tf_op jit(solution)/shard_map/all_to_all | solution.py:488
  51.0 3.9 %collective-permute-start = (bf16[8,640]{1,0:T(8,128)(2,1)S(1)}, bf16[8,640]{1,0:T(8,128)(2,1)S(1)}, u32[]{:S(2)}, u32[]{:S(2)}) collective-permute-start(bf16[8,640]{1,0:T(8,128)(2,1)S(1)} %get-tuple-element.45), channel_id=1, source_target_pairs={{0,16},{16,32},{32,48},{48,64},{64,80},{80,96},{96,112},{112,128},... | collective-permute-start | bytes 30728 | tf_op jit(solution)/shard_map/ppermute | solution.py:479
  54.2 5.7 %copy-start.2 = (bf16[128,2048]{1,0:T(8,128)(2,1)S(1)}, bf16[128,2048]{1,0:T(8,128)(2,1)}, u32[]{:S(2)}) copy-start(bf16[128,2048]{1,0:T(8,128)(2,1)} %w_out.1) | copy-start | bytes 1572868
